TPU v7x, 512 devices: a whole 4x4x16 slice. The times are simulated.
512 devices in a mesh: seq: 64 (over z, y), chan: 8 (over x, core).
Axes of the slice: x: 4, y: 4, z: 16, core: 2. Of those that a mesh axis runs over, the one named last changes fastest.
Arguments:
- signal: bfloat16 [8192, 2048], P('seq', 'chan'), may hold values from -6 to 6
- cotangent: bfloat16 [8192, 2048], P('seq', 'chan'), may hold values from -6 to 6
- w_proj: bfloat16 [2048, 560], P('chan'), may hold values from -0.009765625 to 0.009765625
- w_delta: bfloat16 [2, 256, 2048], P(None, None, 'chan'), may hold values from -5.03125 to 5.03125
- delta_bias: float32 [2, 2048], P(None, 'chan'), may hold values from -1 to 0.5
- decay_log: float32 [2, 12, 2048], P(None, None, 'chan'), may hold values from -12 to -3, as said below
- skip_gain: float32 [2048], P('chan'), may hold values from 0.5 to 1.5
Outputs:
- layer_out: bfloat16 [8192, 2048], P('seq', 'chan')
- signal_grad: bfloat16 [8192, 2048], P('seq', 'chan')
Inputs may be any that keep to these rules, and one draw needn't show every extreme that they name: `decay_log`: each entry is the logarithm of a positive decay rate.
All inputs are finite; a program needn't handle non-finite values.
Results may differ from a plain program's by a relative error of at most 0.0085.
Values may be sent and summed in bfloat16 or wider, within the bound.
No kernel may reach another device: no remote copies, remote signals or barrier semaphores. Data moves between devices by JAX's collectives and lax.ppermute only.
A program may use at most 64 MiB of HBM per device.

v0:
```python
import math

import jax
import jax.numpy as jnp
from jax import lax
from jax.sharding import PartitionSpec as P


def entering_2(part, axis, combine, identity, reverse):
    count = lax.axis_size(axis)
    place = lax.axis_index(axis)
    ahead = count - 1 - place if reverse else place
    gathered = jax.tree.map(lambda a: lax.all_gather(a, axis), part)
    state = jax.tree.map(lambda a, e: jnp.zeros_like(a) + jnp.asarray(e, a.dtype), part, identity)

    def one(hop, state):
        source = count - 1 - hop if reverse else hop
        return combine(
            state, jax.tree.map(lambda a: lax.dynamic_index_in_dim(a, source, 0, False), gathered)
        )

    return lax.fori_loop(0, ahead, one, state)


def compose_one(earlier, later):
    return (earlier[0] * later[0], later[0] * earlier[1] + later[1])


def compose_pairs(earlier, later):
    return (
        earlier[0] * later[0],
        later[0] * earlier[1] + later[1],
        earlier[2] * later[2],
        later[2] * earlier[3] + later[3],
    )


def linear_scan(decay, drive, entry, falling):
    length, depth, lanes = drive.shape
    inner = math.gcd(length, 16)
    groups = length // inner
    decay_groups = decay.reshape(groups, inner, depth, lanes)
    drive_groups = drive.reshape(groups, inner, depth, lanes)
    running = jnp.zeros((groups, depth, lanes), jnp.float32)
    product = jnp.ones((groups, depth, lanes), jnp.float32)
    saved_states = [None] * inner
    saved_products = [None] * inner
    columns = range(inner - 1, -1, -1) if falling else range(inner)
    for column in columns:
        running = decay_groups[:, column] * running + drive_groups[:, column]
        product = decay_groups[:, column] * product
        saved_states[column] = running
        saved_products[column] = product
    local_states = jnp.stack(saved_states, 1)
    cumulative = jnp.stack(saved_products, 1)
    edge = 0 if falling else inner - 1
    scanned = lax.associative_scan(
        compose_one, (cumulative[:, edge], local_states[:, edge]), reverse=falling, axis=0
    )
    after = scanned[0] * entry[None] + scanned[1]
    if falling:
        entering = jnp.concatenate([after[1:], entry[None]], 0)
    else:
        entering = jnp.concatenate([entry[None], after[:-1]], 0)
    return (local_states + cumulative * entering[:, None]).reshape(length, depth, lanes)


def summaries(delta, rate, signal_part, cot_part, in_mat, out_mat, falling):
    cumul = jnp.cumsum(delta, axis=0)
    total = cumul[-1]
    weight = delta * signal_part
    if falling:
        state_power = cumul - delta
        adjoint_power = total[None] - cumul + delta
    else:
        state_power = total[None] - cumul
        adjoint_power = cumul
    state_sum = jnp.sum(
        jnp.exp(rate[None] * state_power[:, None, :]) * (in_mat[:, :, None] * weight[:, None, :]), 0
    )
    adjoint_sum = jnp.sum(
        jnp.exp(rate[None] * adjoint_power[:, None, :])
        * (out_mat[:, :, None] * cot_part[:, None, :]),
        0,
    )
    return (rate * total[None], state_sum, adjoint_sum)


def direction_pass(
    delta, rate, signal_part, cot_part, in_mat, out_mat, entry, adjoint_entry, falling
):
    decay = jnp.exp(delta[:, None, :] * rate[None])
    weight = delta * signal_part
    drive = weight[:, None, :] * in_mat[:, :, None]
    states = linear_scan(decay, drive, entry, falling)
    outputs = jnp.sum(out_mat[:, :, None] * states, 1)
    source = cot_part[:, None, :] * out_mat[:, :, None]
    carried = linear_scan(decay, decay * source, adjoint_entry, not falling)
    if falling:
        adjoint = source + jnp.concatenate([adjoint_entry[None], carried[:-1]], 0)
        neighbour = jnp.concatenate([states[1:], entry[None]], 0)
    else:
        adjoint = source + jnp.concatenate([carried[1:], adjoint_entry[None]], 0)
        neighbour = jnp.concatenate([entry[None], states[:-1]], 0)
    grad_out = jnp.sum(cot_part[:, None, :] * states, 2)
    grad_in = jnp.sum(adjoint * weight[:, None, :], 2)
    grad_delta = jnp.sum(
        adjoint * (in_mat[:, :, None] * signal_part[:, None, :] + neighbour * decay * rate[None]), 1
    )
    grad_sig = jnp.sum(adjoint * in_mat[:, :, None], 1) * delta
    return (outputs, grad_sig, grad_delta, grad_in, grad_out)


def local(signal, cotangent, w_proj, w_delta, delta_bias, decay_log, skip_gain):
    rows, width = signal.shape
    rank = w_delta.shape[1]
    depth = decay_log.shape[1]
    partial_proj = jnp.dot(signal, w_proj, preferred_element_type=jnp.float32)
    projected = lax.psum(partial_proj, "chan").astype(jnp.bfloat16)
    low_fwd = projected[:, :rank]
    low_bwd = projected[:, rank : 2 * rank]
    gates = projected[:, 2 * rank :].astype(jnp.float32)
    in_fwd = gates[:, :depth]
    out_fwd = gates[:, depth : 2 * depth]
    in_bwd = gates[:, 2 * depth : 3 * depth]
    out_bwd = gates[:, 3 * depth : 4 * depth]
    pre_fwd = jnp.dot(low_fwd, w_delta[0], preferred_element_type=jnp.float32) + delta_bias[0]
    pre_bwd = jnp.dot(low_bwd, w_delta[1], preferred_element_type=jnp.float32) + delta_bias[1]
    delta_fwd = jax.nn.softplus(pre_fwd)
    delta_bwd = jax.nn.softplus(pre_bwd)
    rate_fwd = -jnp.exp(decay_log[0])
    rate_bwd = -jnp.exp(decay_log[1])
    signal_wide = signal.astype(jnp.float32)
    cot_wide = cotangent.astype(jnp.float32)
    lanes = min(128, width)
    blocks = width // lanes

    def cut(array, start):
        return lax.dynamic_slice_in_dim(array, start, lanes, array.ndim - 1)

    def first_pass(block, carry):
        start = block * lanes
        forward = summaries(
            cut(delta_fwd, start),
            cut(rate_fwd, start),
            cut(signal_wide, start),
            cut(cot_wide, start),
            in_fwd,
            out_fwd,
            False,
        )
        backward = summaries(
            cut(delta_bwd, start),
            cut(rate_bwd, start),
            cut(signal_wide, start),
            cut(cot_wide, start),
            in_bwd,
            out_bwd,
            True,
        )
        pieces = forward + backward
        return tuple(
            (
                lax.dynamic_update_slice_in_dim(whole, piece, start, 1)
                for whole, piece in zip(carry, pieces)
            )
        )

    empty = jnp.zeros((depth, width), jnp.float32)
    log_fwd, state_fwd, adjoint_fwd, log_bwd, state_bwd, adjoint_bwd = lax.fori_loop(
        0, blocks, first_pass, (empty,) * 6
    )
    unity = jnp.ones((depth, width), jnp.float32)
    identity = (unity, empty, unity, empty)
    rising = entering_2(
        (jnp.exp(log_fwd), state_fwd, jnp.exp(log_bwd), adjoint_bwd),
        "seq",
        compose_pairs,
        identity,
        False,
    )
    falling = entering_2(
        (jnp.exp(log_bwd), state_bwd, jnp.exp(log_fwd), adjoint_fwd),
        "seq",
        compose_pairs,
        identity,
        True,
    )
    enter_fwd = rising[1]
    adjoint_enter_bwd = rising[3]
    enter_bwd = falling[1]
    adjoint_enter_fwd = falling[3]

    def second_pass(block, carry):
        core, grad_sig, grad_pre_f, grad_pre_b, grad_in_f, grad_out_f, grad_in_b, grad_out_b = carry
        start = block * lanes
        forward = direction_pass(
            cut(delta_fwd, start),
            cut(rate_fwd, start),
            cut(signal_wide, start),
            cut(cot_wide, start),
            in_fwd,
            out_fwd,
            cut(enter_fwd, start),
            cut(adjoint_enter_fwd, start),
            False,
        )
        backward = direction_pass(
            cut(delta_bwd, start),
            cut(rate_bwd, start),
            cut(signal_wide, start),
            cut(cot_wide, start),
            in_bwd,
            out_bwd,
            cut(enter_bwd, start),
            cut(adjoint_enter_bwd, start),
            True,
        )
        pre_grad_f = forward[2] * jax.nn.sigmoid(cut(pre_fwd, start))
        pre_grad_b = backward[2] * jax.nn.sigmoid(cut(pre_bwd, start))
        core = lax.dynamic_update_slice_in_dim(core, forward[0] + backward[0], start, 1)
        grad_sig = lax.dynamic_update_slice_in_dim(grad_sig, forward[1] + backward[1], start, 1)
        grad_pre_f = lax.dynamic_update_slice_in_dim(grad_pre_f, pre_grad_f, start, 1)
        grad_pre_b = lax.dynamic_update_slice_in_dim(grad_pre_b, pre_grad_b, start, 1)
        return (
            core,
            grad_sig,
            grad_pre_f,
            grad_pre_b,
            grad_in_f + forward[3],
            grad_out_f + forward[4],
            grad_in_b + backward[3],
            grad_out_b + backward[4],
        )

    blank_rows = jnp.zeros((rows, width), jnp.float32)
    blank_gates = jnp.zeros((rows, depth), jnp.float32)
    initial = (
        blank_rows,
        blank_rows,
        blank_rows,
        blank_rows,
        blank_gates,
        blank_gates,
        blank_gates,
        blank_gates,
    )
    core, grad_sig, grad_pre_f, grad_pre_b, grad_in_f, grad_out_f, grad_in_b, grad_out_b = (
        lax.fori_loop(0, blocks, second_pass, initial)
    )
    layer_out = (core + skip_gain * signal_wide).astype(jnp.bfloat16)
    dims = (((1,), (1,)), ((), ()))
    grad_low_f = lax.dot_general(
        grad_pre_f.astype(jnp.bfloat16), w_delta[0], dims, preferred_element_type=jnp.float32
    )
    grad_low_b = lax.dot_general(
        grad_pre_b.astype(jnp.bfloat16), w_delta[1], dims, preferred_element_type=jnp.float32
    )
    grad_parts = jnp.concatenate(
        [grad_low_f, grad_low_b, grad_in_f, grad_out_f, grad_in_b, grad_out_b], 1
    )
    grad_proj = lax.psum(grad_parts, "chan").astype(jnp.bfloat16)
    signal_grad = (
        lax.dot_general(grad_proj, w_proj, dims, preferred_element_type=jnp.float32)
        + grad_sig
        + skip_gain * cot_wide
    )
    return (layer_out, signal_grad.astype(jnp.bfloat16))


def solution(mesh):
    in_specs = (
        P("seq", "chan"),
        P("seq", "chan"),
        P("chan", None),
        P(None, None, "chan"),
        P(None, "chan"),
        P(None, None, "chan"),
        P("chan"),
    )
    out_specs = (P("seq", "chan"), P("seq", "chan"))
    return jax.shard_map(local, mesh=mesh, in_specs=in_specs, out_specs=out_specs, check_vma=False)
```

profile of v0, /device:TPU:504, one launch (start us, length us, event | category | flops | bytes accessed | tf_op | source)
XLA Modules:
  0.0 1432.5 jit_solution(3421313002463477451)
XLA Ops:
  2.7 28.9 %all-reduce.50 = bf16[128,560]{0,1:T(8,128)(2,1)S(1)} all-reduce(f32[128,560]{0,1:T(8,128)S(1)} %fusion.156), channel_id=1, replica_groups=mesh['seq'=64,'chan'=8] {'chan'}, use_global_device_ids=true, to_apply=%region_0.0 | all-reduce | flops 71680 | bytes 430080 | tf_op jit(solution)/shard_map/psum | solution.py:119
  41.1 98.2 %all-gather.6 = f32[64,12,256]{2,1,0:T(8,128)S(1)} all-gather(f32[1,12,256]{2,1,0:T(8,128)S(1)} %exponential_bitcast_fusion.1), channel_id=2, replica_groups=mesh['seq'=64,'chan'=8] {'seq'}, dimensions={0}, use_global_device_ids=true | all-gather | bytes 798720 | tf_op jit(solution)/shard_map/all_gather | solution.py:13
  139.3 99.4 %all-gather.8 = f32[64,12,256]{2,1,0:T(8,128)S(1)} all-gather(f32[1,12,256]{2,1,0:T(8,128)S(1)} %exponential_bitcast_fusion), channel_id=4, replica_groups=mesh['seq'=64,'chan'=8] {'seq'}, dimensions={0}, use_global_device_ids=true | all-gather | bytes 798720 | tf_op jit(solution)/shard_map/all_gather | solution.py:13
  238.7 107.7 %all-gather.10 = f32[64,12,256]{2,1,0:T(8,128)} all-gather(f32[1,12,256]{2,1,0:T(8,128)S(1)} %bitcast.1374), channel_id=6, replica_groups=mesh['seq'=64,'chan'=8] {'seq'}, dimensions={0}, use_global_device_ids=true | all-gather | bytes 798720 | tf_op jit(solution)/shard_map/all_gather | solution.py:13
  346.3 108.6 %all-gather.11 = f32[64,12,256]{2,1,0:T(8,128)} all-gather(f32[1,12,256]{2,1,0:T(8,128)S(1)} %bitcast.1373), channel_id=7, replica_groups=mesh['seq'=64,'chan'=8] {'seq'}, dimensions={0}, use_global_device_ids=true | all-gather | bytes 798720 | tf_op jit(solution)/shard_map/all_gather | solution.py:13
  454.9 156.6 %all-gather.7 = f32[64,12,256]{2,1,0:T(8,128)} all-gather(f32[1,12,256]{2,1,0:T(8,128)S(1)} %bitcast.1372), channel_id=3, replica_groups=mesh['seq'=64,'chan'=8] {'seq'}, dimensions={0}, use_global_device_ids=true | all-gather | bytes 798720 | tf_op jit(solution)/shard_map/all_gather | solution.py:13
  611.5 109.0 %all-gather.9 = f32[64,12,256]{2,1,0:T(8,128)} all-gather(f32[1,12,256]{2,1,0:T(8,128)S(1)} %bitcast.1375), channel_id=5, replica_groups=mesh['seq'=64,'chan'=8] {'seq'}, dimensions={0}, use_global_device_ids=true | all-gather | bytes 798720 | tf_op jit(solution)/shard_map/all_gather | solution.py:13
  720.5 49.2 %while.86 = (s32[]{:T(128)}, f32[12,256]{1,0:T(8,128)S(1)}, f32[12,256]{1,0:T(8,128)S(1)}, s32[]{:T(128)}, f32[64,12,256]{2,1,0:T(8,128)S(1)}, /*index=5*/f32[64...) while((s32[]{:T(128)}, f32[12,256]{1,0:T(8,128)S(1)}, ...), condition=%wide.region_10.11_spmd, body=%wide.region_9.10_spmd.sunk | while | flops 12293 | bytes 98451 | solution.py:22
  773.1 625.5 %while.88 = (s32[]{:T(128)}, f32[128,256]{1,0:T(8,128)}, f32[128,256]{1,0:T(8,128)}, bf16[128,256]{1,0:T(8,128)(2,1)}, bf16[128,256]{1,0:T(8,128)(2,1)}, /*index...) while((s32[]{:T(128)}, f32[128,256]{1,0:T(8,128)}, ...), condition=%wide.region_24.25_spmd.clone, body=%wide.region_13.24_spmd.clone.sunk | while | flops 17229824 | bytes 121105632 | solution.py:249
  833.7 6.4 pad.810
  917.1 6.4 pad.803
  947.3 6.4 pad.802
  957.9 6.4 pad.801
  966.5 6.4 pad.800
  1016.1 6.4 pad.795
  1050.1 6.4 pad.793
  1146.4 6.4 pad.810
  1229.8 6.4 pad.803
  1260.0 6.4 pad.802
  1270.6 6.4 pad.801
  1279.2 6.4 pad.800
  1328.8 6.4 pad.795
  1362.9 6.4 pad.793
  1403.2 27.0 %all-reduce.51 = bf16[128,560]{1,0:T(8,128)(2,1)S(1)} all-reduce(f32[128,560]{1,0:T(8,128)S(1)} %concatenate.171), channel_id=1, replica_groups=mesh['seq'=64,'chan'=8] {'chan'}, use_global_device_ids=true, to_apply=%region_25.26 | all-reduce | flops 71680 | bytes 430080 | tf_op jit(solution)/shard_map/psum | solution.py:262
  (1158 shorter events, 606.8 us)
Async XLA Ops:
  2.7 29.6 %copy-start.104 = (bf16[2,256,256]{2,1,0:T(8,128)(2,1)S(1)}, bf16[2,256,256]{2,1,0:T(8,128)(2,1)}, u32[]{:S(2)}) copy-start(bf16[2,256,256]{2,1,0:T(8,128)(2,1)} %param.18) | copy-start | bytes 786436
  773.2 3.2 copy-start.39
  773.2 3.2 copy-start.41
  773.2 3.2 copy-start.31
  773.2 4.6 copy-start.80
  773.2 4.6 copy-start.69
  773.2 5.4 copy-start.76
  852.6 7.1 copy-start.26
  1057.9 7.1 copy-start.27
  1080.6 1.7 copy-start.102
  1083.0 2.5 copy-start.42
  1083.0 2.5 copy-start.81
  1085.9 3.2 copy-start.39
  1085.9 3.2 copy-start.41
  1085.9 3.2 copy-start.31
  1085.9 4.5 copy-start.80
  1086.0 4.5 copy-start.69
  1086.0 5.4 copy-start.76
  1165.3 7.1 copy-start.26
  1370.6 7.1 copy-start.27
  1395.8 2.5 copy-start.42
  1395.8 2.5 copy-start.81
  1403.2 27.0 %copy-start.89 = (f32[128,256]{1,0:T(8,128)S(1)}, f32[128,256]{1,0:T(8,128)}, u32[]{:S(2)}) copy-start(f32[128,256]{1,0:T(8,128)} %get-tuple-element.944) | copy-start | bytes 393220
  1403.2 27.0 %copy-start.107 = (bf16[128,256]{1,0:T(8,128)(2,1)S(1)}, bf16[128,256]{1,0:T(8,128)(2,1)}, u32[]{:S(2)}) copy-start(bf16[128,256]{1,0:T(8,128)(2,1)} %param.16) | copy-start | bytes 196612
  (184 other events, 181.5 us)
where the time goes:
time: 1460 us; the launch traced here: 1430 us
  blocking collectives  735 us (50%)
  local copies, waits for them, and re-layouts  481 us (33%)
  other arithmetic  205 us (14%)
    all_gather x6, blocking collectives, entering_2(): gathered = jax.tree.map(lambda a: lax.all_gather(a, axis), part)  679 us
    pad x48, local copies, waits for them, and re-layouts, linear_scan(): lax.associative_scan(compose_one, (cumulative[:, edge], local_states[:, e...  205 us
    slice x124, local copies, waits for them, and re-layouts, linear_scan(): lax.associative_scan(compose_one, (cumulative[:, edge], local_states[:, e...  97.4 us
    while x434, local copies, waits for them, and re-layouts  82.4 us
    slice x8, local copies, waits for them, and re-layouts, linear_scan(): entering = jnp.concatenate([entry[None], after[:-1]], 0)  51 us
    add x63, other arithmetic, compose_pairs(): later[2] * earlier[3] + later[3]  47.5 us
    add x40, other arithmetic, linear_scan(): lax.associative_scan(compose_one, (cumulative[:, edge], local_states[:, e...  38.1 us

commit v1 on v0

v1 whole, which is shorter than its diff:
```python
import math

import jax
import jax.numpy as jnp
from jax import lax
from jax.experimental import pallas as pl
from jax.experimental.pallas import tpu as pltpu
from jax.sharding import PartitionSpec as P

GROUPS = 8
LANES = 128
SLOTS = 16
LOG2E = math.log2(math.e)
LN2 = math.log(2.0)
FAR = 1e30
NT = (((1,), (1,)), ((), ()))
F32 = jnp.float32
BF16 = jnp.bfloat16


def dot(a, b, dims=(((1,), (0,)), ((), ()))):
    return lax.dot_general(a, b, dims, preferred_element_type=F32)


def grouping(rows, inverse=False):
    steps = rows // GROUPS
    row = lax.broadcasted_iota(jnp.int32, (rows, rows), 1 if inverse else 0)
    token = lax.broadcasted_iota(jnp.int32, (rows, rows), 0 if inverse else 1)
    return jnp.where(token == (row % GROUPS) * steps + row // GROUPS, 1.0, 0.0).astype(BF16)


def project_kernel(signal, cotangent, w_proj, signal_out, cot_out, part_out):
    order = grouping(signal.shape[0])
    grouped = dot(order, signal[...])
    signal_out[...] = grouped
    cot_out[...] = dot(order, cotangent[...])
    part_out[...] = dot(grouped.astype(BF16), w_proj[...]).astype(BF16)


def spread_gates(gates, spread):
    count = gates.shape[1]
    for pair in range(count // 2):
        source = lax.broadcasted_iota(jnp.int32, (count, 2 * LANES), 0)
        lane = lax.broadcasted_iota(jnp.int32, (count, 2 * LANES), 1)
        pick = jnp.where(source == 2 * pair + lane // LANES, 1.0, 0.0).astype(BF16)
        spread[:, pair * 2 * LANES : (pair + 1) * 2 * LANES] = dot(gates, pick)


def at(step):
    return pl.ds(pl.multiple_of(step * GROUPS, GROUPS), GROUPS)


def lane_block(block):
    return slice(block * LANES, (block + 1) * LANES)


def spread_rates(decay_log, rates):
    depth = decay_log.shape[1]
    width = decay_log.shape[2]
    for way in range(2):
        scaled = -jnp.exp(decay_log[way]) * LOG2E
        for n in range(depth):
            rates[way, n] = jnp.broadcast_to(scaled[n : n + 1], (GROUPS, width))


def summary_kernel(
    projected,
    w_delta,
    bias,
    decay_log,
    signal,
    cot,
    delta_out,
    slope_out,
    local_out,
    ahead_out,
    payload,
    spread,
    rates,
    weight,
):
    rows, width = signal.shape
    rank = w_delta.shape[1]
    depth = decay_log.shape[1]
    steps = rows // GROUPS
    blocks = width // LANES
    spread_gates(projected[:, 2 * rank :], spread)
    spread_rates(decay_log, rates)
    payload[...] = jnp.zeros_like(payload)
    group = lax.broadcasted_iota(jnp.int32, (GROUPS, LANES), 0)
    for way in range(2):
        pre = dot(projected[:, way * rank : (way + 1) * rank], w_delta[way]) + bias[way : way + 1]
        delta = jnp.maximum(pre, 0.0) + jnp.log1p(jnp.exp(-jnp.abs(pre)))
        delta_out[way] = delta
        slope_out[way] = 1.0 / (1.0 + jnp.exp(-pre))
        weight[...] = delta * signal[...]
        falling = way == 1

        def gate(step, which, n):
            column = (2 * way + which) * depth + n
            return spread[at(step), column * LANES : (column + 1) * LANES]

        def walk(index, carry):
            states, carried, total = carry
            low, high = index, steps - 1 - index
            state_step = high if falling else low
            adjoint_step = low if falling else high
            new_states = []
            new_carried = []
            new_total = []
            for block in range(blocks):
                lanes = lane_block(block)
                d_state = delta_out[way, at(state_step), lanes]
                d_adjoint = delta_out[way, at(adjoint_step), lanes]
                w_state = weight[at(state_step), lanes]
                g_adjoint = cot[at(adjoint_step), lanes]
                new_total.append(total[block] + d_state)
                for n in range(depth):
                    rate = rates[way, n, :, lanes]
                    slot = block * depth + n
                    new_states.append(
                        jnp.exp2(d_state * rate) * states[slot] + w_state * gate(state_step, 0, n)
                    )
                    new_carried.append(
                        jnp.exp2(d_adjoint * rate)
                        * (g_adjoint * gate(adjoint_step, 1, n) + carried[slot])
                    )
            return (tuple(new_states), tuple(new_carried), tuple(new_total))

        zero = jnp.zeros((GROUPS, LANES), F32)
        many = (zero,) * (blocks * depth)
        states, carried, total = lax.fori_loop(0, steps, walk, (many, many, (zero,) * blocks))
        for block in range(blocks):
            lanes = lane_block(block)

            def shift(array, by, down):
                return pltpu.roll(array, GROUPS - by if down else by, 0)

            def beyond(by, down):
                return group >= GROUPS - by if down else group < by

            whole = jnp.sum(total[block], 0, keepdims=True)
            for kind, down, finals in ((0, falling, states), (1, not falling, carried)):
                windows = []
                window = total[block]
                ahead = jnp.where(beyond(1, down), 0.0, shift(window, 1, down))
                for by in (1, 2, 4):
                    windows.append(jnp.where(beyond(by, down), FAR, window))
                    outside = beyond(by, down)
                    window = window + jnp.where(outside, 0.0, shift(window, by, down))
                    ahead = ahead + jnp.where(outside, 0.0, shift(ahead, by, down))
                ahead_out[2 * way + kind, :, lanes] = ahead
                edge = 0 if down else GROUPS - 1
                for n in range(depth):
                    rate = rates[way, n, :, lanes]
                    scanned = finals[block * depth + n]
                    for by, span in zip((1, 2, 4), windows):
                        scanned = scanned + jnp.exp2(rate * span) * shift(scanned, by, down)
                    local_out[2 * way + kind, n, :, lanes] = jnp.where(
                        beyond(1, down), 0.0, shift(scanned, 1, down)
                    )
                    slot = (2 * way + kind) * SLOTS + n
                    payload[slot, block : block + 1] = scanned[edge : edge + 1]
                    payload[slot, blocks + block : blocks + block + 1] = jnp.exp2(
                        rate[:1] * whole
                    )


def shard_scan_kernel(place, parts, entries):
    shards, double, _ = parts.shape
    blocks = double // 2

    def scan(order):
        state = jnp.zeros((blocks, LANES), F32)
        for shard in order:
            entries[shard] = state
            state = parts[shard, blocks:] * state + parts[shard, :blocks]

    kind = place[0] // SLOTS
    falling = jnp.logical_or(kind == 1, kind == 2)

    @pl.when(falling)
    def _():
        scan(range(shards - 1, -1, -1))

    @pl.when(jnp.logical_not(falling))
    def _():
        scan(range(shards))


def gradient_kernel(
    projected,
    w_delta,
    decay_log,
    skip_gain,
    signal,
    cot,
    delta,
    slope,
    local,
    ahead,
    entries,
    layer_out,
    parts_out,
    direct_out,
    spread,
    rates,
    weight,
    core,
    grad_pre,
    kept,
    products,
    sums,
):
    rows, width = signal.shape
    rank = w_delta.shape[1]
    depth = decay_log.shape[1]
    steps = rows // GROUPS
    blocks = width // LANES
    spread_gates(projected[:, 2 * rank :], spread)
    spread_rates(decay_log, rates)
    core[...] = skip_gain[...] * signal[...]
    direct_out[...] = skip_gain[...] * cot[...]
    for way in range(2):
        weight[...] = delta[way] * signal[...]
        falling = way == 1

        def gate(step, which, n):
            column = (2 * way + which) * depth + n
            return spread[at(step), column * LANES : (column + 1) * LANES]

        def entering(kind):
            result = []
            for block in range(blocks):
                lanes = lane_block(block)
                gap = ahead[2 * way + kind, :, lanes]
                for n in range(depth):
                    slot = (2 * way + kind) * SLOTS + n
                    result.append(
                        local[2 * way + kind, n, :, lanes]
                        + jnp.exp2(gap * rates[way, n, :, lanes]) * entries[slot, block : block + 1]
                    )
            return tuple(result)

        def put_products(which, step, pieces):
            start = pl.multiple_of(step * depth * GROUPS, SLOTS)
            for block in range(blocks):
                stacked = jnp.concatenate(pieces[block], 0).astype(BF16)
                products[which, pl.ds(start, depth * GROUPS), lane_block(block)] = stacked

        def walk_states(index, states):
            step = steps - 1 - index if falling else index
            result = []
            pieces = []
            for block in range(blocks):
                lanes = lane_block(block)
                d = delta[way, at(step), lanes]
                w = weight[at(step), lanes]
                g = cot[at(step), lanes]
                total = core[at(step), lanes]
                row = []
                for n in range(depth):
                    slot = block * depth + n
                    faded = jnp.exp2(d * rates[way, n, :, lanes]) * states[slot]
                    kept[step, n, :, lanes] = faded
                    state = faded + w * gate(step, 0, n)
                    total = total + gate(step, 1, n) * state
                    row.append(g * state)
                    result.append(state)
                core[at(step), lanes] = total
                pieces.append(row)
            put_products(2 * way + 1, step, pieces)
            return tuple(result)

        lax.fori_loop(0, steps, walk_states, entering(0))

        def walk_adjoints(index, carried):
            step = index if falling else steps - 1 - index
            result = []
            pieces = []
            for block in range(blocks):
                lanes = lane_block(block)
                d = delta[way, at(step), lanes]
                w = weight[at(step), lanes]
                g = cot[at(step), lanes]
                through = jnp.zeros((GROUPS, LANES), F32)
                fading = jnp.zeros((GROUPS, LANES), F32)
                row = []
                for n in range(depth):
                    slot = block * depth + n
                    rate = rates[way, n, :, lanes]
                    adjoint = g * gate(step, 1, n) + carried[slot]
                    result.append(jnp.exp2(d * rate) * adjoint)
                    through = through + adjoint * gate(step, 0, n)
                    fading = fading + adjoint * kept[step, n, :, lanes] * rate
                    row.append(adjoint * w)
                grad_delta = through * signal[at(step), lanes] + fading * LN2
                direct_out[at(step), lanes] = direct_out[at(step), lanes] + through * d
                grad_pre[way, at(step), lanes] = grad_delta * slope[way, at(step), lanes]
                pieces.append(row)
            put_products(2 * way, step, pieces)
            return tuple(result)

        lax.fori_loop(0, steps, walk_adjoints, entering(1))

    ungroup = grouping(rows, inverse=True)
    layer_out[...] = dot(ungroup, core[...].astype(BF16)).astype(BF16)
    for way in range(2):
        parts_out[:, way * rank : (way + 1) * rank] = dot(
            grad_pre[way].astype(BF16), w_delta[way], NT
        ).astype(BF16)
    ones = jnp.ones((width, LANES), BF16)
    for which in range(4):
        sums[which] = dot(products[which], ones)
    lane = lax.broadcasted_iota(jnp.int32, (GROUPS, LANES), 1)
    for step in range(steps):
        merged = jnp.zeros((GROUPS, LANES), F32)
        for which in range(4):
            for n in range(depth):
                start = (step * depth + n) * GROUPS
                merged = jnp.where(
                    lane == which * depth + n, sums[which, start : start + GROUPS], merged
                )
        parts_out[step * GROUPS : (step + 1) * GROUPS, 2 * rank :] = merged[
            :, : 4 * depth
        ].astype(BF16)


def finish_kernel(grad_proj, w_proj, direct, signal_grad):
    total = dot(grad_proj[...], w_proj[...], NT) + direct[...]
    ungroup = grouping(direct.shape[0], inverse=True)
    signal_grad[...] = dot(ungroup, total.astype(BF16)).astype(BF16)


def shape(*dims, dtype=F32):
    return jax.ShapeDtypeStruct(dims, dtype)


def sum_over_chan(part):
    count = lax.axis_size("chan")
    rows, columns = part.shape
    pieces = part.reshape(count, rows // count, columns)
    arrived = lax.all_to_all(pieces, "chan", 0, 0, tiled=True)
    total = jnp.sum(arrived.astype(F32), 0).astype(BF16)
    copies = jnp.broadcast_to(total[None], (count,) + total.shape)
    return lax.all_to_all(copies, "chan", 0, 0, tiled=True).reshape(rows, columns)


def local(signal, cotangent, w_proj, w_delta, delta_bias, decay_log, skip_gain):
    rows, width = signal.shape
    columns = w_proj.shape[1]
    depth = decay_log.shape[1]
    steps = rows // GROUPS
    blocks = width // LANES
    shards = lax.axis_size("seq")
    if shards != 4 * SLOTS or depth > SLOTS:
        raise ValueError("shard count")
    gates = 4 * depth
    signal_wide, cot_wide, part = pl.pallas_call(
        project_kernel,
        out_shape=(shape(rows, width), shape(rows, width), shape(rows, columns, dtype=BF16)),
        name="project",
    )(signal, cotangent, w_proj)
    projected = sum_over_chan(part)
    delta, slope, local_states, ahead, payload = pl.pallas_call(
        summary_kernel,
        out_shape=(
            shape(2, rows, width),
            shape(2, rows, width),
            shape(4, depth, GROUPS, width),
            shape(4, GROUPS, width),
            shape(shards, 2 * blocks, LANES),
        ),
        scratch_shapes=[
            pltpu.VMEM((rows, gates * LANES), F32),
            pltpu.VMEM((2, depth, GROUPS, width), F32),
            pltpu.VMEM((rows, width), F32),
        ],
        name="summary",
    )(projected, w_delta, delta_bias, decay_log, signal_wide, cot_wide)
    parts = lax.all_to_all(payload, "seq", 0, 0, tiled=True)
    place = lax.axis_index("seq").astype(jnp.int32).reshape(1)
    entries = pl.pallas_call(
        shard_scan_kernel,
        out_shape=shape(shards, blocks, LANES),
        in_specs=[
            pl.BlockSpec(memory_space=pltpu.SMEM),
            pl.BlockSpec(memory_space=pltpu.VMEM),
        ],
        out_specs=pl.BlockSpec(memory_space=pltpu.VMEM),
        name="shard_scan",
    )(place, parts)
    entries = lax.all_to_all(entries, "seq", 0, 0, tiled=True)
    layer_out, grad_parts, direct = pl.pallas_call(
        gradient_kernel,
        out_shape=(
            shape(rows, width, dtype=BF16),
            shape(rows, columns, dtype=BF16),
            shape(rows, width),
        ),
        scratch_shapes=[
            pltpu.VMEM((rows, gates * LANES), F32),
            pltpu.VMEM((2, depth, GROUPS, width), F32),
            pltpu.VMEM((rows, width), F32),
            pltpu.VMEM((rows, width), F32),
            pltpu.VMEM((2, rows, width), F32),
            pltpu.VMEM((steps, depth, GROUPS, width), F32),
            pltpu.VMEM((4, rows * depth, width), BF16),
            pltpu.VMEM((4, rows * depth, LANES), F32),
        ],
        name="gradient",
    )(
        projected,
        w_delta,
        decay_log,
        skip_gain.reshape(1, width),
        signal_wide,
        cot_wide,
        delta,
        slope,
        local_states,
        ahead,
        entries,
    )
    grad_proj = sum_over_chan(grad_parts)
    signal_grad = pl.pallas_call(
        finish_kernel, out_shape=shape(rows, width, dtype=BF16), name="finish"
    )(grad_proj, w_proj, direct)
    return (layer_out, signal_grad)


def solution(mesh):
    in_specs = (
        P("seq", "chan"),
        P("seq", "chan"),
        P("chan", None),
        P(None, None, "chan"),
        P(None, "chan"),
        P(None, None, "chan"),
        P("chan"),
    )
    out_specs = (P("seq", "chan"), P("seq", "chan"))
    return jax.shard_map(local, mesh=mesh, in_specs=in_specs, out_specs=out_specs, check_vma=False)
```

time: 1460 us -> 119 us (0.08)
  the two profiles are of different devices: /device:TPU:504 before, /device:TPU:1 now
where the time goes in v1:
time: 119 us
  blocking collectives  57.8 us (49%)
  waiting for transfers between devices  20.2 us (17%)
  starting transfers between devices  18.4 us (15%)
  Pallas kernels  17.1 us (14%)
  local copies, waits for them, and re-layouts  4.49 us (4%)
    all_to_all x2, blocking collectives, sum_over_chan(): arrived = lax.all_to_all(pieces, 'chan', 0, 0, tiled=True)  28.1 us
    all_to_all x1, blocking collectives, local(): entries = lax.all_to_all(entries, 'seq', 0, 0, tiled=True)  20.2 us
    all_to_all x1, waiting for transfers between devices, local(): parts = lax.all_to_all(payload, 'seq', 0, 0, tiled=True)  15.3 us
    all_to_all x1, starting transfers between devices, local(): parts = lax.all_to_all(payload, 'seq', 0, 0, tiled=True)  14.1 us
    all_to_all x1, blocking collectives, sum_over_chan(): lax.all_to_all(copies, 'chan', 0, 0, tiled=True).reshape(rows, columns)  9.52 us
    pallas_call x1, Pallas kernels, local(): pl.pallas_call(gradient_kernel, out_shape=(shape(rows, width, dtype=BF16)...  6.64 us
    all_to_all x1, waiting for transfers between devices, sum_over_chan(): lax.all_to_all(copies, 'chan', 0, 0, tiled=True).reshape(rows, columns)  4.95 us
    pallas_call x1, Pallas kernels, local(): pl.pallas_call(summary_kernel, out_shape=(shape(2, rows, width), shape(2,...  4.62 us
  transfers between devices with their start and end apart: 2, of which 2 were waited for; matrix products, arithmetic and copies ran while one was open for 1% of the time, Pallas kernels for 0%

profile of v1, /device:TPU:1, one launch (start us, length us, event | category | flops | bytes accessed | tf_op | source)
XLA Modules:
  0.0 118.8 jit_solution(12253543964513790446)
XLA Ops:
  0.6 1.9 %copy.9.w_proj = bf16[256,560]{1,0:T(8,128)(2,1)} copy(bf16[256,560]{0,1:T(8,128)(2,1)} %param.9) | data formatting | bytes 573440 | tf_op args[2]
  2.5 2.0 %project.1 = (f32[128,256]{1,0:T(8,128)}, f32[128,256]{1,0:T(8,128)}, bf16[128,560]{1,0:T(8,128)(2,1)}) custom-call(bf16[128,256]{1,0:T(8,128)(2,1)} %signal.1, bf16[128,256]{1,0:T(8,128)(2,1)} %cotangent.1, bf16[256,560]{1,0:T(8,128)(2,1)} %copy.9.w_proj), custom_call_target="tpu_custom_call" | custom-call | tf_op jit(solution)/shard_map/project/pallas_call | solution.py:359
  4.5 15.7 %all_to_all.30 = bf16[8,16,560]{2,1,0:T(8,128)(2,1)S(1)} all-to-all(bf16[8,16,560]{2,1,0:T(8,128)(2,1)} %bitcast.10), channel_id=1, replica_groups=mesh['seq'=64,'chan'=8] {'chan'}, dimensions={0} | all-to-all | bytes 286720 | tf_op jit(solution)/shard_map/all_to_all | solution.py:343
  20.2 0.7 broadcast_in_dim.4
  20.9 0.0 copy-start.2
  20.9 4.3 %all-to-all-start.1 = ((bf16[8,16,560]{2,1,0:T(8,128)(2,1)}), bf16[8,16,560]{2,1,0:T(8,128)(2,1)S(1)}, u32[]{:S(2)}, u32[]{:S(2)}) async-start(bf16[8,16,560]{2,1,0:T(8,128)(2,1)} %broadcast_in_dim.4), calls=%async_computation.1 | async-start | bytes 327680 | tf_op jit(solution)/shard_map/all_to_all | solution.py:346
  25.2 0.0 copy-done.2
  25.2 0.6 copy.11.decay_log
  25.8 5.0 %all-to-all-done.1 = bf16[8,16,560]{2,1,0:T(8,128)(2,1)S(1)} async-done(((bf16[8,16,560]{2,1,0:T(8,128)(2,1)}), bf16[8,16,560]{2,1,0:T(8,128)(2,1)S(1)}, u32[]{:S(2)}, u32[]{:S(2)}) %all-to-all-start.1) | async-done | bytes 143392 | tf_op jit(solution)/shard_map/all_to_all | solution.py:346
  30.8 0.0 copy-start
  30.8 0.7 copy-done
  31.5 4.6 %summary.1 = (f32[2,128,256]{2,1,0:T(8,128)}, f32[2,128,256]{2,1,0:T(8,128)}, f32[4,12,8,256]{3,2,1,0:T(8,128)}, f32[4,8,256]{2,1,0:T(8,128)}, f32[64,4,128]{2,1,0:T(4,128)}) custom-call(bf16[128,560]{1,0:T(8,128)(2,1)} %bitcast.6, bf16[2,256,256]{2,1,0:T(8,128)(2,1)} %w_delta.3, f32[2,256]{1,0:T(2,128)} %bias.1, f32[2,12,256]{2,1,0:T(8,128)} %copy.11.decay_log, ...), custom_call_target="tpu_custom_call" | custom-call | tf_op jit(solution)/shard_map/summary/pallas_call | solution.py:365
  36.1 14.1 %all-to-all-start.2 = ((f32[64,4,128]{2,1,0:T(4,128)}), f32[64,4,128]{2,1,0:T(4,128)S(1)}, u32[]{:S(2)}, u32[]{:S(2)}) async-start(f32[64,4,128]{2,1,0:T(4,128)} %get-tuple-element.20), calls=%async_computation.2 | async-start | bytes 262144 | tf_op jit(solution)/shard_map/all_to_all | solution.py:381
  50.2 15.3 %all-to-all-done.2.parts = f32[64,4,128]{2,1,0:T(4,128)S(1)} async-done(((f32[64,4,128]{2,1,0:T(4,128)}), f32[64,4,128]{2,1,0:T(4,128)S(1)}, u32[]{:S(2)}, u32[]{:S(2)}) %all-to-all-start.2) | async-done | bytes 131104 | tf_op jit(solution)/shard_map/all_to_all | solution.py:381
  65.5 0.0 copy-start.1
  65.5 0.6 copy-done.1
  66.1 1.7 %shard_scan.1 = f32[64,2,128]{2,1,0:T(2,128)} custom-call(s32[1]{0:T(128)} %bitcast.3.place, f32[64,4,128]{2,1,0:T(4,128)} %copy-done.1), custom_call_target="tpu_custom_call" | custom-call | tf_op jit(solution)/shard_map/shard_scan/pallas_call | solution.py:383
  67.8 20.2 %all_to_all.31.entries = f32[64,2,128]{2,1,0:T(2,128)} all-to-all(f32[64,2,128]{2,1,0:T(2,128)} %shard_scan.1), channel_id=1, replica_groups=mesh['seq'=64,'chan'=8] {'seq'}, dimensions={0} | all-to-all | bytes 131072 | tf_op jit(solution)/shard_map/all_to_all | solution.py:393
  87.9 6.6 %gradient.1 = (bf16[128,256]{1,0:T(8,128)(2,1)}, bf16[128,560]{1,0:T(8,128)(2,1)}, f32[128,256]{1,0:T(8,128)}) custom-call(bf16[128,560]{1,0:T(8,128)(2,1)} %bitcast.7, bf16[2,256,256]{2,1,0:T(8,128)(2,1)} %w_delta.3, f32[2,12,256]{2,1,0:T(8,128)} %copy.11.decay_log, f32[1,256]{1,0:T(1,128)} %bitcast.11, f32[128,256]{1,0:T(8,128)} %get-tuple-element.14.signal, ...), custom_call_target="tpu_custom_call" | custom-call | tf_op jit(solution)/shard_map/gradient/pallas_call | solution.py:394
  94.6 12.5 %all_to_all.32 = bf16[8,16,560]{2,1,0:T(8,128)(2,1)S(1)} all-to-all(bf16[8,16,560]{2,1,0:T(8,128)(2,1)} %bitcast.9), channel_id=1, replica_groups=mesh['seq'=64,'chan'=8] {'chan'}, dimensions={0} | all-to-all | bytes 286720 | tf_op jit(solution)/shard_map/all_to_all | solution.py:343
  107.1 9.5 %all_to_all.33 = bf16[8,16,560]{2,1,0:T(8,128)(2,1)} all-to-all(bf16[8,16,560]{2,1,0:T(8,128)(2,1)S(1)} %broadcast_in_dim.5), channel_id=1, replica_groups=mesh['seq'=64,'chan'=8] {'chan'}, dimensions={0} | all-to-all | bytes 286720 | tf_op jit(solution)/shard_map/all_to_all | solution.py:346
  116.6 2.1 %finish.1 = bf16[128,256]{1,0:T(8,128)(2,1)} custom-call(bf16[128,560]{1,0:T(8,128)(2,1)} %bitcast.8, bf16[256,560]{1,0:T(8,128)(2,1)} %copy.9.w_proj, f32[128,256]{1,0:T(8,128)} %get-tuple-element.23.direct), custom_call_target="tpu_custom_call" | custom-call | tf_op jit(solution)/shard_map/finish/pallas_call | solution.py:426
  (3 shorter events, 0.1 us)
Async XLA Ops:
  20.9 4.3 %copy-start.2 = (f32[2,12,256]{2,0,1:T(2,128)S(1)}, f32[2,12,256]{2,0,1:T(2,128)}, u32[]{:S(2)}) copy-start(f32[2,12,256]{2,0,1:T(2,128)} %param.12) | copy-start | bytes 73732
  20.9 9.9 %all-to-all-start.1 = ((bf16[8,16,560]{2,1,0:T(8,128)(2,1)}), bf16[8,16,560]{2,1,0:T(8,128)(2,1)S(1)}, u32[]{:S(2)}, u32[]{:S(2)}) async-start(bf16[8,16,560]{2,1,0:T(8,128)(2,1)} %broadcast_in_dim.4), calls=%async_computation.1 | async-start | bytes 327680 | tf_op jit(solution)/shard_map/all_to_all | solution.py:346
  30.8 0.7 copy-start
  36.1 29.4 %all-to-all-start.2 = ((f32[64,4,128]{2,1,0:T(4,128)}), f32[64,4,128]{2,1,0:T(4,128)S(1)}, u32[]{:S(2)}, u32[]{:S(2)}) async-start(f32[64,4,128]{2,1,0:T(4,128)} %get-tuple-element.20), calls=%async_computation.2 | async-start | bytes 262144 | tf_op jit(solution)/shard_map/all_to_all | solution.py:381
  65.5 0.6 copy-start.1

commit v2 on v1

v2 whole, which is shorter than its diff:
```python
import math

import jax
import jax.numpy as jnp
from jax import lax
from jax.experimental import pallas as pl
from jax.experimental.pallas import tpu as pltpu
from jax.sharding import PartitionSpec as P

GROUPS = 8
LANES = 128
SLOTS = 16
LOG2E = math.log2(math.e)
LN2 = math.log(2.0)
FAR = 1e30
NT = (((1,), (1,)), ((), ()))
F32 = jnp.float32
BF16 = jnp.bfloat16


def dot(a, b, dims=(((1,), (0,)), ((), ()))):
    return lax.dot_general(a, b, dims, preferred_element_type=F32)


def grouping(rows, inverse=False):
    steps = rows // GROUPS
    row = lax.broadcasted_iota(jnp.int32, (rows, rows), 1 if inverse else 0)
    token = lax.broadcasted_iota(jnp.int32, (rows, rows), 0 if inverse else 1)
    return jnp.where(token == (row % GROUPS) * steps + row // GROUPS, 1.0, 0.0).astype(BF16)


def project_kernel(signal, w_proj, signal_out, part_out):
    grouped = dot(grouping(signal.shape[0]), signal[...])
    signal_out[...] = grouped
    part_out[...] = dot(grouped.astype(BF16), w_proj[...], NT).astype(BF16)


def prepare_kernel(cotangent, decay_log, cot_out, rates):
    cot_out[...] = dot(grouping(cotangent.shape[0]), cotangent[...])
    depth, _, width = decay_log.shape
    for n in range(depth):
        scaled = -jnp.exp(decay_log[n]) * LOG2E
        for way in range(2):
            rates[way, n] = jnp.broadcast_to(scaled[way : way + 1], (GROUPS, width))


def at(step):
    return pl.ds(pl.multiple_of(step * GROUPS, GROUPS), GROUPS)


def lane_block(block):
    return slice(block * LANES, (block + 1) * LANES)


def spread(row, column):
    return jnp.broadcast_to(row[:, column : column + 1], (GROUPS, LANES))


def summary_kernel(
    projected,
    w_delta,
    bias,
    rates,
    signal,
    cot,
    delta_out,
    slope_out,
    local_out,
    ahead_out,
    payload,
    gates,
    weight,
    fades,
):
    rows, width = signal.shape
    rank = w_delta.shape[1]
    depth = rates.shape[1]
    steps = rows // GROUPS
    blocks = width // LANES
    gates[:, : 4 * depth] = projected[:, 2 * rank :].astype(F32)
    payload[...] = jnp.zeros_like(payload)
    group = lax.broadcasted_iota(jnp.int32, (GROUPS, LANES), 0)
    for way in range(2):
        pre = dot(projected[:, way * rank : (way + 1) * rank], w_delta[way]) + bias[way : way + 1]
        delta = jnp.maximum(pre, 0.0) + jnp.log1p(jnp.exp(-jnp.abs(pre)))
        delta_out[way] = delta
        slope_out[way] = 1.0 / (1.0 + jnp.exp(-pre))
        weight[...] = delta * signal[...]
        falling = way == 1
        zero = jnp.zeros((GROUPS, LANES), F32)
        many = (zero,) * (blocks * depth)

        def walk_states(index, carry):
            states, total = carry
            step = steps - 1 - index if falling else index
            row = gates[at(step), :]
            d = [delta_out[way, at(step), lane_block(block)] for block in range(blocks)]
            w = [weight[at(step), lane_block(block)] for block in range(blocks)]
            result = []
            for n in range(depth):
                gate = spread(row, 2 * way * depth + n)
                for block in range(blocks):
                    fade = jnp.exp2(d[block] * rates[way, n, :, lane_block(block)])
                    fades[step, n, :, lane_block(block)] = fade
                    result.append(fade * states[n * blocks + block] + w[block] * gate)
            return (tuple(result), tuple(t + x for t, x in zip(total, d)))

        states, total = lax.fori_loop(0, steps, walk_states, (many, (zero,) * blocks))

        def walk_adjoints(index, carried):
            step = index if falling else steps - 1 - index
            row = gates[at(step), :]
            g = [cot[at(step), lane_block(block)] for block in range(blocks)]
            result = []
            for n in range(depth):
                gate = spread(row, (2 * way + 1) * depth + n)
                for block in range(blocks):
                    fade = fades[step, n, :, lane_block(block)]
                    result.append(fade * (g[block] * gate + carried[n * blocks + block]))
            return tuple(result)

        carried = lax.fori_loop(0, steps, walk_adjoints, many)
        for block in range(blocks):
            lanes = lane_block(block)

            def shift(array, by, down):
                return pltpu.roll(array, GROUPS - by if down else by, 0)

            def beyond(by, down):
                return group >= GROUPS - by if down else group < by

            whole = jnp.sum(total[block], 0, keepdims=True)
            for kind, down, finals in ((0, falling, states), (1, not falling, carried)):
                windows = []
                window = total[block]
                ahead = jnp.where(beyond(1, down), 0.0, shift(window, 1, down))
                for by in (1, 2, 4):
                    windows.append(jnp.where(beyond(by, down), FAR, window))
                    outside = beyond(by, down)
                    window = window + jnp.where(outside, 0.0, shift(window, by, down))
                    ahead = ahead + jnp.where(outside, 0.0, shift(ahead, by, down))
                ahead_out[2 * way + kind, :, lanes] = ahead
                edge = 0 if down else GROUPS - 1
                for n in range(depth):
                    rate = rates[way, n, :, lanes]
                    scanned = finals[n * blocks + block]
                    for by, span in zip((1, 2, 4), windows):
                        scanned = scanned + jnp.exp2(rate * span) * shift(scanned, by, down)
                    local_out[2 * way + kind, n, :, lanes] = jnp.where(
                        beyond(1, down), 0.0, shift(scanned, 1, down)
                    )
                    slot = (2 * way + kind) * SLOTS + n
                    payload[slot, block : block + 1] = scanned[edge : edge + 1]
                    payload[slot, blocks + block : blocks + block + 1] = jnp.exp2(
                        rate[:1] * whole
                    )


def shard_scan_kernel(place, parts, entries):
    shards, double, _ = parts.shape
    blocks = double // 2

    def scan(order):
        state = jnp.zeros((blocks, LANES), F32)
        for shard in order:
            entries[shard] = state
            state = parts[shard, blocks:] * state + parts[shard, :blocks]

    kind = place[0] // SLOTS
    falling = jnp.logical_or(kind == 1, kind == 2)

    @pl.when(falling)
    def _():
        scan(range(shards - 1, -1, -1))

    @pl.when(jnp.logical_not(falling))
    def _():
        scan(range(shards))


def gradient_kernel(
    projected,
    w_delta,
    rates,
    skip_gain,
    signal,
    cot,
    delta,
    slope,
    local,
    ahead,
    entries,
    layer_out,
    parts_out,
    direct_out,
    gates,
    weight,
    core,
    grad_pre,
    fades,
    kept,
    gate_grad,
):
    rows, width = signal.shape
    rank = w_delta.shape[1]
    depth = rates.shape[1]
    steps = rows // GROUPS
    blocks = width // LANES
    gates[:, : 4 * depth] = projected[:, 2 * rank :].astype(F32)
    core[...] = skip_gain[...] * signal[...]
    direct_out[...] = skip_gain[...] * cot[...]
    gate_grad[...] = jnp.zeros_like(gate_grad)
    lane = lax.broadcasted_iota(jnp.int32, (GROUPS, LANES), 1)
    for way in range(2):
        weight[...] = delta[way] * signal[...]
        falling = way == 1
        first = 2 * way * depth

        def entering(kind):
            gap = [ahead[2 * way + kind, :, lane_block(block)] for block in range(blocks)]
            return tuple(
                local[2 * way + kind, n, :, lane_block(block)]
                + jnp.exp2(gap[block] * rates[way, n, :, lane_block(block)])
                * entries[(2 * way + kind) * SLOTS + n, block : block + 1]
                for n in range(depth)
                for block in range(blocks)
            )

        def pieces(array, step):
            return [array[at(step), lane_block(block)] for block in range(blocks)]

        def total_over_lanes(products):
            return jnp.sum(sum(products[1:], products[0]), 1, keepdims=True)

        def walk_states(index, states):
            step = steps - 1 - index if falling else index
            row = gates[at(step), :]
            d, w, g = pieces(delta.at[way], step), pieces(weight, step), pieces(cot, step)
            total = pieces(core, step)
            merged = gate_grad[at(step), :]
            result = []
            for n in range(depth):
                gate_in = spread(row, first + n)
                gate_out = spread(row, first + depth + n)
                products = []
                for block in range(blocks):
                    lanes = lane_block(block)
                    fade = jnp.exp2(d[block] * rates[way, n, :, lanes])
                    fades[step, n, :, lanes] = fade
                    faded = fade * states[n * blocks + block]
                    kept[step, n, :, lanes] = faded
                    state = faded + w[block] * gate_in
                    total[block] = total[block] + gate_out * state
                    products.append(g[block] * state)
                    result.append(state)
                merged = jnp.where(lane == first + depth + n, total_over_lanes(products), merged)
            for block in range(blocks):
                core[at(step), lane_block(block)] = total[block]
            gate_grad[at(step), :] = merged
            return tuple(result)

        lax.fori_loop(0, steps, walk_states, entering(0))

        def walk_adjoints(index, carried):
            step = index if falling else steps - 1 - index
            row = gates[at(step), :]
            w, g = pieces(weight, step), pieces(cot, step)
            merged = gate_grad[at(step), :]
            through = [jnp.zeros((GROUPS, LANES), F32)] * blocks
            fading = [jnp.zeros((GROUPS, LANES), F32)] * blocks
            result = []
            for n in range(depth):
                gate_in = spread(row, first + n)
                gate_out = spread(row, first + depth + n)
                products = []
                for block in range(blocks):
                    lanes = lane_block(block)
                    adjoint = g[block] * gate_out + carried[n * blocks + block]
                    result.append(fades[step, n, :, lanes] * adjoint)
                    through[block] = through[block] + adjoint * gate_in
                    fading[block] = fading[block] + (
                        adjoint * kept[step, n, :, lanes] * rates[way, n, :, lanes]
                    )
                    products.append(adjoint * w[block])
                merged = jnp.where(lane == first + n, total_over_lanes(products), merged)
            gate_grad[at(step), :] = merged
            for block in range(blocks):
                lanes = lane_block(block)
                grad_delta = through[block] * signal[at(step), lanes] + fading[block] * LN2
                direct_out[at(step), lanes] = (
                    direct_out[at(step), lanes] + through[block] * delta[way, at(step), lanes]
                )
                grad_pre[way, at(step), lanes] = grad_delta * slope[way, at(step), lanes]
            return tuple(result)

        lax.fori_loop(0, steps, walk_adjoints, entering(1))

    for way in range(2):
        parts_out[:, way * rank : (way + 1) * rank] = dot(
            grad_pre[way].astype(BF16), w_delta[way], NT
        ).astype(BF16)
    parts_out[:, 2 * rank :] = gate_grad[:, : 4 * depth].astype(BF16)
    ungroup = grouping(rows, inverse=True)
    layer_out[...] = dot(ungroup, core[...].astype(BF16)).astype(BF16)


def finish_kernel(grad_proj, w_proj, direct, signal_grad):
    total = dot(grad_proj[...], w_proj[...]) + direct[...]
    ungroup = grouping(direct.shape[0], inverse=True)
    signal_grad[...] = dot(ungroup, total.astype(BF16)).astype(BF16)


def shape(*dims, dtype=F32):
    return jax.ShapeDtypeStruct(dims, dtype)


def sum_over_chan(part):
    count = lax.axis_size("chan")
    rows, columns = part.shape
    pieces = part.reshape(count, rows // count, columns)
    arrived = lax.all_to_all(pieces, "chan", 0, 0, tiled=True)
    total = jnp.sum(arrived.astype(F32), 0).astype(BF16)
    copies = jnp.broadcast_to(total[None], (count,) + total.shape)
    return lax.all_to_all(copies, "chan", 0, 0, tiled=True).reshape(rows, columns)


def kernel(body, out_shape, mebibytes, scratch=(), cost=0, **more):
    return pl.pallas_call(
        body,
        out_shape=out_shape,
        scratch_shapes=[pltpu.VMEM(dims, dtype) for dims, dtype in scratch],
        compiler_params=pltpu.CompilerParams(vmem_limit_bytes=mebibytes << 20),
        cost_estimate=pl.CostEstimate(flops=cost, bytes_accessed=cost, transcendentals=0),
        name=body.__name__,
        **more,
    )


def local(signal, cotangent, w_proj, w_delta, delta_bias, decay_log, skip_gain):
    rows, width = signal.shape
    columns = w_proj.shape[1]
    depth = decay_log.shape[1]
    steps = rows // GROUPS
    blocks = width // LANES
    shards = lax.axis_size("seq")
    if shards != 4 * SLOTS or depth > SLOTS:
        raise ValueError("shard count")
    w_turned = w_proj.T
    place = lax.axis_index("seq").astype(jnp.int32).reshape(1)
    signal_wide, part = kernel(
        project_kernel, (shape(rows, width), shape(rows, columns, dtype=BF16)), 8
    )(signal, w_turned)
    cot_wide, rates = kernel(
        prepare_kernel,
        (shape(rows, width), shape(2, depth, GROUPS, width)),
        8,
        cost=1 << 20,
    )(cotangent, decay_log.transpose(1, 0, 2))
    projected = sum_over_chan(part)
    stack = ((steps, depth, GROUPS, width), F32)
    delta, slope, local_states, ahead, payload = kernel(
        summary_kernel,
        (
            shape(2, rows, width),
            shape(2, rows, width),
            shape(4, depth, GROUPS, width),
            shape(4, GROUPS, width),
            shape(shards, 2 * blocks, LANES),
        ),
        20,
        (((rows, LANES), F32), ((rows, width), F32), stack),
    )(projected, w_delta, delta_bias, rates, signal_wide, cot_wide)
    parts = lax.all_to_all(payload, "seq", 0, 0, tiled=True)
    entries = kernel(
        shard_scan_kernel,
        shape(shards, blocks, LANES),
        4,
        in_specs=[
            pl.BlockSpec(memory_space=pltpu.SMEM),
            pl.BlockSpec(memory_space=pltpu.VMEM),
        ],
        out_specs=pl.BlockSpec(memory_space=pltpu.VMEM),
    )(place, parts)
    entries = lax.all_to_all(entries, "seq", 0, 0, tiled=True)
    layer_out, grad_parts, direct = kernel(
        gradient_kernel,
        (
            shape(rows, width, dtype=BF16),
            shape(rows, columns, dtype=BF16),
            shape(rows, width),
        ),
        24,
        (
            ((rows, LANES), F32),
            ((rows, width), F32),
            ((rows, width), F32),
            ((2, rows, width), F32),
            stack,
            stack,
            ((rows, LANES), F32),
        ),
    )(
        projected,
        w_delta,
        rates,
        skip_gain.reshape(1, width),
        signal_wide,
        cot_wide,
        delta,
        slope,
        local_states,
        ahead,
        entries,
    )
    grad_proj = sum_over_chan(grad_parts)
    signal_grad = kernel(finish_kernel, shape(rows, width, dtype=BF16), 8)(
        grad_proj, w_turned, direct
    )
    return (layer_out, signal_grad)


def solution(mesh):
    in_specs = (
        P("seq", "chan"),
        P("seq", "chan"),
        P("chan", None),
        P(None, None, "chan"),
        P(None, "chan"),
        P(None, None, "chan"),
        P("chan"),
    )
    out_specs = (P("seq", "chan"), P("seq", "chan"))
    return jax.shard_map(local, mesh=mesh, in_specs=in_specs, out_specs=out_specs, check_vma=False)
```

time: 119 us -> 131 us (1.10)
  Pallas kernels: 17.1 us -> 31.9 us
  blocking collectives: 57.8 us -> 54.2 us
    pallas_call x5 -> x6, Pallas kernels: 17.1 us -> 31.9 us  [the longest x1 23.3 us: local(): kernel(gradient_kernel, (shape(rows, width, dtype=BF16), shape(rows, colu...]
    all_to_all x2, blocking collectives: 28.1 us -> 25.4 us  [sum_over_chan(): arrived = lax.all_to_all(pieces, 'chan', 0, 0, tiled=True)]
    unnamed x8 -> x16, local copies, waits for them, and re-layouts: 3.8 us -> 3.17 us
  transfers between devices with their start and end apart: 2 -> 2, of which waited for: 2 -> 2; matrix products, arithmetic and copies ran while one was open for 1% -> 0% of each run, Pallas kernels for 0% -> 0%
where the time goes in v2:
time: 131 us
  blocking collectives  54.2 us (41%)
  Pallas kernels  31.9 us (24%)
  waiting for transfers between devices  20.7 us (16%)
  starting transfers between devices  19.1 us (15%)
  local copies, waits for them, and re-layouts  3.86 us (3%)
    all_to_all x2, blocking collectives, sum_over_chan(): arrived = lax.all_to_all(pieces, 'chan', 0, 0, tiled=True)  25.4 us
    pallas_call x1, Pallas kernels, local(): kernel(gradient_kernel, (shape(rows, width, dtype=BF16), shape(rows, colu...  23.3 us
    all_to_all x1, blocking collectives, local(): entries = lax.all_to_all(entries, 'seq', 0, 0, tiled=True)  19.9 us
    all_to_all x1, waiting for transfers between devices, local(): parts = lax.all_to_all(payload, 'seq', 0, 0, tiled=True)  15.3 us
    all_to_all x1, starting transfers between devices, local(): parts = lax.all_to_all(payload, 'seq', 0, 0, tiled=True)  14.8 us
    all_to_all x1, blocking collectives, sum_over_chan(): lax.all_to_all(copies, 'chan', 0, 0, tiled=True).reshape(rows, columns)  8.98 us
    pallas_call x1, Pallas kernels, local(): kernel(summary_kernel, (shape(2, rows, width), shape(2, rows, width), sha...  6.97 us
    all_to_all x1, waiting for transfers between devices, sum_over_chan(): lax.all_to_all(copies, 'chan', 0, 0, tiled=True).reshape(rows, columns)  5.41 us
  transfers between devices with their start and end apart: 2, of which 2 were waited for; matrix products, arithmetic and copies ran while one was open for 0% of the time, Pallas kernels for 0%

profile of v2, /device:TPU:1, one launch (start us, length us, event | category | flops | bytes accessed | tf_op | source)
XLA Modules:
  0.0 130.5 jit_solution(14417832809931508634)
XLA Ops:
  0.6 0.0 copy-start
  0.6 0.9 copy-done
  1.6 0.8 copy-done.4
  2.4 0.3 project_kernel.1
  2.7 14.8 %all_to_all.30 = bf16[8,16,560]{2,1,0:T(8,128)(2,1)S(1)} all-to-all(bf16[8,16,560]{2,1,0:T(8,128)(2,1)S(1)} %bitcast.14), channel_id=1, replica_groups=mesh['seq'=64,'chan'=8] {'chan'}, dimensions={0} | all-to-all | bytes 286720 | tf_op jit(solution)/shard_map/all_to_all | solution.py:321
  17.6 0.0 copy-start.2
  17.6 0.7 broadcast_in_dim.4
  18.2 4.3 %all-to-all-start.1 = ((bf16[8,16,560]{2,1,0:T(8,128)(2,1)}), bf16[8,16,560]{2,1,0:T(8,128)(2,1)S(1)}, u32[]{:S(2)}, u32[]{:S(2)}) async-start(bf16[8,16,560]{2,1,0:T(8,128)(2,1)} %broadcast_in_dim.4), calls=%async_computation.1 | async-start | bytes 327680 | tf_op jit(solution)/shard_map/all_to_all | solution.py:324
  22.6 0.0 copy-done.3
  22.6 0.0 copy-done.5
  22.6 0.2 prepare_kernel.1
  22.7 5.4 %all-to-all-done.1 = bf16[8,16,560]{2,1,0:T(8,128)(2,1)S(1)} async-done(((bf16[8,16,560]{2,1,0:T(8,128)(2,1)}), bf16[8,16,560]{2,1,0:T(8,128)(2,1)S(1)}, u32[]{:S(2)}, u32[]{:S(2)}) %all-to-all-start.1) | async-done | bytes 143392 | tf_op jit(solution)/shard_map/all_to_all | solution.py:324
  28.1 0.7 copy-done.6
  28.8 7.0 %summary_kernel.1 = (f32[2,128,256]{2,1,0:T(8,128)S(1)}, f32[2,128,256]{2,1,0:T(8,128)S(1)}, f32[4,12,8,256]{3,2,1,0:T(8,128)S(1)}, f32[4,8,256]{2,1,0:T(8,128)S(1)}, f32[64,4,128]{2,1,0:T(4,128)}) custom-call(bf16[128,560]{1,0:T(8,128)(2,1)S(1)} %bitcast.8, bf16[2,256,256]{2,1,0:T(8,128)(2,1)S(1)} %copy-done.2, f32[2,256]{1,0:T(2,128)S(1)} %copy-done.6, ...), custom_call_target="tpu_custom_call" | custom-call | tf_op jit(solution)/shard_map/summary_kernel/pallas_call | solution.py:361
  35.8 14.8 %all-to-all-start.2 = ((f32[64,4,128]{2,1,0:T(4,128)}), f32[64,4,128]{2,1,0:T(4,128)S(1)}, u32[]{:S(2)}, u32[]{:S(2)}) async-start(f32[64,4,128]{2,1,0:T(4,128)} %get-tuple-element.22), calls=%async_computation.2 | async-start | bytes 262144 | tf_op jit(solution)/shard_map/all_to_all | solution.py:373
  50.6 15.3 %all-to-all-done.2.parts = f32[64,4,128]{2,1,0:T(4,128)S(1)} async-done(((f32[64,4,128]{2,1,0:T(4,128)}), f32[64,4,128]{2,1,0:T(4,128)S(1)}, u32[]{:S(2)}, u32[]{:S(2)}) %all-to-all-start.2) | async-done | bytes 131104 | tf_op jit(solution)/shard_map/all_to_all | solution.py:373
  65.9 0.1 shard_scan_kernel.1
  66.0 19.9 %all_to_all.31.entries = f32[64,2,128]{2,1,0:T(2,128)S(1)} all-to-all(f32[64,2,128]{2,1,0:T(2,128)S(1)} %shard_scan_kernel.1), channel_id=1, replica_groups=mesh['seq'=64,'chan'=8] {'seq'}, dimensions={0} | all-to-all | bytes 131072 | tf_op jit(solution)/shard_map/all_to_all | solution.py:384
  85.9 0.7 copy-done.7
  86.6 23.3 %gradient_kernel.1 = (bf16[128,256]{1,0:T(8,128)(2,1)}, bf16[128,560]{1,0:T(8,128)(2,1)S(1)}, f32[128,256]{1,0:T(8,128)S(1)}) custom-call(bf16[128,560]{1,0:T(8,128)(2,1)S(1)} %bitcast.9, bf16[2,256,256]{2,1,0:T(8,128)(2,1)S(1)} %copy-done.2, f32[2,12,8,256]{3,2,1,0:T(8,128)S(1)} %get-tuple-element.15.rates, f32[1,256]{1,0:T(1,128)S(1)} %bitcast.16, ...), custom_call_target="tpu_custom_call" | custom-call | tf_op jit(solution)/shard_map/gradient_kernel/pallas_call | solution.py:385
  109.8 10.6 %all_to_all.32 = bf16[8,16,560]{2,1,0:T(8,128)(2,1)S(1)} all-to-all(bf16[8,16,560]{2,1,0:T(8,128)(2,1)S(1)} %bitcast.13), channel_id=1, replica_groups=mesh['seq'=64,'chan'=8] {'chan'}, dimensions={0} | all-to-all | bytes 286720 | tf_op jit(solution)/shard_map/all_to_all | solution.py:321
  120.5 0.0 copy-start.1
  120.5 9.0 %all_to_all.33 = bf16[8,16,560]{2,1,0:T(8,128)(2,1)S(1)} all-to-all(bf16[8,16,560]{2,1,0:T(8,128)(2,1)S(1)} %broadcast_in_dim.5), channel_id=1, replica_groups=mesh['seq'=64,'chan'=8] {'chan'}, dimensions={0} | all-to-all | bytes 286720 | tf_op jit(solution)/shard_map/all_to_all | solution.py:324
  129.5 1.0 finish_kernel.1
  (10 shorter events, 0.1 us)
Async XLA Ops:
  0.6 1.0 copy-start
  1.6 0.8 copy-start.4
  17.6 10.6 %copy-start.2 = (bf16[2,256,256]{2,1,0:T(8,128)(2,1)S(1)}, bf16[2,256,256]{2,1,0:T(8,128)(2,1)}, u32[]{:S(2)}) copy-start(bf16[2,256,256]{2,1,0:T(8,128)(2,1)} %w_delta.3) | copy-start | bytes 786436
  18.2 4.3 %copy-start.3 = (bf16[128,256]{1,0:T(8,128)(2,1)S(1)}, bf16[128,256]{1,0:T(8,128)(2,1)}, u32[]{:S(2)}) copy-start(bf16[128,256]{1,0:T(8,128)(2,1)} %cotangent.1) | copy-start | bytes 196612
  18.2 4.3 %copy-start.5 = (f32[2,12,256]{2,0,1:T(2,128)S(1)}, f32[2,12,256]{2,0,1:T(2,128)}, u32[]{:S(2)}) copy-start(f32[2,12,256]{2,0,1:T(2,128)} %param.12) | copy-start | bytes 73732
  18.2 9.9 %all-to-all-start.1 = ((bf16[8,16,560]{2,1,0:T(8,128)(2,1)}), bf16[8,16,560]{2,1,0:T(8,128)(2,1)S(1)}, u32[]{:S(2)}, u32[]{:S(2)}) async-start(bf16[8,16,560]{2,1,0:T(8,128)(2,1)} %broadcast_in_dim.4), calls=%async_computation.1 | async-start | bytes 327680 | tf_op jit(solution)/shard_map/all_to_all | solution.py:324
  28.1 0.7 copy-start.6
  35.8 30.1 %all-to-all-start.2 = ((f32[64,4,128]{2,1,0:T(4,128)}), f32[64,4,128]{2,1,0:T(4,128)S(1)}, u32[]{:S(2)}, u32[]{:S(2)}) async-start(f32[64,4,128]{2,1,0:T(4,128)} %get-tuple-element.22), calls=%async_computation.2 | async-start | bytes 262144 | tf_op jit(solution)/shard_map/all_to_all | solution.py:373
  85.9 0.7 copy-start.7
  120.5 9.0 %copy-start.1 = (bf16[256,560]{0,1:T(8,128)(2,1)S(1)}, bf16[256,560]{0,1:T(8,128)(2,1)}, u32[]{:S(2)}) copy-start(bf16[256,560]{0,1:T(8,128)(2,1)} %param.9) | copy-start | bytes 860164

commit v3 on v2

--- a/solution.py
+++ b/solution.py
@@ -9,7 +9,6 @@
 
 GROUPS = 8
 LANES = 128
-SLOTS = 16
 LOG2E = math.log2(math.e)
 LN2 = math.log(2.0)
 FAR = 1e30
@@ -35,13 +34,17 @@
     part_out[...] = dot(grouped.astype(BF16), w_proj[...], NT).astype(BF16)
 
 
-def prepare_kernel(cotangent, decay_log, cot_out, rates):
+def prepare_kernel(cotangent, decay_log, bias, skip_gain, cot_out, rates, flat, bias_out, gain_out):
     cot_out[...] = dot(grouping(cotangent.shape[0]), cotangent[...])
+    bias_out[...] = bias[...]
+    gain_out[...] = skip_gain[...]
     depth, _, width = decay_log.shape
+    flat[...] = jnp.zeros_like(flat)
     for n in range(depth):
         scaled = -jnp.exp(decay_log[n]) * LOG2E
         for way in range(2):
             rates[way, n] = jnp.broadcast_to(scaled[way : way + 1], (GROUPS, width))
+            flat[way, n : n + 1] = scaled[way : way + 1]
 
 
 def at(step):
@@ -52,8 +55,17 @@
     return slice(block * LANES, (block + 1) * LANES)
 
 
-def spread(row, column):
-    return jnp.broadcast_to(row[:, column : column + 1], (GROUPS, LANES))
+def spread_gates(gates, spread):
+    count = gates.shape[1]
+    for pair in range(count // 2):
+        source = lax.broadcasted_iota(jnp.int32, (count, 2 * LANES), 0)
+        lane = lax.broadcasted_iota(jnp.int32, (count, 2 * LANES), 1)
+        pick = jnp.where(source == 2 * pair + lane // LANES, 1.0, 0.0).astype(BF16)
+        spread[:, pair * 2 * LANES : (pair + 1) * 2 * LANES] = dot(gates, pick)
+
+
+def gate_at(spread, step, column):
+    return spread[at(step), column * LANES : (column + 1) * LANES]
 
 
 def summary_kernel(
@@ -68,16 +80,16 @@
     local_out,
     ahead_out,
     payload,
-    gates,
     weight,
     fades,
+    spread,
 ):
     rows, width = signal.shape
     rank = w_delta.shape[1]
     depth = rates.shape[1]
     steps = rows // GROUPS
     blocks = width // LANES
-    gates[:, : 4 * depth] = projected[:, 2 * rank :].astype(F32)
+    spread_gates(projected[:, 2 * rank :], spread)
     payload[...] = jnp.zeros_like(payload)
     group = lax.broadcasted_iota(jnp.int32, (GROUPS, LANES), 0)
     for way in range(2):
@@ -93,12 +105,11 @@
         def walk_states(index, carry):
             states, total = carry
             step = steps - 1 - index if falling else index
-            row = gates[at(step), :]
             d = [delta_out[way, at(step), lane_block(block)] for block in range(blocks)]
             w = [weight[at(step), lane_block(block)] for block in range(blocks)]
             result = []
             for n in range(depth):
-                gate = spread(row, 2 * way * depth + n)
+                gate = gate_at(spread, step, 2 * way * depth + n)
                 for block in range(blocks):
                     fade = jnp.exp2(d[block] * rates[way, n, :, lane_block(block)])
                     fades[step, n, :, lane_block(block)] = fade
@@ -109,11 +120,10 @@
 
         def walk_adjoints(index, carried):
             step = index if falling else steps - 1 - index
-            row = gates[at(step), :]
             g = [cot[at(step), lane_block(block)] for block in range(blocks)]
             result = []
             for n in range(depth):
-                gate = spread(row, (2 * way + 1) * depth + n)
+                gate = gate_at(spread, step, (2 * way + 1) * depth + n)
                 for block in range(blocks):
                     fade = fades[step, n, :, lane_block(block)]
                     result.append(fade * (g[block] * gate + carried[n * blocks + block]))
@@ -149,33 +159,74 @@
                     local_out[2 * way + kind, n, :, lanes] = jnp.where(
                         beyond(1, down), 0.0, shift(scanned, 1, down)
                     )
-                    slot = (2 * way + kind) * SLOTS + n
-                    payload[slot, block : block + 1] = scanned[edge : edge + 1]
-                    payload[slot, blocks + block : blocks + block + 1] = jnp.exp2(
-                        rate[:1] * whole
-                    )
-
-
-def shard_scan_kernel(place, parts, entries):
-    shards, double, _ = parts.shape
-    blocks = double // 2
-
-    def scan(order):
-        state = jnp.zeros((blocks, LANES), F32)
-        for shard in order:
-            entries[shard] = state
-            state = parts[shard, blocks:] * state + parts[shard, :blocks]
-
-    kind = place[0] // SLOTS
+                    payload[2 * way + kind, n : n + 1, lanes] = scanned[edge : edge + 1]
+                payload[2 * way + kind, depth : depth + 1, lanes] = whole
+
+
+def fall_or_rise(kind, run):
     falling = jnp.logical_or(kind == 1, kind == 2)
 
     @pl.when(falling)
     def _():
-        scan(range(shards - 1, -1, -1))
+        run(True)
 
     @pl.when(jnp.logical_not(falling))
     def _():
-        scan(range(shards))
+        run(False)
+
+
+def order(count, falling):
+    return range(count - 1, -1, -1) if falling else range(count)
+
+
+def shard_fade(parts, flat, way, shard):
+    depth = parts.shape[1] - 4
+    return jnp.exp2(flat[way] * parts[shard, depth : depth + 1])
+
+
+def row_kernel(place, parts, flat, copies):
+    shards, slots, width = parts.shape
+    depth = slots - 4
+    kind = place[1]
+    slot = lax.broadcasted_iota(jnp.int32, (slots, width), 0)
+
+    def run(falling):
+        state = jnp.zeros((slots, width), F32)
+        for shard in order(shards, falling):
+            state = shard_fade(parts, flat, kind // 2, shard) * state + parts[shard]
+        total = parts[0, depth : depth + 1]
+        for shard in range(1, shards):
+            total = total + parts[shard, depth : depth + 1]
+        coarse = total.astype(BF16).astype(F32)
+        packed = jnp.where(slot == depth, coarse, state)
+        packed = jnp.where(slot == depth + 1, total - coarse, packed).astype(BF16)
+        for copy in range(copies.shape[0]):
+            copies[copy] = packed
+
+    fall_or_rise(kind, run)
+
+
+def entry_kernel(place, rows, parts, flat, entries):
+    count, slots, width = rows.shape
+    shards = parts.shape[0]
+    depth = slots - 4
+    here = place[0]
+    kind = place[1]
+    rates = flat[kind // 2]
+
+    def run(falling):
+        state = jnp.zeros((slots, width), F32)
+        for row in order(count, falling):
+            block = rows[row].astype(F32)
+            total = block[depth : depth + 1] + block[depth + 1 : depth + 2]
+            passed = jnp.exp2(rates * total) * state + block
+            before = row > here if falling else row < here
+            state = jnp.where(before, passed, state)
+        for shard in order(shards, falling):
+            entries[shard] = state
+            state = shard_fade(parts, flat, kind // 2, shard) * state + parts[shard]
+
+    fall_or_rise(kind, run)
 
 
 def gradient_kernel(
@@ -193,24 +244,22 @@
     layer_out,
     parts_out,
     direct_out,
-    gates,
     weight,
     core,
     grad_pre,
     fades,
     kept,
-    gate_grad,
+    products,
+    spread,
 ):
     rows, width = signal.shape
     rank = w_delta.shape[1]
     depth = rates.shape[1]
     steps = rows // GROUPS
     blocks = width // LANES
-    gates[:, : 4 * depth] = projected[:, 2 * rank :].astype(F32)
+    spread_gates(projected[:, 2 * rank :], spread)
     core[...] = skip_gain[...] * signal[...]
     direct_out[...] = skip_gain[...] * cot[...]
-    gate_grad[...] = jnp.zeros_like(gate_grad)
-    lane = lax.broadcasted_iota(jnp.int32, (GROUPS, LANES), 1)
     for way in range(2):
         weight[...] = delta[way] * signal[...]
         falling = way == 1
@@ -221,7 +270,7 @@
             return tuple(
                 local[2 * way + kind, n, :, lane_block(block)]
                 + jnp.exp2(gap[block] * rates[way, n, :, lane_block(block)])
-                * entries[(2 * way + kind) * SLOTS + n, block : block + 1]
+                * entries[2 * way + kind, n : n + 1, lane_block(block)]
                 for n in range(depth)
                 for block in range(blocks)
             )
@@ -229,20 +278,21 @@
         def pieces(array, step):
             return [array[at(step), lane_block(block)] for block in range(blocks)]
 
-        def total_over_lanes(products):
-            return jnp.sum(sum(products[1:], products[0]), 1, keepdims=True)
+        def put_products(which, step, rows_of):
+            start = pl.multiple_of(step * depth * GROUPS, 2 * GROUPS)
+            for block in range(blocks):
+                stacked = jnp.concatenate(rows_of[block], 0).astype(BF16)
+                products[which, pl.ds(start, depth * GROUPS), lane_block(block)] = stacked
 
         def walk_states(index, states):
             step = steps - 1 - index if falling else index
-            row = gates[at(step), :]
             d, w, g = pieces(delta.at[way], step), pieces(weight, step), pieces(cot, step)
             total = pieces(core, step)
-            merged = gate_grad[at(step), :]
+            rows_of = [[] for _ in range(blocks)]
             result = []
             for n in range(depth):
-                gate_in = spread(row, first + n)
-                gate_out = spread(row, first + depth + n)
-                products = []
+                gate_in = gate_at(spread, step, first + n)
+                gate_out = gate_at(spread, step, first + depth + n)
                 for block in range(blocks):
                     lanes = lane_block(block)
                     fade = jnp.exp2(d[block] * rates[way, n, :, lanes])
@@ -251,28 +301,25 @@
                     kept[step, n, :, lanes] = faded
                     state = faded + w[block] * gate_in
                     total[block] = total[block] + gate_out * state
-                    products.append(g[block] * state)
+                    rows_of[block].append(g[block] * state)
                     result.append(state)
-                merged = jnp.where(lane == first + depth + n, total_over_lanes(products), merged)
             for block in range(blocks):
                 core[at(step), lane_block(block)] = total[block]
-            gate_grad[at(step), :] = merged
+            put_products(2 * way + 1, step, rows_of)
             return tuple(result)
 
         lax.fori_loop(0, steps, walk_states, entering(0))
 
         def walk_adjoints(index, carried):
             step = index if falling else steps - 1 - index
-            row = gates[at(step), :]
             w, g = pieces(weight, step), pieces(cot, step)
-            merged = gate_grad[at(step), :]
+            rows_of = [[] for _ in range(blocks)]
             through = [jnp.zeros((GROUPS, LANES), F32)] * blocks
             fading = [jnp.zeros((GROUPS, LANES), F32)] * blocks
             result = []
             for n in range(depth):
-                gate_in = spread(row, first + n)
-                gate_out = spread(row, first + depth + n)
-                products = []
+                gate_in = gate_at(spread, step, first + n)
+                gate_out = gate_at(spread, step, first + depth + n)
                 for block in range(blocks):
                     lanes = lane_block(block)
                     adjoint = g[block] * gate_out + carried[n * blocks + block]
@@ -281,9 +328,8 @@
                     fading[block] = fading[block] + (
                         adjoint * kept[step, n, :, lanes] * rates[way, n, :, lanes]
                     )
-                    products.append(adjoint * w[block])
-                merged = jnp.where(lane == first + n, total_over_lanes(products), merged)
-            gate_grad[at(step), :] = merged
+                    rows_of[block].append(adjoint * w[block])
+            put_products(2 * way, step, rows_of)
             for block in range(blocks):
                 lanes = lane_block(block)
                 grad_delta = through[block] * signal[at(step), lanes] + fading[block] * LN2
@@ -299,7 +345,21 @@
         parts_out[:, way * rank : (way + 1) * rank] = dot(
             grad_pre[way].astype(BF16), w_delta[way], NT
         ).astype(BF16)
-    parts_out[:, 2 * rank :] = gate_grad[:, : 4 * depth].astype(BF16)
+    ones = jnp.ones((width, LANES), BF16)
+    lane = lax.broadcasted_iota(jnp.int32, (GROUPS, LANES), 1)
+    height = depth * GROUPS
+    for start in range(0, steps, 4):
+        merged = [jnp.zeros((GROUPS, LANES), F32)] * 4
+        for which in range(4):
+            sums = dot(products[which, start * height : (start + 4) * height], ones)
+            for step in range(4):
+                for n in range(depth):
+                    row = step * height + n * GROUPS
+                    merged[step] = jnp.where(
+                        lane == which * depth + n, sums[row : row + GROUPS], merged[step]
+                    )
+        stacked = jnp.concatenate(merged, 0)[:, : 4 * depth].astype(BF16)
+        parts_out[start * GROUPS : (start + 4) * GROUPS, 2 * rank :] = stacked
     ungroup = grouping(rows, inverse=True)
     layer_out[...] = dot(ungroup, core[...].astype(BF16)).astype(BF16)
 
@@ -341,22 +401,38 @@
     columns = w_proj.shape[1]
     depth = decay_log.shape[1]
     steps = rows // GROUPS
-    blocks = width // LANES
     shards = lax.axis_size("seq")
-    if shards != 4 * SLOTS or depth > SLOTS:
+    if shards % 4:
         raise ValueError("shard count")
     w_turned = w_proj.T
-    place = lax.axis_index("seq").astype(jnp.int32).reshape(1)
+    shard = lax.axis_index("seq").astype(jnp.int32)
+    place = jnp.stack([shard // 4, shard % 4])
+    along_y = [[z * 4 + y for y in range(4)] for z in range(shards // 4)]
+    along_z = [[z * 4 + y for z in range(shards // 4)] for y in range(4)]
+    slots = depth + 4
+    whole = pl.BlockSpec(memory_space=pltpu.VMEM)
+    scalars = pl.BlockSpec(memory_space=pltpu.SMEM)
+
+    def exchange(array, groups):
+        return lax.all_to_all(array, "seq", 0, 0, tiled=True, axis_index_groups=groups)
+
     signal_wide, part = kernel(
         project_kernel, (shape(rows, width), shape(rows, columns, dtype=BF16)), 8
     )(signal, w_turned)
-    cot_wide, rates = kernel(
+    cot_wide, rates, flat, bias, gain = kernel(
         prepare_kernel,
-        (shape(rows, width), shape(2, depth, GROUPS, width)),
+        (
+            shape(rows, width),
+            shape(2, depth, GROUPS, width),
+            shape(2, slots, width),
+            shape(2, width),
+            shape(1, width),
+        ),
         8,
         cost=1 << 20,
-    )(cotangent, decay_log.transpose(1, 0, 2))
+    )(cotangent, decay_log.transpose(1, 0, 2), delta_bias, skip_gain.reshape(1, width))
     projected = sum_over_chan(part)
+    wide = ((rows, 4 * depth * LANES), F32)
     stack = ((steps, depth, GROUPS, width), F32)
     delta, slope, local_states, ahead, payload = kernel(
         summary_kernel,
@@ -365,23 +441,28 @@
             shape(2, rows, width),
             shape(4, depth, GROUPS, width),
             shape(4, GROUPS, width),
-            shape(shards, 2 * blocks, LANES),
+            shape(4, slots, width),
         ),
         20,
-        (((rows, LANES), F32), ((rows, width), F32), stack),
-    )(projected, w_delta, delta_bias, rates, signal_wide, cot_wide)
-    parts = lax.all_to_all(payload, "seq", 0, 0, tiled=True)
+        (((rows, width), F32), stack, wide),
+    )(projected, w_delta, bias, rates, signal_wide, cot_wide)
+    parts = exchange(payload, along_y)
+    copies = kernel(
+        row_kernel,
+        shape(shards // 4, slots, width, dtype=BF16),
+        4,
+        in_specs=[scalars, whole, whole],
+        out_specs=whole,
+    )(place, parts, flat)
+    row_totals = exchange(copies, along_z)
     entries = kernel(
-        shard_scan_kernel,
-        shape(shards, blocks, LANES),
+        entry_kernel,
+        shape(4, slots, width),
         4,
-        in_specs=[
-            pl.BlockSpec(memory_space=pltpu.SMEM),
-            pl.BlockSpec(memory_space=pltpu.VMEM),
-        ],
-        out_specs=pl.BlockSpec(memory_space=pltpu.VMEM),
-    )(place, parts)
-    entries = lax.all_to_all(entries, "seq", 0, 0, tiled=True)
+        in_specs=[scalars, whole, whole, whole],
+        out_specs=whole,
+    )(place, row_totals, parts, flat)
+    entries = exchange(entries, along_y)
     layer_out, grad_parts, direct = kernel(
         gradient_kernel,
         (
@@ -389,21 +470,21 @@
             shape(rows, columns, dtype=BF16),
             shape(rows, width),
         ),
-        24,
+        28,
         (
-            ((rows, LANES), F32),
             ((rows, width), F32),
             ((rows, width), F32),
             ((2, rows, width), F32),
             stack,
             stack,
-            ((rows, LANES), F32),
+            ((4, rows * depth, width), BF16),
+            wide,
         ),
     )(
         projected,
         w_delta,
         rates,
-        skip_gain.reshape(1, width),
+        gain,
         signal_wide,
         cot_wide,
         delta,

time: 131 us -> 100 us (0.76)
  Pallas kernels: 31.9 us -> 11 us
  blocking collectives: 54.2 us -> 67.7 us
  waiting for transfers between devices: 20.7 us -> 9.02 us
  starting transfers between devices: 19.1 us -> 7.61 us
    pallas_call x1, Pallas kernels: 23.3 us -> 5 us  [local(): kernel(gradient_kernel, (shape(rows, width, dtype=BF16), shape(rows, colu...]
    all_to_all x1, starting transfers between devices: 14.8 us -> 3.28 us  [exchange(): lax.all_to_all(array, 'seq', 0, 0, tiled=True, axis_index_groups=groups)]
    all_to_all x1 -> x2, blocking collectives: 19.9 us -> 30.8 us  [exchange(): lax.all_to_all(array, 'seq', 0, 0, tiled=True, axis_index_groups=groups)]
    all_to_all x1, waiting for transfers between devices: 15.3 us -> 4.36 us  [exchange(): lax.all_to_all(array, 'seq', 0, 0, tiled=True, axis_index_groups=groups)]
    pallas_call x1, Pallas kernels: 6.97 us -> 3.23 us  [local(): kernel(summary_kernel, (shape(2, rows, width), shape(2, rows, width), sha...]
    all_to_all x2, blocking collectives: 25.4 us -> 27.9 us  [sum_over_chan(): arrived = lax.all_to_all(pieces, 'chan', 0, 0, tiled=True)]
where the time goes in v3:
time: 100 us; the launch traced here: 99.4 us
  blocking collectives  67.7 us (68%)
  Pallas kernels  11 us (11%)
  waiting for transfers between devices  9.02 us (9%)
  starting transfers between devices  7.61 us (8%)
  local copies, waits for them, and re-layouts  3.22 us (3%)
    all_to_all x2, blocking collectives, exchange(): lax.all_to_all(array, 'seq', 0, 0, tiled=True, axis_index_groups=groups)  30.8 us
    all_to_all x2, blocking collectives, sum_over_chan(): arrived = lax.all_to_all(pieces, 'chan', 0, 0, tiled=True)  27.9 us
    all_to_all x1, blocking collectives, sum_over_chan(): lax.all_to_all(copies, 'chan', 0, 0, tiled=True).reshape(rows, columns)  8.98 us
    pallas_call x1, Pallas kernels, local(): kernel(gradient_kernel, (shape(rows, width, dtype=BF16), shape(rows, colu...  5 us
    all_to_all x1, waiting for transfers between devices, sum_over_chan(): lax.all_to_all(copies, 'chan', 0, 0, tiled=True).reshape(rows, columns)  4.66 us
    all_to_all x1, waiting for transfers between devices, exchange(): lax.all_to_all(array, 'seq', 0, 0, tiled=True, axis_index_groups=groups)  4.36 us
    all_to_all x1, starting transfers between devices, sum_over_chan(): lax.all_to_all(copies, 'chan', 0, 0, tiled=True).reshape(rows, columns)  4.32 us
    all_to_all x1, starting transfers between devices, exchange(): lax.all_to_all(array, 'seq', 0, 0, tiled=True, axis_index_groups=groups)  3.28 us
  transfers between devices with their start and end apart: 2, of which 2 were waited for; matrix products, arithmetic and copies ran while one was open for 0% of the time, Pallas kernels for 0%

profile of v3, /device:TPU:1, one launch (start us, length us, event | category | flops | bytes accessed | tf_op | source)
XLA Modules:
  0.0 99.4 jit_solution(5624896242570850499)
XLA Ops:
  0.6 0.0 copy-start
  0.6 0.9 copy-done
  1.6 0.8 copy-done.4
  2.4 0.3 project_kernel.1
  2.7 14.8 %all_to_all.35 = bf16[8,16,560]{2,1,0:T(8,128)(2,1)S(1)} all-to-all(bf16[8,16,560]{2,1,0:T(8,128)(2,1)S(1)} %bitcast.15), channel_id=1, replica_groups=mesh['seq'=64,'chan'=8] {'chan'}, dimensions={0} | all-to-all | bytes 286720 | tf_op jit(solution)/shard_map/all_to_all | solution.py:381
  17.6 0.7 broadcast_in_dim.4
  18.2 4.3 %all-to-all-start.1 = ((bf16[8,16,560]{2,1,0:T(8,128)(2,1)}), bf16[8,16,560]{2,1,0:T(8,128)(2,1)S(1)}, u32[]{:S(2)}, u32[]{:S(2)}) async-start(bf16[8,16,560]{2,1,0:T(8,128)(2,1)} %broadcast_in_dim.4), calls=%async_computation.1 | async-start | bytes 327680 | tf_op jit(solution)/shard_map/all_to_all | solution.py:384
  22.6 0.0 copy-done.3
  22.6 0.7 copy-done.5
  23.3 0.2 prepare_kernel.1
  23.5 4.7 %all-to-all-done.1 = bf16[8,16,560]{2,1,0:T(8,128)(2,1)S(1)} async-done(((bf16[8,16,560]{2,1,0:T(8,128)(2,1)}), bf16[8,16,560]{2,1,0:T(8,128)(2,1)S(1)}, u32[]{:S(2)}, u32[]{:S(2)}) %all-to-all-start.1) | async-done | bytes 143392 | tf_op jit(solution)/shard_map/all_to_all | solution.py:384
  28.1 3.2 %summary_kernel.1 = (f32[2,128,256]{2,1,0:T(8,128)S(1)}, f32[2,128,256]{2,1,0:T(8,128)S(1)}, f32[4,12,8,256]{3,2,1,0:T(8,128)S(1)}, f32[4,8,256]{2,1,0:T(8,128)S(1)}, f32[4,16,256]{2,1,0:T(8,128)}) custom-call(bf16[128,560]{1,0:T(8,128)(2,1)S(1)} %bitcast.9, bf16[2,256,256]{2,1,0:T(8,128)(2,1)S(1)} %copy-done.2, f32[2,256]{1,0:T(2,128)S(1)} %get-tuple-element.22.bias, ...), custom_call_target="tpu_custom_call" | custom-call | tf_op jit(solution)/shard_map/summary_kernel/pallas_call | solution.py:437
  31.4 3.3 %all-to-all-start.2 = ((f32[4,16,256]{2,1,0:T(8,128)}), f32[4,16,256]{2,1,0:T(8,128)S(1)}, u32[]{:S(2)}, u32[]{:S(2)}) async-start(f32[4,16,256]{2,1,0:T(8,128)} %get-tuple-element.27), calls=%async_computation.2 | async-start | bytes 131072 | tf_op jit(solution)/shard_map/all_to_all | solution.py:417
  34.7 0.1 pad_add_fusion.place
  34.7 4.4 %all-to-all-done.2.parts = f32[4,16,256]{2,1,0:T(8,128)S(1)} async-done(((f32[4,16,256]{2,1,0:T(8,128)}), f32[4,16,256]{2,1,0:T(8,128)S(1)}, u32[]{:S(2)}, u32[]{:S(2)}) %all-to-all-start.2) | async-done | bytes 65568 | tf_op jit(solution)/shard_map/all_to_all | solution.py:417
  39.1 0.6 row_kernel.1
  39.7 24.0 %all_to_all.36.rows = bf16[16,16,256]{2,1,0:T(8,128)(2,1)S(1)} all-to-all(bf16[16,16,256]{2,1,0:T(8,128)(2,1)S(1)} %row_kernel.1), channel_id=1, replica_groups={{0,32,64,96,128,160,192,224,256,288,320,352,384,416,448,480},{8,40,72,1..., dimensions={0} | all-to-all | bytes 262144 | tf_op jit(solution)/shard_map/all_to_all | solution.py:417
  63.7 0.7 entry_kernel.1
  64.3 6.8 %all_to_all.37.entries = f32[4,16,256]{2,1,0:T(8,128)S(1)} all-to-all(f32[4,16,256]{2,1,0:T(8,128)S(1)} %entry_kernel.1), channel_id=1, replica_groups={{0,8,16,24},{32,40,48,56},{64,72,80,88},{96,104,112,120},{128,136,144,1..., dimensions={0} | all-to-all | bytes 131072 | tf_op jit(solution)/shard_map/all_to_all | solution.py:417
  71.2 5.0 %gradient_kernel.1 = (bf16[128,256]{1,0:T(8,128)(2,1)}, bf16[128,560]{1,0:T(8,128)(2,1)S(1)}, f32[128,256]{1,0:T(8,128)S(1)}) custom-call(bf16[128,560]{1,0:T(8,128)(2,1)S(1)} %bitcast.10, bf16[2,256,256]{2,1,0:T(8,128)(2,1)S(1)} %copy-done.2, f32[2,12,8,256]{3,2,1,0:T(8,128)S(1)} %get-tuple-element.18.rates, f32[1,256]{1,0:T(1,128)S(1)} %get-tuple-element.19.skip_gain, ...), custom_call_target="tpu_custom_call" | custom-call | tf_op jit(solution)/shard_map/gradient_kernel/pallas_call | solution.py:466
  76.2 13.2 %all_to_all.38 = bf16[8,16,560]{2,1,0:T(8,128)(2,1)S(1)} all-to-all(bf16[8,16,560]{2,1,0:T(8,128)(2,1)S(1)} %bitcast.14), channel_id=1, replica_groups=mesh['seq'=64,'chan'=8] {'chan'}, dimensions={0} | all-to-all | bytes 286720 | tf_op jit(solution)/shard_map/all_to_all | solution.py:381
  89.4 0.0 copy-start.1
  89.4 9.0 %all_to_all.39 = bf16[8,16,560]{2,1,0:T(8,128)(2,1)S(1)} all-to-all(bf16[8,16,560]{2,1,0:T(8,128)(2,1)S(1)} %broadcast_in_dim.5), channel_id=1, replica_groups=mesh['seq'=64,'chan'=8] {'chan'}, dimensions={0} | all-to-all | bytes 286720 | tf_op jit(solution)/shard_map/all_to_all | solution.py:384
  98.4 1.0 %finish_kernel.1 = bf16[128,256]{1,0:T(8,128)(2,1)} custom-call(bf16[128,560]{1,0:T(8,128)(2,1)S(1)} %bitcast.13, bf16[560,256]{1,0:T(8,128)(2,1)S(1)} %bitcast.12, f32[128,256]{1,0:T(8,128)S(1)} %get-tuple-element.31.direct), custom_call_target="tpu_custom_call" | custom-call | tf_op jit(solution)/shard_map/finish_kernel/pallas_call | solution.py:497
  (13 shorter events, 0.1 us)
Async XLA Ops:
  0.6 1.0 copy-start
  1.6 0.8 copy-start.4
  18.2 4.3 %copy-start.3 = (bf16[128,256]{1,0:T(8,128)(2,1)S(1)}, bf16[128,256]{1,0:T(8,128)(2,1)}, u32[]{:S(2)}) copy-start(bf16[128,256]{1,0:T(8,128)(2,1)} %cotangent.1) | copy-start | bytes 196612
  18.2 9.9 %copy-start.2 = (bf16[2,256,256]{2,1,0:T(8,128)(2,1)S(1)}, bf16[2,256,256]{2,1,0:T(8,128)(2,1)}, u32[]{:S(2)}) copy-start(bf16[2,256,256]{2,1,0:T(8,128)(2,1)} %w_delta.3) | copy-start | bytes 786436
  18.2 9.9 %all-to-all-start.1 = ((bf16[8,16,560]{2,1,0:T(8,128)(2,1)}), bf16[8,16,560]{2,1,0:T(8,128)(2,1)S(1)}, u32[]{:S(2)}, u32[]{:S(2)}) async-start(bf16[8,16,560]{2,1,0:T(8,128)(2,1)} %broadcast_in_dim.4), calls=%async_computation.1 | async-start | bytes 327680 | tf_op jit(solution)/shard_map/all_to_all | solution.py:384
  22.6 0.7 copy-start.5
  22.6 0.7 copy-start.6
  22.6 0.7 copy-start.7
  31.4 7.7 %all-to-all-start.2 = ((f32[4,16,256]{2,1,0:T(8,128)}), f32[4,16,256]{2,1,0:T(8,128)S(1)}, u32[]{:S(2)}, u32[]{:S(2)}) async-start(f32[4,16,256]{2,1,0:T(8,128)} %get-tuple-element.27), calls=%async_computation.2 | async-start | bytes 131072 | tf_op jit(solution)/shard_map/all_to_all | solution.py:417
  89.4 9.0 %copy-start.1 = (bf16[256,560]{0,1:T(8,128)(2,1)S(1)}, bf16[256,560]{0,1:T(8,128)(2,1)}, u32[]{:S(2)}) copy-start(bf16[256,560]{0,1:T(8,128)(2,1)} %param.9) | copy-start | bytes 860164

commit v4 on v3

--- a/solution.py
+++ b/solution.py
@@ -28,10 +28,34 @@
     return jnp.where(token == (row % GROUPS) * steps + row // GROUPS, 1.0, 0.0).astype(BF16)
 
 
-def project_kernel(signal, w_proj, signal_out, part_out):
-    grouped = dot(grouping(signal.shape[0]), signal[...])
+def project_kernel(signal, w_proj, signal_out, part_out, signal_here, w_here, done):
+    fetches = [
+        pltpu.make_async_copy(signal, signal_here, done.at[0]),
+        pltpu.make_async_copy(w_proj, w_here, done.at[1]),
+    ]
+    for fetch in fetches:
+        fetch.start()
+    order = grouping(signal_here.shape[0])
+    fetches[0].wait()
+    grouped = dot(order, signal_here[...])
     signal_out[...] = grouped
-    part_out[...] = dot(grouped.astype(BF16), w_proj[...], NT).astype(BF16)
+    fetches[1].wait()
+    part_out[...] = dot(grouped.astype(BF16), w_here[...], NT)
+
+
+def pair_kernel(place, both, copies):
+    half = both.shape[0] // 4
+    start = pl.multiple_of(place[2] * half, half)
+    total = both[pl.ds(start, half), :] + both[pl.ds(2 * half + start, half), :]
+    for copy in range(copies.shape[0]):
+        copies[copy] = total.astype(BF16)
+
+
+def chips_kernel(parts, total):
+    result = parts[0].astype(F32)
+    for chip in range(1, parts.shape[0]):
+        result = result + parts[chip].astype(F32)
+    total[...] = result.astype(BF16)
 
 
 def prepare_kernel(cotangent, decay_log, bias, skip_gain, cot_out, rates, flat, bias_out, gain_out):
@@ -344,7 +368,7 @@
     for way in range(2):
         parts_out[:, way * rank : (way + 1) * rank] = dot(
             grad_pre[way].astype(BF16), w_delta[way], NT
-        ).astype(BF16)
+        )
     ones = jnp.ones((width, LANES), BF16)
     lane = lax.broadcasted_iota(jnp.int32, (GROUPS, LANES), 1)
     height = depth * GROUPS
@@ -358,7 +382,7 @@
                     merged[step] = jnp.where(
                         lane == which * depth + n, sums[row : row + GROUPS], merged[step]
                     )
-        stacked = jnp.concatenate(merged, 0)[:, : 4 * depth].astype(BF16)
+        stacked = jnp.concatenate(merged, 0)[:, : 4 * depth]
         parts_out[start * GROUPS : (start + 4) * GROUPS, 2 * rank :] = stacked
     ungroup = grouping(rows, inverse=True)
     layer_out[...] = dot(ungroup, core[...].astype(BF16)).astype(BF16)
@@ -374,26 +398,40 @@
     return jax.ShapeDtypeStruct(dims, dtype)
 
 
-def sum_over_chan(part):
-    count = lax.axis_size("chan")
-    rows, columns = part.shape
-    pieces = part.reshape(count, rows // count, columns)
-    arrived = lax.all_to_all(pieces, "chan", 0, 0, tiled=True)
-    total = jnp.sum(arrived.astype(F32), 0).astype(BF16)
-    copies = jnp.broadcast_to(total[None], (count,) + total.shape)
-    return lax.all_to_all(copies, "chan", 0, 0, tiled=True).reshape(rows, columns)
+WHOLE = pl.BlockSpec(memory_space=pltpu.VMEM)
+SCALARS = pl.BlockSpec(memory_space=pltpu.SMEM)
 
 
 def kernel(body, out_shape, mebibytes, scratch=(), cost=0, **more):
     return pl.pallas_call(
         body,
         out_shape=out_shape,
-        scratch_shapes=[pltpu.VMEM(dims, dtype) for dims, dtype in scratch],
+        scratch_shapes=[
+            pltpu.VMEM(*each) if isinstance(each, tuple) else each for each in scratch
+        ],
         compiler_params=pltpu.CompilerParams(vmem_limit_bytes=mebibytes << 20),
         cost_estimate=pl.CostEstimate(flops=cost, bytes_accessed=cost, transcendentals=0),
         name=body.__name__,
         **more,
     )
+
+
+def sum_over_chan(part, place):
+    count = lax.axis_size("chan")
+    rows, columns = part.shape
+    pairs = [[2 * chip, 2 * chip + 1] for chip in range(count // 2)]
+    across = [list(range(core, count, 2)) for core in range(2)]
+    both = lax.all_gather(part, "chan", axis=0, tiled=True, axis_index_groups=pairs)
+    copies = kernel(
+        pair_kernel,
+        shape(count // 2, rows // 2, columns, dtype=BF16),
+        4,
+        in_specs=[SCALARS, WHOLE],
+        out_specs=WHOLE,
+    )(place, both)
+    parts = lax.all_to_all(copies, "chan", 0, 0, tiled=True, axis_index_groups=across)
+    half = kernel(chips_kernel, shape(rows // 2, columns, dtype=BF16), 4)(parts)
+    return lax.all_gather(half, "chan", axis=0, tiled=True, axis_index_groups=pairs)
 
 
 def local(signal, cotangent, w_proj, w_delta, delta_bias, decay_log, skip_gain):
@@ -406,19 +444,23 @@
         raise ValueError("shard count")
     w_turned = w_proj.T
     shard = lax.axis_index("seq").astype(jnp.int32)
-    place = jnp.stack([shard // 4, shard % 4])
+    core = lax.axis_index("chan").astype(jnp.int32) % 2
+    place = jnp.stack([shard // 4, shard % 4, core])
     along_y = [[z * 4 + y for y in range(4)] for z in range(shards // 4)]
     along_z = [[z * 4 + y for z in range(shards // 4)] for y in range(4)]
     slots = depth + 4
-    whole = pl.BlockSpec(memory_space=pltpu.VMEM)
-    scalars = pl.BlockSpec(memory_space=pltpu.SMEM)
 
     def exchange(array, groups):
         return lax.all_to_all(array, "seq", 0, 0, tiled=True, axis_index_groups=groups)
 
     signal_wide, part = kernel(
-        project_kernel, (shape(rows, width), shape(rows, columns, dtype=BF16)), 8
-    )(signal, w_turned)
+        project_kernel,
+        (shape(rows, width), shape(rows, columns)),
+        8,
+        (((rows, width), BF16), ((columns, width), BF16), pltpu.SemaphoreType.DMA((2,))),
+        in_specs=[pl.BlockSpec(memory_space=pltpu.HBM)] * 2,
+        out_specs=(WHOLE, WHOLE),
+    )(*(pltpu.with_memory_space_constraint(each, pltpu.HBM) for each in (signal, w_turned)))
     cot_wide, rates, flat, bias, gain = kernel(
         prepare_kernel,
         (
@@ -431,7 +473,7 @@
         8,
         cost=1 << 20,
     )(cotangent, decay_log.transpose(1, 0, 2), delta_bias, skip_gain.reshape(1, width))
-    projected = sum_over_chan(part)
+    projected = sum_over_chan(part, place)
     wide = ((rows, 4 * depth * LANES), F32)
     stack = ((steps, depth, GROUPS, width), F32)
     delta, slope, local_states, ahead, payload = kernel(
@@ -451,23 +493,23 @@
         row_kernel,
         shape(shards // 4, slots, width, dtype=BF16),
         4,
-        in_specs=[scalars, whole, whole],
-        out_specs=whole,
+        in_specs=[SCALARS, WHOLE, WHOLE],
+        out_specs=WHOLE,
     )(place, parts, flat)
     row_totals = exchange(copies, along_z)
     entries = kernel(
         entry_kernel,
         shape(4, slots, width),
         4,
-        in_specs=[scalars, whole, whole, whole],
-        out_specs=whole,
+        in_specs=[SCALARS, WHOLE, WHOLE, WHOLE],
+        out_specs=WHOLE,
     )(place, row_totals, parts, flat)
     entries = exchange(entries, along_y)
     layer_out, grad_parts, direct = kernel(
         gradient_kernel,
         (
             shape(rows, width, dtype=BF16),
-            shape(rows, columns, dtype=BF16),
+            shape(rows, columns),
             shape(rows, width),
         ),
         28,
@@ -493,7 +535,7 @@
         ahead,
         entries,
     )
-    grad_proj = sum_over_chan(grad_parts)
+    grad_proj = sum_over_chan(grad_parts, place)
     signal_grad = kernel(finish_kernel, shape(rows, width, dtype=BF16), 8)(
         grad_proj, w_turned, direct
     )

time: 100 us -> 93.1 us (0.931)
  starting transfers between devices: 7.61 us -> 3.58 us
  waiting for transfers between devices: 9.02 us -> 6.19 us
  local copies, waits for them, and re-layouts: 3.22 us -> 0.68 us
  Pallas kernels: 11 us -> 13.3 us
    all_to_all x3 -> x1, blocking collectives: 36.9 us -> 9.18 us  [sum_over_chan(): lax.all_to_all(copies, 'chan', 0, 0, tiled=True, axis_index_groups=across)]
    all_gather x0 -> x4, blocking collectives: none -> 21.7 us  [the longest x2 15.7 us: sum_over_chan(): lax.all_gather(part, 'chan', axis=0, tiled=True, axis_index_groups=pairs)]
    all_to_all x2 -> x3, blocking collectives: 30.8 us -> 37.2 us  [exchange(): lax.all_to_all(array, 'seq', 0, 0, tiled=True, axis_index_groups=groups)]
    all_to_all x2 -> x1, starting transfers between devices: 7.61 us -> 3.58 us  [sum_over_chan(): lax.all_to_all(copies, 'chan', 0, 0, tiled=True, axis_index_groups=across)]
    pallas_call x2 -> x6, Pallas kernels: 0.98 us -> 3.91 us  [the longest x2 1.87 us: sum_over_chan(): kernel(pair_kernel, shape(count // 2, rows // 2, columns, dtype=BF16), 4,...]
    all_to_all x2 -> x1, waiting for transfers between devices: 9.02 us -> 6.19 us  [sum_over_chan(): lax.all_to_all(copies, 'chan', 0, 0, tiled=True, axis_index_groups=across)]
    unnamed x16 -> x12, local copies, waits for them, and re-layouts: 2.53 us -> 0.68 us
  transfers between devices with their start and end apart: 2 -> 1, of which waited for: 2 -> 1; matrix products, arithmetic and copies ran while one was open for 0% -> 0% of each run, Pallas kernels for 0% -> 0%
where the time goes in v4:
time: 93.1 us; the launch traced here: 92.7 us
  blocking collectives  68.1 us (73%)
  Pallas kernels  13.3 us (14%)
  waiting for transfers between devices  6.19 us (7%)
  starting transfers between devices  3.58 us (4%)
    all_to_all x3, blocking collectives, exchange(): lax.all_to_all(array, 'seq', 0, 0, tiled=True, axis_index_groups=groups)  37.2 us
    all_gather x2, blocking collectives, sum_over_chan(): lax.all_gather(part, 'chan', axis=0, tiled=True, axis_index_groups=pairs)  15.7 us
    all_to_all x1, blocking collectives, sum_over_chan(): lax.all_to_all(copies, 'chan', 0, 0, tiled=True, axis_index_groups=across)  9.18 us
    all_to_all x1, waiting for transfers between devices, sum_over_chan(): lax.all_to_all(copies, 'chan', 0, 0, tiled=True, axis_index_groups=across)  6.19 us
    all_gather x2, blocking collectives, sum_over_chan(): lax.all_gather(half, 'chan', axis=0, tiled=True, axis_index_groups=pairs)  6.01 us
    pallas_call x1, Pallas kernels, local(): kernel(gradient_kernel, (shape(rows, width, dtype=BF16), shape(rows, colu...  5.01 us
    all_to_all x1, starting transfers between devices, sum_over_chan(): lax.all_to_all(copies, 'chan', 0, 0, tiled=True, axis_index_groups=across)  3.58 us
    pallas_call x1, Pallas kernels, local(): kernel(summary_kernel, (shape(2, rows, width), shape(2, rows, width), sha...  2.6 us
  transfers between devices with their start and end apart: 1, of which 1 were waited for; matrix products, arithmetic and copies ran while one was open for 0% of the time, Pallas kernels for 0%

profile of v4, /device:TPU:1, one launch (start us, length us, event | category | flops | bytes accessed | tf_op | source)
XLA Modules:
  0.0 92.7 jit_solution(16474498561730078604)
XLA Ops:
  0.7 1.3 %project_kernel.1 = (f32[128,256]{1,0:T(8,128)S(1)}, f32[128,560]{1,0:T(8,128)S(1)}) custom-call(bf16[128,256]{1,0:T(8,128)(2,1)} %signal.1, bf16[560,256]{1,0:T(8,128)(2,1)} %bitcast.6), custom_call_target="tpu_custom_call" | custom-call | tf_op jit(solution)/shard_map/project_kernel/pallas_call | solution.py:456
  1.9 8.7 %all_gather.12.both = f32[256,560]{1,0:T(8,128)S(1)} all-gather(f32[128,560]{1,0:T(8,128)S(1)} %get-tuple-element.17), channel_id=1, replica_groups={{0,1},{2,3},{4,5},{6,7},{8,9},{10,11},{12,13},{14,15},{16,17},{18,19},{..., dimensions={0}, use_global_device_ids=true | all-gather | bytes 860160 | tf_op jit(solution)/shard_map/all_gather | solution.py:424
  10.7 0.1 pad_add_fusion.place
  10.8 1.3 %pair_kernel.2 = bf16[4,64,560]{2,1,0:T(8,128)(2,1)} custom-call(s32[3]{0:T(128)S(1)} %pad_add_fusion.place, f32[256,560]{1,0:T(8,128)S(1)} %all_gather.12.both), custom_call_target="tpu_custom_call" | custom-call | tf_op jit(solution)/shard_map/pair_kernel/pallas_call | solution.py:425
  12.1 3.6 %all-to-all-start = ((bf16[4,64,560]{2,1,0:T(8,128)(2,1)}), bf16[4,64,560]{2,1,0:T(8,128)(2,1)S(1)}, u32[]{:S(2)}, u32[]{:S(2)}) async-start(bf16[4,64,560]{2,1,0:T(8,128)(2,1)} %pair_kernel.2), calls=%async_computation | async-start | bytes 655360 | tf_op jit(solution)/shard_map/all_to_all | solution.py:432
  15.6 0.0 copy-start.4
  15.7 0.0 copy-start.5
  15.7 0.6 copy-done.4
  16.3 0.0 copy-done.5
  16.3 0.2 prepare_kernel.1
  16.5 6.2 %all-to-all-done.parts = bf16[4,64,560]{2,1,0:T(8,128)(2,1)S(1)} async-done(((bf16[4,64,560]{2,1,0:T(8,128)(2,1)}), bf16[4,64,560]{2,1,0:T(8,128)(2,1)S(1)}, u32[]{:S(2)}, u32[]{:S(2)}) %all-to-all-start) | async-done | bytes 286752 | tf_op jit(solution)/shard_map/all_to_all | solution.py:432
  22.8 2.8 %all_gather.13.projected = bf16[128,560]{1,0:T(8,128)(2,1)S(1)} all-gather(bf16[64,560]{1,0:T(8,128)(2,1)S(1)} %chips_kernel.2), channel_id=1, replica_groups={{0,1},{2,3},{4,5},{6,7},{8,9},{10,11},{12,13},{14,15},{16,17},{18,19},{..., dimensions={0}, use_global_device_ids=true | all-gather | bytes 215040 | tf_op jit(solution)/shard_map/all_gather | solution.py:434
  25.6 2.6 %summary_kernel.1 = (f32[2,128,256]{2,1,0:T(8,128)S(1)}, f32[2,128,256]{2,1,0:T(8,128)S(1)}, f32[4,12,8,256]{3,2,1,0:T(8,128)S(1)}, f32[4,8,256]{2,1,0:T(8,128)S(1)}, f32[4,16,256]{2,1,0:T(8,128)S(1)}) custom-call(bf16[128,560]{1,0:T(8,128)(2,1)S(1)} %all_gather.13.projected, bf16[2,256,256]{2,1,0:T(8,128)(2,1)S(1)} %copy-done.1, ...), custom_call_target="tpu_custom_call" | custom-call | tf_op jit(solution)/shard_map/summary_kernel/pallas_call | solution.py:479
  28.2 6.8 %all_to_all.25.parts = f32[4,16,256]{2,1,0:T(8,128)S(1)} all-to-all(f32[4,16,256]{2,1,0:T(8,128)S(1)} %get-tuple-element.27), channel_id=1, replica_groups={{0,8,16,24},{32,40,48,56},{64,72,80,88},{96,104,112,120},{128,136,144,1..., dimensions={0} | all-to-all | bytes 131072 | tf_op jit(solution)/shard_map/all_to_all | solution.py:454
  35.0 0.6 row_kernel.1
  35.6 23.5 %all_to_all.26.rows = bf16[16,16,256]{2,1,0:T(8,128)(2,1)S(1)} all-to-all(bf16[16,16,256]{2,1,0:T(8,128)(2,1)S(1)} %row_kernel.1), channel_id=1, replica_groups={{0,32,64,96,128,160,192,224,256,288,320,352,384,416,448,480},{8,40,72,1..., dimensions={0} | all-to-all | bytes 262144 | tf_op jit(solution)/shard_map/all_to_all | solution.py:454
  59.1 0.7 entry_kernel.1
  59.8 6.8 %all_to_all.27.entries = f32[4,16,256]{2,1,0:T(8,128)S(1)} all-to-all(f32[4,16,256]{2,1,0:T(8,128)S(1)} %entry_kernel.1), channel_id=1, replica_groups={{0,8,16,24},{32,40,48,56},{64,72,80,88},{96,104,112,120},{128,136,144,1..., dimensions={0} | all-to-all | bytes 131072 | tf_op jit(solution)/shard_map/all_to_all | solution.py:454
  66.7 5.0 %gradient_kernel.1 = (bf16[128,256]{1,0:T(8,128)(2,1)}, f32[128,560]{1,0:T(8,128)S(1)}, f32[128,256]{1,0:T(8,128)S(1)}) custom-call(bf16[128,560]{1,0:T(8,128)(2,1)S(1)} %all_gather.13.projected, bf16[2,256,256]{2,1,0:T(8,128)(2,1)S(1)} %copy-done.1, f32[2,12,8,256]{3,2,1,0:T(8,128)S(1)} %get-tuple-element.18.rates, ...), custom_call_target="tpu_custom_call" | custom-call | tf_op jit(solution)/shard_map/gradient_kernel/pallas_call | solution.py:508
  71.7 7.0 %all_gather.14.both = f32[256,560]{1,0:T(8,128)S(1)} all-gather(f32[128,560]{1,0:T(8,128)S(1)} %get-tuple-element.30), channel_id=1, replica_groups={{0,1},{2,3},{4,5},{6,7},{8,9},{10,11},{12,13},{14,15},{16,17},{18,19},{..., dimensions={0}, use_global_device_ids=true | all-gather | bytes 860160 | tf_op jit(solution)/shard_map/all_gather | solution.py:424
  78.7 0.6 pair_kernel.3
  79.2 9.2 %all_to_all.28.parts = bf16[4,64,560]{2,1,0:T(8,128)(2,1)S(1)} all-to-all(bf16[4,64,560]{2,1,0:T(8,128)(2,1)S(1)} %pair_kernel.3), channel_id=1, replica_groups={{0,2,4,6},{1,3,5,7},{8,10,12,14},{9,11,13,15},{16,18,20,22},{17,19,21,2..., dimensions={0} | all-to-all | bytes 573440 | tf_op jit(solution)/shard_map/all_to_all | solution.py:432
  88.5 3.2 %all_gather.15.grad_proj = bf16[128,560]{1,0:T(8,128)(2,1)S(1)} all-gather(bf16[64,560]{1,0:T(8,128)(2,1)S(1)} %chips_kernel.3), channel_id=1, replica_groups={{0,1},{2,3},{4,5},{6,7},{8,9},{10,11},{12,13},{14,15},{16,17},{18,19},{..., dimensions={0}, use_global_device_ids=true | all-gather | bytes 215040 | tf_op jit(solution)/shard_map/all_gather | solution.py:434
  91.7 1.0 %finish_kernel.1 = bf16[128,256]{1,0:T(8,128)(2,1)} custom-call(bf16[128,560]{1,0:T(8,128)(2,1)S(1)} %all_gather.15.grad_proj, bf16[560,256]{1,0:T(8,128)(2,1)S(1)} %bitcast.7, f32[128,256]{1,0:T(8,128)S(1)} %get-tuple-element.31.direct), custom_call_target="tpu_custom_call" | custom-call | tf_op jit(solution)/shard_map/finish_kernel/pallas_call | solution.py:539
  (10 shorter events, 0.1 us)
Async XLA Ops:
  12.1 3.6 %copy-start.2 = (bf16[128,256]{1,0:T(8,128)(2,1)S(1)}, bf16[128,256]{1,0:T(8,128)(2,1)}, u32[]{:S(2)}) copy-start(bf16[128,256]{1,0:T(8,128)(2,1)} %cotangent.1) | copy-start | bytes 196612
  12.1 3.6 %copy-start.3 = (f32[2,12,256]{2,0,1:T(2,128)S(1)}, f32[2,12,256]{2,0,1:T(2,128)}, u32[]{:S(2)}) copy-start(f32[2,12,256]{2,0,1:T(2,128)} %param.12) | copy-start | bytes 73732
  12.1 10.7 %all-to-all-start = ((bf16[4,64,560]{2,1,0:T(8,128)(2,1)}), bf16[4,64,560]{2,1,0:T(8,128)(2,1)S(1)}, u32[]{:S(2)}, u32[]{:S(2)}) async-start(bf16[4,64,560]{2,1,0:T(8,128)(2,1)} %pair_kernel.2), calls=%async_computation | async-start | bytes 655360 | tf_op jit(solution)/shard_map/all_to_all | solution.py:432
  15.6 0.7 copy-start.4
  15.7 0.7 copy-start.5
  16.5 9.0 %copy-start.1 = (bf16[2,256,256]{2,1,0:T(8,128)(2,1)S(1)}, bf16[2,256,256]{2,1,0:T(8,128)(2,1)}, u32[]{:S(2)}) copy-start(bf16[2,256,256]{2,1,0:T(8,128)(2,1)} %w_delta.3) | copy-start | bytes 786436
  88.4 3.3 %copy-start = (bf16[256,560]{0,1:T(8,128)(2,1)S(1)}, bf16[256,560]{0,1:T(8,128)(2,1)}, u32[]{:S(2)}) copy-start(bf16[256,560]{0,1:T(8,128)(2,1)} %param.9) | copy-start | bytes 860164

commit v5 on v4

--- a/solution.py
+++ b/solution.py
@@ -43,9 +43,9 @@
     part_out[...] = dot(grouped.astype(BF16), w_here[...], NT)
 
 
-def pair_kernel(place, both, copies):
+def pair_kernel(both, copies):
     half = both.shape[0] // 4
-    start = pl.multiple_of(place[2] * half, half)
+    start = pl.multiple_of(lax.axis_index("chan") % 2 * half, half)
     total = both[pl.ds(start, half), :] + both[pl.ds(2 * half + start, half), :]
     for copy in range(copies.shape[0]):
         copies[copy] = total.astype(BF16)
@@ -90,6 +90,13 @@
 
 def gate_at(spread, step, column):
     return spread[at(step), column * LANES : (column + 1) * LANES]
+
+
+def put_total(shares, kind, lanes, total):
+    depth = shares.shape[1] - 4
+    coarse = total.astype(BF16).astype(F32)
+    shares[kind, depth : depth + 1, lanes] = coarse
+    shares[kind, depth + 1 : depth + 2, lanes] = total - coarse
 
 
 def summary_kernel(
@@ -107,6 +114,7 @@
     weight,
     fades,
     spread,
+    shares,
 ):
     rows, width = signal.shape
     rank = w_delta.shape[1]
@@ -114,7 +122,7 @@
     steps = rows // GROUPS
     blocks = width // LANES
     spread_gates(projected[:, 2 * rank :], spread)
-    payload[...] = jnp.zeros_like(payload)
+    shares[...] = jnp.zeros_like(shares)
     group = lax.broadcasted_iota(jnp.int32, (GROUPS, LANES), 0)
     for way in range(2):
         pre = dot(projected[:, way * rank : (way + 1) * rank], w_delta[way]) + bias[way : way + 1]
@@ -183,74 +191,74 @@
                     local_out[2 * way + kind, n, :, lanes] = jnp.where(
                         beyond(1, down), 0.0, shift(scanned, 1, down)
                     )
-                    payload[2 * way + kind, n : n + 1, lanes] = scanned[edge : edge + 1]
-                payload[2 * way + kind, depth : depth + 1, lanes] = whole
-
-
-def fall_or_rise(kind, run):
-    falling = jnp.logical_or(kind == 1, kind == 2)
-
-    @pl.when(falling)
-    def _():
-        run(True)
-
-    @pl.when(jnp.logical_not(falling))
-    def _():
-        run(False)
+                    shares[2 * way + kind, n : n + 1, lanes] = scanned[edge : edge + 1]
+                put_total(shares, 2 * way + kind, lanes, whole)
+    payload[0] = shares[...].astype(BF16)
+    for copy in range(1, payload.shape[0]):
+        payload[copy] = payload[0]
+
+
+RISING = (0, 3)
+FALLING = (1, 2)
 
 
 def order(count, falling):
     return range(count - 1, -1, -1) if falling else range(count)
 
 
-def shard_fade(parts, flat, way, shard):
-    depth = parts.shape[1] - 4
-    return jnp.exp2(flat[way] * parts[shard, depth : depth + 1])
-
-
-def row_kernel(place, parts, flat, copies):
-    shards, slots, width = parts.shape
+def pass_by(state, block, rates):
+    depth = block.shape[0] - 4
+    total = block[depth : depth + 1] + block[depth + 1 : depth + 2]
+    return jnp.exp2(rates * total) * state + block
+
+
+def row_kernel(parts, flat, copies):
+    shards, _, slots, width = parts.shape
     depth = slots - 4
-    kind = place[1]
+    here = lax.axis_index("seq") // shards
     slot = lax.broadcasted_iota(jnp.int32, (slots, width), 0)
-
-    def run(falling):
+    packed = []
+    for kind in range(4):
         state = jnp.zeros((slots, width), F32)
-        for shard in order(shards, falling):
-            state = shard_fade(parts, flat, kind // 2, shard) * state + parts[shard]
-        total = parts[0, depth : depth + 1]
-        for shard in range(1, shards):
-            total = total + parts[shard, depth : depth + 1]
+        total = jnp.zeros((1, width), F32)
+        for shard in order(shards, kind in FALLING):
+            block = parts[shard, kind].astype(F32)
+            total = total + block[depth : depth + 1] + block[depth + 1 : depth + 2]
+            state = pass_by(state, block, flat[kind // 2])
         coarse = total.astype(BF16).astype(F32)
-        packed = jnp.where(slot == depth, coarse, state)
-        packed = jnp.where(slot == depth + 1, total - coarse, packed).astype(BF16)
-        for copy in range(copies.shape[0]):
-            copies[copy] = packed
-
-    fall_or_rise(kind, run)
-
-
-def entry_kernel(place, rows, parts, flat, entries):
-    count, slots, width = rows.shape
+        state = jnp.where(slot == depth, coarse, state)
+        state = jnp.where(slot == depth + 1, total - coarse, state)
+        packed.append(jnp.where(slot > depth + 1, 0.0, state).astype(BF16))
+    for row in range(copies.shape[0]):
+
+        @pl.when(row > here)
+        def _():
+            for place, kind in enumerate(RISING):
+                copies[row, place] = packed[kind]
+
+        @pl.when(row <= here)
+        def _():
+            for place, kind in enumerate(FALLING):
+                copies[row, place] = packed[kind]
+
+
+def entry_kernel(rows, parts, flat, entries):
+    count, _, slots, width = rows.shape
     shards = parts.shape[0]
-    depth = slots - 4
-    here = place[0]
-    kind = place[1]
-    rates = flat[kind // 2]
-
-    def run(falling):
-        state = jnp.zeros((slots, width), F32)
-        for row in order(count, falling):
-            block = rows[row].astype(F32)
-            total = block[depth : depth + 1] + block[depth + 1 : depth + 2]
-            passed = jnp.exp2(rates * total) * state + block
-            before = row > here if falling else row < here
-            state = jnp.where(before, passed, state)
-        for shard in order(shards, falling):
-            entries[shard] = state
-            state = shard_fade(parts, flat, kind // 2, shard) * state + parts[shard]
-
-    fall_or_rise(kind, run)
+    place = lax.axis_index("seq")
+    row_here = place // shards
+    here = place % shards
+    for falling, kinds in ((False, RISING), (True, FALLING)):
+        for slot, kind in enumerate(kinds):
+            rates = flat[kind // 2]
+            state = jnp.zeros((slots, width), F32)
+            for row in order(count, falling):
+                passed = pass_by(state, rows[row, slot].astype(F32), rates)
+                state = jnp.where(row > row_here if falling else row < row_here, passed, state)
+            for shard in order(shards, falling):
+                passed = pass_by(state, parts[shard, kind].astype(F32), rates)
+                state = jnp.where(shard > here if falling else shard < here, passed, state)
+            entries[kind] = state
 
 
 def gradient_kernel(
@@ -399,7 +407,6 @@
 
 
 WHOLE = pl.BlockSpec(memory_space=pltpu.VMEM)
-SCALARS = pl.BlockSpec(memory_space=pltpu.SMEM)
 
 
 def kernel(body, out_shape, mebibytes, scratch=(), cost=0, **more):
@@ -416,7 +423,7 @@
     )
 
 
-def sum_over_chan(part, place):
+def sum_over_chan(part):
     count = lax.axis_size("chan")
     rows, columns = part.shape
     pairs = [[2 * chip, 2 * chip + 1] for chip in range(count // 2)]
@@ -426,9 +433,7 @@
         pair_kernel,
         shape(count // 2, rows // 2, columns, dtype=BF16),
         4,
-        in_specs=[SCALARS, WHOLE],
-        out_specs=WHOLE,
-    )(place, both)
+    )(both)
     parts = lax.all_to_all(copies, "chan", 0, 0, tiled=True, axis_index_groups=across)
     half = kernel(chips_kernel, shape(rows // 2, columns, dtype=BF16), 4)(parts)
     return lax.all_gather(half, "chan", axis=0, tiled=True, axis_index_groups=pairs)
@@ -443,9 +448,6 @@
     if shards % 4:
         raise ValueError("shard count")
     w_turned = w_proj.T
-    shard = lax.axis_index("seq").astype(jnp.int32)
-    core = lax.axis_index("chan").astype(jnp.int32) % 2
-    place = jnp.stack([shard // 4, shard % 4, core])
     along_y = [[z * 4 + y for y in range(4)] for z in range(shards // 4)]
     along_z = [[z * 4 + y for z in range(shards // 4)] for y in range(4)]
     slots = depth + 4
@@ -473,7 +475,7 @@
         8,
         cost=1 << 20,
     )(cotangent, decay_log.transpose(1, 0, 2), delta_bias, skip_gain.reshape(1, width))
-    projected = sum_over_chan(part, place)
+    projected = sum_over_chan(part)
     wide = ((rows, 4 * depth * LANES), F32)
     stack = ((steps, depth, GROUPS, width), F32)
     delta, slope, local_states, ahead, payload = kernel(
@@ -483,28 +485,15 @@
             shape(2, rows, width),
             shape(4, depth, GROUPS, width),
             shape(4, GROUPS, width),
-            shape(4, slots, width),
+            shape(4, 4, slots, width, dtype=BF16),
         ),
         20,
-        (((rows, width), F32), stack, wide),
+        (((rows, width), F32), stack, wide, ((4, slots, width), F32)),
     )(projected, w_delta, bias, rates, signal_wide, cot_wide)
     parts = exchange(payload, along_y)
-    copies = kernel(
-        row_kernel,
-        shape(shards // 4, slots, width, dtype=BF16),
-        4,
-        in_specs=[SCALARS, WHOLE, WHOLE],
-        out_specs=WHOLE,
-    )(place, parts, flat)
+    copies = kernel(row_kernel, shape(shards // 4, 2, slots, width, dtype=BF16), 4)(parts, flat)
     row_totals = exchange(copies, along_z)
-    entries = kernel(
-        entry_kernel,
-        shape(4, slots, width),
-        4,
-        in_specs=[SCALARS, WHOLE, WHOLE, WHOLE],
-        out_specs=WHOLE,
-    )(place, row_totals, parts, flat)
-    entries = exchange(entries, along_y)
+    entries = kernel(entry_kernel, shape(4, slots, width), 4)(row_totals, parts, flat)
     layer_out, grad_parts, direct = kernel(
         gradient_kernel,
         (
@@ -535,7 +524,7 @@
         ahead,
         entries,
     )
-    grad_proj = sum_over_chan(grad_parts, place)
+    grad_proj = sum_over_chan(grad_parts)
     signal_grad = kernel(finish_kernel, shape(rows, width, dtype=BF16), 8)(
         grad_proj, w_turned, direct
     )

time: 93.1 us -> 87.1 us (0.936)
  blocking collectives: 68.1 us -> 64 us
  Pallas kernels: 13.3 us -> 11.5 us
    all_to_all x3 -> x2, blocking collectives: 37.2 us -> 31.5 us  [exchange(): lax.all_to_all(array, 'seq', 0, 0, tiled=True, axis_index_groups=groups)]
    pallas_call x4, Pallas kernels: 3.12 us -> 1.38 us  [the longest x2 0.78 us: sum_over_chan(): kernel(pair_kernel, shape(count // 2, rows // 2, columns, dtype=BF16), 4)]
    all_gather x2, blocking collectives: 15.7 us -> 17.4 us  [sum_over_chan(): lax.all_gather(part, 'chan', axis=0, tiled=True, axis_index_groups=pairs)]
where the time goes in v5:
time: 87.1 us; the launch traced here: 86.7 us
  blocking collectives  64 us (73%)
  Pallas kernels  11.5 us (13%)
  waiting for transfers between devices  6.19 us (7%)
  starting transfers between devices  3.58 us (4%)
    all_to_all x2, blocking collectives, exchange(): lax.all_to_all(array, 'seq', 0, 0, tiled=True, axis_index_groups=groups)  31.5 us
    all_gather x2, blocking collectives, sum_over_chan(): lax.all_gather(part, 'chan', axis=0, tiled=True, axis_index_groups=pairs)  17.4 us
    all_to_all x1, blocking collectives, sum_over_chan(): lax.all_to_all(copies, 'chan', 0, 0, tiled=True, axis_index_groups=across)  9.18 us
    all_to_all x1, waiting for transfers between devices, sum_over_chan(): lax.all_to_all(copies, 'chan', 0, 0, tiled=True, axis_index_groups=across)  6.19 us
    all_gather x2, blocking collectives, sum_over_chan(): lax.all_gather(half, 'chan', axis=0, tiled=True, axis_index_groups=pairs)  6.01 us
    pallas_call x1, Pallas kernels, local(): kernel(gradient_kernel, (shape(rows, width, dtype=BF16), shape(rows, colu...  5.02 us
    all_to_all x1, starting transfers between devices, sum_over_chan(): lax.all_to_all(copies, 'chan', 0, 0, tiled=True, axis_index_groups=across)  3.58 us
    pallas_call x1, Pallas kernels, local(): kernel(summary_kernel, (shape(2, rows, width), shape(2, rows, width), sha...  2.61 us
  transfers between devices with their start and end apart: 1, of which 1 were waited for; matrix products, arithmetic and copies ran while one was open for 0% of the time, Pallas kernels for 0%

profile of v5, /device:TPU:1, one launch (start us, length us, event | category | flops | bytes accessed | tf_op | source)
XLA Modules:
  0.0 86.7 jit_solution(10070855248107470748)
XLA Ops:
  0.6 1.3 %project_kernel.1 = (f32[128,256]{1,0:T(8,128)S(1)}, f32[128,560]{1,0:T(8,128)S(1)}) custom-call(bf16[128,256]{1,0:T(8,128)(2,1)} %signal.1, bf16[560,256]{1,0:T(8,128)(2,1)} %bitcast.3), custom_call_target="tpu_custom_call" | custom-call | tf_op jit(solution)/shard_map/project_kernel/pallas_call | solution.py:458
  1.9 8.7 %all_gather.12.both = f32[256,560]{1,0:T(8,128)S(1)} all-gather(f32[128,560]{1,0:T(8,128)S(1)} %get-tuple-element.17), channel_id=1, replica_groups={{0,1},{2,3},{4,5},{6,7},{8,9},{10,11},{12,13},{14,15},{16,17},{18,19},{..., dimensions={0}, use_global_device_ids=true | all-gather | bytes 860160 | tf_op jit(solution)/shard_map/all_gather | solution.py:431
  10.7 0.8 pair_kernel.2
  11.4 3.6 %all-to-all-start = ((bf16[4,64,560]{2,1,0:T(8,128)(2,1)}), bf16[4,64,560]{2,1,0:T(8,128)(2,1)S(1)}, u32[]{:S(2)}, u32[]{:S(2)}) async-start(bf16[4,64,560]{2,1,0:T(8,128)(2,1)} %pair_kernel.2), calls=%async_computation | async-start | bytes 655360 | tf_op jit(solution)/shard_map/all_to_all | solution.py:437
  15.0 0.0 copy-start.4
  15.0 0.0 copy-start.5
  15.0 0.0 copy-done.2
  15.0 0.0 copy-done.3
  15.0 0.6 copy-done.4
  15.7 0.0 copy-done.5
  15.7 0.2 prepare_kernel.1
  15.9 6.2 %all-to-all-done.parts = bf16[4,64,560]{2,1,0:T(8,128)(2,1)S(1)} async-done(((bf16[4,64,560]{2,1,0:T(8,128)(2,1)}), bf16[4,64,560]{2,1,0:T(8,128)(2,1)S(1)}, u32[]{:S(2)}, u32[]{:S(2)}) %all-to-all-start) | async-done | bytes 286752 | tf_op jit(solution)/shard_map/all_to_all | solution.py:437
  22.1 2.8 %all_gather.13.projected = bf16[128,560]{1,0:T(8,128)(2,1)S(1)} all-gather(bf16[64,560]{1,0:T(8,128)(2,1)S(1)} %chips_kernel.2), channel_id=1, replica_groups={{0,1},{2,3},{4,5},{6,7},{8,9},{10,11},{12,13},{14,15},{16,17},{18,19},{..., dimensions={0}, use_global_device_ids=true | all-gather | bytes 215040 | tf_op jit(solution)/shard_map/all_gather | solution.py:439
  24.9 2.6 %summary_kernel.1 = (f32[2,128,256]{2,1,0:T(8,128)S(1)}, f32[2,128,256]{2,1,0:T(8,128)S(1)}, f32[4,12,8,256]{3,2,1,0:T(8,128)S(1)}, f32[4,8,256]{2,1,0:T(8,128)S(1)}, bf16[4,4,16,256]{3,2,1,0:T(8,128)(2,1)S(1)}) custom-call(bf16[128,560]{1,0:T(8,128)(2,1)S(1)} %all_gather.13.projected, bf16[2,256,256]{2,1,0:T(8,128)(2,1)S(1)} %copy-done.1, ...), custom_call_target="tpu_custom_call" | custom-call | tf_op jit(solution)/shard_map/summary_kernel/pallas_call | solution.py:481
  27.5 7.2 %all_to_all.20.parts = bf16[4,4,16,256]{3,2,1,0:T(8,128)(2,1)S(1)} all-to-all(bf16[4,4,16,256]{3,2,1,0:T(8,128)(2,1)S(1)} %get-tuple-element.27), channel_id=1, replica_groups={{0,8,16,24},{32,40,48,56},{64,72,80,88},{96,104,112,120},{128,136,144,1..., dimensions={0} | all-to-all | bytes 262144 | tf_op jit(solution)/shard_map/all_to_all | solution.py:456
  34.8 0.2 row_kernel.1
  35.0 24.3 %all_to_all.21.rows = bf16[16,2,16,256]{3,2,1,0:T(8,128)(2,1)S(1)} all-to-all(bf16[16,2,16,256]{3,2,1,0:T(8,128)(2,1)S(1)} %row_kernel.1), channel_id=1, replica_groups={{0,32,64,96,128,160,192,224,256,288,320,352,384,416,448,480},{8,40,72,1..., dimensions={0} | all-to-all | bytes 524288 | tf_op jit(solution)/shard_map/all_to_all | solution.py:456
  59.2 0.4 entry_kernel.1.entries
  59.6 5.0 %gradient_kernel.1 = (bf16[128,256]{1,0:T(8,128)(2,1)}, f32[128,560]{1,0:T(8,128)S(1)}, f32[128,256]{1,0:T(8,128)S(1)}) custom-call(bf16[128,560]{1,0:T(8,128)(2,1)S(1)} %all_gather.13.projected, bf16[2,256,256]{2,1,0:T(8,128)(2,1)S(1)} %copy-done.1, f32[2,12,8,256]{3,2,1,0:T(8,128)S(1)} %get-tuple-element.18.rates, ...), custom_call_target="tpu_custom_call" | custom-call | tf_op jit(solution)/shard_map/gradient_kernel/pallas_call | solution.py:497
  64.6 8.6 %all_gather.14.both = f32[256,560]{1,0:T(8,128)S(1)} all-gather(f32[128,560]{1,0:T(8,128)S(1)} %get-tuple-element.30), channel_id=1, replica_groups={{0,1},{2,3},{4,5},{6,7},{8,9},{10,11},{12,13},{14,15},{16,17},{18,19},{..., dimensions={0}, use_global_device_ids=true | all-gather | bytes 860160 | tf_op jit(solution)/shard_map/all_gather | solution.py:431
  73.3 9.2 %all_to_all.22.parts = bf16[4,64,560]{2,1,0:T(8,128)(2,1)S(1)} all-to-all(bf16[4,64,560]{2,1,0:T(8,128)(2,1)S(1)} %pair_kernel.3), channel_id=1, replica_groups={{0,2,4,6},{1,3,5,7},{8,10,12,14},{9,11,13,15},{16,18,20,22},{17,19,21,2..., dimensions={0} | all-to-all | bytes 573440 | tf_op jit(solution)/shard_map/all_to_all | solution.py:437
  82.5 3.2 %all_gather.15.grad_proj = bf16[128,560]{1,0:T(8,128)(2,1)S(1)} all-gather(bf16[64,560]{1,0:T(8,128)(2,1)S(1)} %chips_kernel.3), channel_id=1, replica_groups={{0,1},{2,3},{4,5},{6,7},{8,9},{10,11},{12,13},{14,15},{16,17},{18,19},{..., dimensions={0}, use_global_device_ids=true | all-gather | bytes 215040 | tf_op jit(solution)/shard_map/all_gather | solution.py:439
  85.7 0.0 copy-done
  85.7 1.0 %finish_kernel.1 = bf16[128,256]{1,0:T(8,128)(2,1)} custom-call(bf16[128,560]{1,0:T(8,128)(2,1)S(1)} %all_gather.15.grad_proj, bf16[560,256]{1,0:T(8,128)(2,1)S(1)} %bitcast.4, f32[128,256]{1,0:T(8,128)S(1)} %get-tuple-element.31.direct), custom_call_target="tpu_custom_call" | custom-call | tf_op jit(solution)/shard_map/finish_kernel/pallas_call | solution.py:528
  (8 shorter events, 0.1 us)
Async XLA Ops:
  11.4 3.6 %copy-start.2 = (bf16[128,256]{1,0:T(8,128)(2,1)S(1)}, bf16[128,256]{1,0:T(8,128)(2,1)}, u32[]{:S(2)}) copy-start(bf16[128,256]{1,0:T(8,128)(2,1)} %cotangent.1) | copy-start | bytes 196612
  11.4 3.6 %copy-start.3 = (f32[2,12,256]{2,0,1:T(2,128)S(1)}, f32[2,12,256]{2,0,1:T(2,128)}, u32[]{:S(2)}) copy-start(f32[2,12,256]{2,0,1:T(2,128)} %param.12) | copy-start | bytes 73732
  11.4 10.7 %all-to-all-start = ((bf16[4,64,560]{2,1,0:T(8,128)(2,1)}), bf16[4,64,560]{2,1,0:T(8,128)(2,1)S(1)}, u32[]{:S(2)}, u32[]{:S(2)}) async-start(bf16[4,64,560]{2,1,0:T(8,128)(2,1)} %pair_kernel.2), calls=%async_computation | async-start | bytes 655360 | tf_op jit(solution)/shard_map/all_to_all | solution.py:437
  15.0 0.7 copy-start.4
  15.0 0.7 copy-start.5
  15.9 9.0 %copy-start.1 = (bf16[2,256,256]{2,1,0:T(8,128)(2,1)S(1)}, bf16[2,256,256]{2,1,0:T(8,128)(2,1)}, u32[]{:S(2)}) copy-start(bf16[2,256,256]{2,1,0:T(8,128)(2,1)} %w_delta.3) | copy-start | bytes 786436
  82.5 3.3 %copy-start = (bf16[256,560]{0,1:T(8,128)(2,1)S(1)}, bf16[256,560]{0,1:T(8,128)(2,1)}, u32[]{:S(2)}) copy-start(bf16[256,560]{0,1:T(8,128)(2,1)} %param.9) | copy-start | bytes 860164

commit v6 on v5

--- a/solution.py
+++ b/solution.py
@@ -79,12 +79,12 @@
     return slice(block * LANES, (block + 1) * LANES)
 
 
-def spread_gates(gates, spread):
+def spread_gates(gates, spread, first=0):
     count = gates.shape[1]
-    for pair in range(count // 2):
+    for pair in range(spread.shape[1] // (2 * LANES)):
         source = lax.broadcasted_iota(jnp.int32, (count, 2 * LANES), 0)
         lane = lax.broadcasted_iota(jnp.int32, (count, 2 * LANES), 1)
-        pick = jnp.where(source == 2 * pair + lane // LANES, 1.0, 0.0).astype(BF16)
+        pick = jnp.where(source == first + 2 * pair + lane // LANES, 1.0, 0.0).astype(BF16)
         spread[:, pair * 2 * LANES : (pair + 1) * 2 * LANES] = dot(gates, pick)
 
 
@@ -193,13 +193,9 @@
                     )
                     shares[2 * way + kind, n : n + 1, lanes] = scanned[edge : edge + 1]
                 put_total(shares, 2 * way + kind, lanes, whole)
-    payload[0] = shares[...].astype(BF16)
-    for copy in range(1, payload.shape[0]):
-        payload[copy] = payload[0]
-
-
-RISING = (0, 3)
-FALLING = (1, 2)
+    for shard in range(payload.shape[0]):
+        way = shard % 2
+        payload[shard] = shares[2 * way : 2 * way + 2].astype(BF16)
 
 
 def order(count, falling):
@@ -212,19 +208,24 @@
     return jnp.exp2(rates * total) * state + block
 
 
+def place_of(shards):
+    place = lax.axis_index("seq")
+    return place // shards, place % shards, place % 2
+
+
 def row_kernel(parts, flat, copies):
     shards, _, slots, width = parts.shape
     depth = slots - 4
-    here = lax.axis_index("seq") // shards
+    here, _, way = place_of(shards)
     slot = lax.broadcasted_iota(jnp.int32, (slots, width), 0)
     packed = []
-    for kind in range(4):
+    for falling in (False, True):
         state = jnp.zeros((slots, width), F32)
         total = jnp.zeros((1, width), F32)
-        for shard in order(shards, kind in FALLING):
-            block = parts[shard, kind].astype(F32)
+        for shard in order(shards, falling):
+            block = parts[shard, 1 - way if falling else way].astype(F32)
             total = total + block[depth : depth + 1] + block[depth + 1 : depth + 2]
-            state = pass_by(state, block, flat[kind // 2])
+            state = pass_by(state, block, flat[way])
         coarse = total.astype(BF16).astype(F32)
         state = jnp.where(slot == depth, coarse, state)
         state = jnp.where(slot == depth + 1, total - coarse, state)
@@ -233,39 +234,36 @@
 
         @pl.when(row > here)
         def _():
-            for place, kind in enumerate(RISING):
-                copies[row, place] = packed[kind]
+            copies[row] = packed[0]
 
         @pl.when(row <= here)
         def _():
-            for place, kind in enumerate(FALLING):
-                copies[row, place] = packed[kind]
-
-
-def entry_kernel(rows, parts, flat, entries):
-    count, _, slots, width = rows.shape
+            copies[row] = packed[1]
+
+
+def entry_kernel(rows, parts, flat, mine, other, every):
+    count, slots, width = rows.shape
     shards = parts.shape[0]
-    place = lax.axis_index("seq")
-    row_here = place // shards
-    here = place % shards
-    for falling, kinds in ((False, RISING), (True, FALLING)):
-        for slot, kind in enumerate(kinds):
-            rates = flat[kind // 2]
-            state = jnp.zeros((slots, width), F32)
-            for row in order(count, falling):
-                passed = pass_by(state, rows[row, slot].astype(F32), rates)
-                state = jnp.where(row > row_here if falling else row < row_here, passed, state)
-            for shard in order(shards, falling):
-                passed = pass_by(state, parts[shard, kind].astype(F32), rates)
-                state = jnp.where(shard > here if falling else shard < here, passed, state)
-            entries[kind] = state
-
-
-def gradient_kernel(
+    row_here, here, way = place_of(shards)
+    rates = flat[way]
+    for falling in (False, True):
+        kind = 1 - way if falling else way
+        state = jnp.zeros((slots, width), F32)
+        for row in order(count, falling):
+            passed = pass_by(state, rows[row].astype(F32), rates)
+            state = jnp.where(row > row_here if falling else row < row_here, passed, state)
+        for shard in order(shards, falling):
+            every[shard] = state
+            state = pass_by(state, parts[shard, kind].astype(F32), rates)
+        mine[kind] = every[here]
+        other[kind] = every[here + 1 - 2 * way]
+
+
+def direction_gradient(
+    way,
     projected,
     w_delta,
     rates,
-    skip_gain,
     signal,
     cot,
     delta,
@@ -273,11 +271,11 @@
     local,
     ahead,
     entries,
-    layer_out,
-    parts_out,
-    direct_out,
+    core,
+    direct,
+    low,
+    gate_grad,
     weight,
-    core,
     grad_pre,
     fades,
     kept,
@@ -289,100 +287,94 @@
     depth = rates.shape[1]
     steps = rows // GROUPS
     blocks = width // LANES
-    spread_gates(projected[:, 2 * rank :], spread)
-    core[...] = skip_gain[...] * signal[...]
-    direct_out[...] = skip_gain[...] * cot[...]
-    for way in range(2):
-        weight[...] = delta[way] * signal[...]
-        falling = way == 1
-        first = 2 * way * depth
-
-        def entering(kind):
-            gap = [ahead[2 * way + kind, :, lane_block(block)] for block in range(blocks)]
-            return tuple(
-                local[2 * way + kind, n, :, lane_block(block)]
-                + jnp.exp2(gap[block] * rates[way, n, :, lane_block(block)])
-                * entries[2 * way + kind, n : n + 1, lane_block(block)]
-                for n in range(depth)
-                for block in range(blocks)
-            )
-
-        def pieces(array, step):
-            return [array[at(step), lane_block(block)] for block in range(blocks)]
-
-        def put_products(which, step, rows_of):
-            start = pl.multiple_of(step * depth * GROUPS, 2 * GROUPS)
-            for block in range(blocks):
-                stacked = jnp.concatenate(rows_of[block], 0).astype(BF16)
-                products[which, pl.ds(start, depth * GROUPS), lane_block(block)] = stacked
-
-        def walk_states(index, states):
-            step = steps - 1 - index if falling else index
-            d, w, g = pieces(delta.at[way], step), pieces(weight, step), pieces(cot, step)
-            total = pieces(core, step)
-            rows_of = [[] for _ in range(blocks)]
-            result = []
-            for n in range(depth):
-                gate_in = gate_at(spread, step, first + n)
-                gate_out = gate_at(spread, step, first + depth + n)
-                for block in range(blocks):
-                    lanes = lane_block(block)
-                    fade = jnp.exp2(d[block] * rates[way, n, :, lanes])
-                    fades[step, n, :, lanes] = fade
-                    faded = fade * states[n * blocks + block]
-                    kept[step, n, :, lanes] = faded
-                    state = faded + w[block] * gate_in
-                    total[block] = total[block] + gate_out * state
-                    rows_of[block].append(g[block] * state)
-                    result.append(state)
-            for block in range(blocks):
-                core[at(step), lane_block(block)] = total[block]
-            put_products(2 * way + 1, step, rows_of)
-            return tuple(result)
-
-        lax.fori_loop(0, steps, walk_states, entering(0))
-
-        def walk_adjoints(index, carried):
-            step = index if falling else steps - 1 - index
-            w, g = pieces(weight, step), pieces(cot, step)
-            rows_of = [[] for _ in range(blocks)]
-            through = [jnp.zeros((GROUPS, LANES), F32)] * blocks
-            fading = [jnp.zeros((GROUPS, LANES), F32)] * blocks
-            result = []
-            for n in range(depth):
-                gate_in = gate_at(spread, step, first + n)
-                gate_out = gate_at(spread, step, first + depth + n)
-                for block in range(blocks):
-                    lanes = lane_block(block)
-                    adjoint = g[block] * gate_out + carried[n * blocks + block]
-                    result.append(fades[step, n, :, lanes] * adjoint)
-                    through[block] = through[block] + adjoint * gate_in
-                    fading[block] = fading[block] + (
-                        adjoint * kept[step, n, :, lanes] * rates[way, n, :, lanes]
-                    )
-                    rows_of[block].append(adjoint * w[block])
-            put_products(2 * way, step, rows_of)
+    first = 2 * way * depth
+    spread_gates(projected[:, 2 * rank :], spread, first)
+    weight[...] = delta[way] * signal[...]
+
+    def entering(kind):
+        gap = [ahead[2 * way + kind, :, lane_block(block)] for block in range(blocks)]
+        return tuple(
+            local[2 * way + kind, n, :, lane_block(block)]
+            + jnp.exp2(gap[block] * rates[way, n, :, lane_block(block)])
+            * entries[kind, n : n + 1, lane_block(block)]
+            for n in range(depth)
+            for block in range(blocks)
+        )
+
+    def pieces(array, step):
+        return [array[at(step), lane_block(block)] for block in range(blocks)]
+
+    def put_products(which, step, rows_of):
+        start = pl.multiple_of(step * depth * GROUPS, 2 * GROUPS)
+        for block in range(blocks):
+            stacked = jnp.concatenate(rows_of[block], 0).astype(BF16)
+            products[which, pl.ds(start, depth * GROUPS), lane_block(block)] = stacked
+
+    def walk_states(index, states):
+        step = index + way * (steps - 1 - 2 * index)
+        d, w, g = pieces(delta.at[way], step), pieces(weight, step), pieces(cot, step)
+        total = pieces(core, step)
+        rows_of = [[] for _ in range(blocks)]
+        result = []
+        for n in range(depth):
+            gate_in = gate_at(spread, step, n)
+            gate_out = gate_at(spread, step, depth + n)
             for block in range(blocks):
                 lanes = lane_block(block)
-                grad_delta = through[block] * signal[at(step), lanes] + fading[block] * LN2
-                direct_out[at(step), lanes] = (
-                    direct_out[at(step), lanes] + through[block] * delta[way, at(step), lanes]
+                fade = jnp.exp2(d[block] * rates[way, n, :, lanes])
+                fades[step, n, :, lanes] = fade
+                faded = fade * states[n * blocks + block]
+                kept[step, n, :, lanes] = faded
+                state = faded + w[block] * gate_in
+                total[block] = total[block] + gate_out * state
+                rows_of[block].append(g[block] * state)
+                result.append(state)
+        for block in range(blocks):
+            core[at(step), lane_block(block)] = total[block]
+        put_products(1, step, rows_of)
+        return tuple(result)
+
+    lax.fori_loop(0, steps, walk_states, entering(0))
+
+    def walk_adjoints(index, carried):
+        step = steps - 1 - index + way * (2 * index - steps + 1)
+        w, g = pieces(weight, step), pieces(cot, step)
+        rows_of = [[] for _ in range(blocks)]
+        through = [jnp.zeros((GROUPS, LANES), F32)] * blocks
+        fading = [jnp.zeros((GROUPS, LANES), F32)] * blocks
+        result = []
+        for n in range(depth):
+            gate_in = gate_at(spread, step, n)
+            gate_out = gate_at(spread, step, depth + n)
+            for block in range(blocks):
+                lanes = lane_block(block)
+                adjoint = g[block] * gate_out + carried[n * blocks + block]
+                result.append(fades[step, n, :, lanes] * adjoint)
+                through[block] = through[block] + adjoint * gate_in
+                fading[block] = fading[block] + (
+                    adjoint * kept[step, n, :, lanes] * rates[way, n, :, lanes]
                 )
-                grad_pre[way, at(step), lanes] = grad_delta * slope[way, at(step), lanes]
-            return tuple(result)
-
-        lax.fori_loop(0, steps, walk_adjoints, entering(1))
-
-    for way in range(2):
-        parts_out[:, way * rank : (way + 1) * rank] = dot(
-            grad_pre[way].astype(BF16), w_delta[way], NT
-        )
+                rows_of[block].append(adjoint * w[block])
+        put_products(0, step, rows_of)
+        for block in range(blocks):
+            lanes = lane_block(block)
+            grad_delta = through[block] * signal[at(step), lanes] + fading[block] * LN2
+            direct[at(step), lanes] = (
+                direct[at(step), lanes] + through[block] * delta[way, at(step), lanes]
+            )
+            grad_pre[at(step), lanes] = grad_delta * slope[way, at(step), lanes]
+        return tuple(result)
+
+    lax.fori_loop(0, steps, walk_adjoints, entering(1))
+    low[...] = dot(grad_pre[...].astype(BF16), w_delta[way], NT)
     ones = jnp.ones((width, LANES), BF16)
-    lane = lax.broadcasted_iota(jnp.int32, (GROUPS, LANES), 1)
+    lane = lax.broadcasted_iota(jnp.int32, (GROUPS, LANES), 1) - first
     height = depth * GROUPS
     for start in range(0, steps, 4):
-        merged = [jnp.zeros((GROUPS, LANES), F32)] * 4
-        for which in range(4):
+        merged = [
+            gate_grad[(start + step) * GROUPS : (start + step + 1) * GROUPS] for step in range(4)
+        ]
+        for which in range(2):
             sums = dot(products[which, start * height : (start + 4) * height], ones)
             for step in range(4):
                 for n in range(depth):
@@ -390,8 +382,31 @@
                     merged[step] = jnp.where(
                         lane == which * depth + n, sums[row : row + GROUPS], merged[step]
                     )
-        stacked = jnp.concatenate(merged, 0)[:, : 4 * depth]
-        parts_out[start * GROUPS : (start + 4) * GROUPS, 2 * rank :] = stacked
+        gate_grad[start * GROUPS : (start + 4) * GROUPS] = jnp.concatenate(merged, 0)
+
+
+def own_gradient_kernel(skip_gain, *refs):
+    signal, cot = refs[3:5]
+    core, direct, _, gate_grad = refs[10:14]
+    core[...] = skip_gain[...] * signal[...]
+    direct[...] = skip_gain[...] * cot[...]
+    gate_grad[...] = jnp.zeros_like(gate_grad)
+    direction_gradient(lax.axis_index("seq") % 2, *refs)
+
+
+def other_gradient_kernel(own_core, own_direct, own_low, own_gates, *refs):
+    inputs = refs[:10]
+    layer_out, parts_out, direct, core, low, gate_grad = refs[10:16]
+    way = 1 - lax.axis_index("seq") % 2
+    core[...] = own_core[...]
+    direct[...] = own_direct[...]
+    gate_grad[...] = own_gates[...]
+    direction_gradient(way, *inputs, core, direct, low, gate_grad, *refs[16:])
+    rows, rank = low.shape
+    gates = parts_out.shape[1] - 2 * rank
+    parts_out[:, pl.ds(pl.multiple_of(way * rank, LANES), rank)] = low[...]
+    parts_out[:, pl.ds(pl.multiple_of((1 - way) * rank, LANES), rank)] = own_low[...]
+    parts_out[:, 2 * rank :] = gate_grad[:, :gates]
     ungroup = grouping(rows, inverse=True)
     layer_out[...] = dot(ungroup, core[...].astype(BF16)).astype(BF16)
 
@@ -485,45 +500,63 @@
             shape(2, rows, width),
             shape(4, depth, GROUPS, width),
             shape(4, GROUPS, width),
-            shape(4, 4, slots, width, dtype=BF16),
+            shape(4, 2, slots, width, dtype=BF16),
         ),
         20,
         (((rows, width), F32), stack, wide, ((4, slots, width), F32)),
     )(projected, w_delta, bias, rates, signal_wide, cot_wide)
     parts = exchange(payload, along_y)
-    copies = kernel(row_kernel, shape(shards // 4, 2, slots, width, dtype=BF16), 4)(parts, flat)
+    copies = kernel(row_kernel, shape(shards // 4, slots, width, dtype=BF16), 4)(parts, flat)
     row_totals = exchange(copies, along_z)
-    entries = kernel(entry_kernel, shape(4, slots, width), 4)(row_totals, parts, flat)
-    layer_out, grad_parts, direct = kernel(
-        gradient_kernel,
-        (
-            shape(rows, width, dtype=BF16),
-            shape(rows, columns),
-            shape(rows, width),
-        ),
-        28,
-        (
-            ((rows, width), F32),
-            ((rows, width), F32),
-            ((2, rows, width), F32),
-            stack,
-            stack,
-            ((4, rows * depth, width), BF16),
-            wide,
-        ),
-    )(
+    entries, others = kernel(
+        entry_kernel,
+        (shape(2, slots, width), shape(2, slots, width)),
+        4,
+        (((4, slots, width), F32),),
+    )(row_totals, parts, flat)
+    swapped = lax.ppermute(others, "seq", [(shard, shard ^ 1) for shard in range(shards)])
+    rank = w_delta.shape[1]
+    inputs = (
         projected,
         w_delta,
         rates,
-        gain,
         signal_wide,
         cot_wide,
         delta,
         slope,
         local_states,
         ahead,
-        entries,
     )
+    scratch = (
+        ((rows, width), F32),
+        ((rows, width), F32),
+        stack,
+        stack,
+        ((2, rows * depth, width), BF16),
+        ((rows, 2 * depth * LANES), F32),
+    )
+    own = kernel(
+        own_gradient_kernel,
+        (
+            shape(rows, width),
+            shape(rows, width),
+            shape(rows, rank),
+            shape(rows, LANES),
+        ),
+        20,
+        scratch,
+        cost=1 << 22,
+    )(gain, *inputs, entries)
+    layer_out, grad_parts, direct = kernel(
+        other_gradient_kernel,
+        (
+            shape(rows, width, dtype=BF16),
+            shape(rows, columns),
+            shape(rows, width),
+        ),
+        20,
+        (((rows, width), F32), ((rows, rank), F32), ((rows, LANES), F32)) + scratch,
+    )(*own, *inputs, swapped)
     grad_proj = sum_over_chan(grad_parts)
     signal_grad = kernel(finish_kernel, shape(rows, width, dtype=BF16), 8)(
         grad_proj, w_turned, direct

time: 87.1 us -> 86.8 us (level)
  blocking collectives: 64 us -> 61.3 us
  starting transfers between devices: 3.58 us -> 5.78 us
    ppermute x0 -> x1, starting transfers between devices: none -> 2.19 us  [local(): lax.ppermute(others, 'seq', [(shard, shard ^ 1) for shard in range(shards)])]
    all_gather x2, blocking collectives: 17.4 us -> 15.7 us  [sum_over_chan(): lax.all_gather(part, 'chan', axis=0, tiled=True, axis_index_groups=pairs)]
    all_to_all x2, blocking collectives: 31.5 us -> 30.4 us  [exchange(): lax.all_to_all(array, 'seq', 0, 0, tiled=True, axis_index_groups=groups)]
    pallas_call x3 -> x4, Pallas kernels: 5.61 us -> 5.76 us  [the longest x1 3.01 us: local(): kernel(other_gradient_kernel, (shape(rows, width, dtype=BF16), shape(rows...]
  transfers between devices with their start and end apart: 1 -> 2, of which waited for: 1 -> 1; matrix products, arithmetic and copies ran while one was open for 0% -> 0% of each run, Pallas kernels for 0% -> 3%
where the time goes in v6:
time: 86.8 us; the launch traced here: 86.4 us
  blocking collectives  61.3 us (71%)
  Pallas kernels  11.7 us (13%)
  waiting for transfers between devices  6.22 us (7%)
  starting transfers between devices  5.78 us (7%)
    all_to_all x2, blocking collectives, exchange(): lax.all_to_all(array, 'seq', 0, 0, tiled=True, axis_index_groups=groups)  30.4 us
    all_gather x2, blocking collectives, sum_over_chan(): lax.all_gather(part, 'chan', axis=0, tiled=True, axis_index_groups=pairs)  15.7 us
    all_to_all x1, blocking collectives, sum_over_chan(): lax.all_to_all(copies, 'chan', 0, 0, tiled=True, axis_index_groups=across)  9.18 us
    all_to_all x1, waiting for transfers between devices, sum_over_chan(): lax.all_to_all(copies, 'chan', 0, 0, tiled=True, axis_index_groups=across)  6.19 us
    all_gather x2, blocking collectives, sum_over_chan(): lax.all_gather(half, 'chan', axis=0, tiled=True, axis_index_groups=pairs)  6.01 us
    all_to_all x1, starting transfers between devices, sum_over_chan(): lax.all_to_all(copies, 'chan', 0, 0, tiled=True, axis_index_groups=across)  3.58 us
    pallas_call x1, Pallas kernels, local(): kernel(other_gradient_kernel, (shape(rows, width, dtype=BF16), shape(rows...  3.01 us
    pallas_call x1, Pallas kernels, local(): kernel(summary_kernel, (shape(2, rows, width), shape(2, rows, width), sha...  2.61 us
  transfers between devices with their start and end apart: 2, of which 1 were waited for; matrix products, arithmetic and copies ran while one was open for 0% of the time, Pallas kernels for 3%

profile of v6, /device:TPU:1, one launch (start us, length us, event | category | flops | bytes accessed | tf_op | source)
XLA Modules:
  0.0 86.4 jit_solution(12187866997212425777)
XLA Ops:
  0.6 1.3 %project_kernel.1 = (f32[128,256]{1,0:T(8,128)S(1)}, f32[128,560]{1,0:T(8,128)S(1)}) custom-call(bf16[128,256]{1,0:T(8,128)(2,1)} %signal.1, bf16[560,256]{1,0:T(8,128)(2,1)} %bitcast.3), custom_call_target="tpu_custom_call" | custom-call | tf_op jit(solution)/shard_map/project_kernel/pallas_call | solution.py:473
  1.9 8.7 %all_gather.12.both = f32[256,560]{1,0:T(8,128)S(1)} all-gather(f32[128,560]{1,0:T(8,128)S(1)} %get-tuple-element.24), channel_id=1, replica_groups={{0,1},{2,3},{4,5},{6,7},{8,9},{10,11},{12,13},{14,15},{16,17},{18,19},{..., dimensions={0}, use_global_device_ids=true | all-gather | bytes 860160 | tf_op jit(solution)/shard_map/all_gather | solution.py:446
  10.7 0.8 pair_kernel.2
  11.4 3.6 %all-to-all-start = ((bf16[4,64,560]{2,1,0:T(8,128)(2,1)}), bf16[4,64,560]{2,1,0:T(8,128)(2,1)S(1)}, u32[]{:S(2)}, u32[]{:S(2)}) async-start(bf16[4,64,560]{2,1,0:T(8,128)(2,1)} %pair_kernel.2), calls=%async_computation | async-start | bytes 655360 | tf_op jit(solution)/shard_map/all_to_all | solution.py:452
  15.0 0.0 copy-start.4
  15.0 0.0 copy-start.5
  15.0 0.6 copy-done.4
  15.7 0.0 copy-done.5
  15.7 0.2 prepare_kernel.1
  15.9 6.2 %all-to-all-done.parts = bf16[4,64,560]{2,1,0:T(8,128)(2,1)S(1)} async-done(((bf16[4,64,560]{2,1,0:T(8,128)(2,1)}), bf16[4,64,560]{2,1,0:T(8,128)(2,1)S(1)}, u32[]{:S(2)}, u32[]{:S(2)}) %all-to-all-start) | async-done | bytes 286752 | tf_op jit(solution)/shard_map/all_to_all | solution.py:452
  22.1 2.8 %all_gather.13.projected.refs_0_ = bf16[128,560]{1,0:T(8,128)(2,1)S(1)} all-gather(bf16[64,560]{1,0:T(8,128)(2,1)S(1)} %chips_kernel.2), channel_id=1, replica_groups={{0,1},{2,3},{4,5},{6,7},{8,9},{10,11},{12,13},{14,15},{16,17},{18,19},{..., dimensions={0}, use_global_device_ids=true | all-gather | bytes 215040 | tf_op jit(solution)/shard_map/all_gather | solution.py:454
  24.9 2.6 %summary_kernel.1 = (f32[2,128,256]{2,1,0:T(8,128)S(1)}, f32[2,128,256]{2,1,0:T(8,128)S(1)}, f32[4,12,8,256]{3,2,1,0:T(8,128)S(1)}, f32[4,8,256]{2,1,0:T(8,128)S(1)}, bf16[4,2,16,256]{3,2,1,0:T(8,128)(2,1)S(1)}) custom-call(bf16[128,560]{1,0:T(8,128)(2,1)S(1)} %all_gather.13.projected.refs_0_, bf16[2,256,256]{2,1,0:T(8,128)(2,1)S(1)} %copy-done, ...), custom_call_target="tpu_custom_call" | custom-call | tf_op jit(solution)/shard_map/summary_kernel/pallas_call | solution.py:496
  27.5 6.8 %all_to_all.20.parts = bf16[4,2,16,256]{3,2,1,0:T(8,128)(2,1)S(1)} all-to-all(bf16[4,2,16,256]{3,2,1,0:T(8,128)(2,1)S(1)} %get-tuple-element.33), channel_id=1, replica_groups={{0,8,16,24},{32,40,48,56},{64,72,80,88},{96,104,112,120},{128,136,144,1..., dimensions={0} | all-to-all | bytes 131072 | tf_op jit(solution)/shard_map/all_to_all | solution.py:471
  34.4 0.2 row_kernel.1
  34.5 23.6 %all_to_all.21.rows = bf16[16,16,256]{2,1,0:T(8,128)(2,1)S(1)} all-to-all(bf16[16,16,256]{2,1,0:T(8,128)(2,1)S(1)} %row_kernel.1), channel_id=1, replica_groups={{0,32,64,96,128,160,192,224,256,288,320,352,384,416,448,480},{8,40,72,1..., dimensions={0} | all-to-all | bytes 262144 | tf_op jit(solution)/shard_map/all_to_all | solution.py:471
  58.1 0.2 entry_kernel.1
  58.2 2.2 %collective-permute-start = (f32[2,16,256]{2,1,0:T(8,128)S(1)}, f32[2,16,256]{2,1,0:T(8,128)S(1)}, u32[]{:S(2)}, u32[]{:S(2)}) collective-permute-start(f32[2,16,256]{2,1,0:T(8,128)S(1)} %get-tuple-element.40), channel_id=1, source_target_pairs={{0,8},{8,0},{16,24},{24,16},{32,40},{40,32},{48,56},{56,48},{64,72... | collective-permute-start | bytes 98312 | tf_op jit(solution)/shard_map/ppermute | solution.py:517
  60.5 2.4 %own_gradient_kernel.1 = (f32[128,256]{1,0:T(8,128)S(1)}, f32[128,256]{1,0:T(8,128)S(1)}, f32[128,256]{1,0:T(8,128)S(1)}, f32[128,128]{1,0:T(8,128)S(1)}) custom-call(f32[1,256]{1,0:T(1,128)S(1)} %get-tuple-element.23.skip_gain, bf16[128,560]{1,0:T(8,128)(2,1)S(1)} %all_gather.13.projected.refs_0_, bf16[2,256,256]{2,1,0:T(8,128)(2,1)S(1)} %copy-done, ...), custom_call_target="tpu_custom_call" | custom-call | flops 4194304 | bytes 4194304 | tf_op jit(solution)/shard_map/own_gradient_kernel/pallas_call | solution.py:538
  62.9 0.0 collective-permute-done.refs_9_
  62.9 3.0 %other_gradient_kernel.1 = (bf16[128,256]{1,0:T(8,128)(2,1)}, f32[128,560]{1,0:T(8,128)S(1)}, f32[128,256]{1,0:T(8,128)S(1)}) custom-call(f32[128,256]{1,0:T(8,128)S(1)} %get-tuple-element.36.own_core, f32[128,256]{1,0:T(8,128)S(1)} %get-tuple-element.37.own_direct, f32[128,256]{1,0:T(8,128)S(1)} %get-tuple-element.38.own_low, ...), custom_call_target="tpu_custom_call" | custom-call | tf_op jit(solution)/shard_map/other_gradient_kernel/pallas_call | solution.py:550
  65.9 7.0 %all_gather.14.both = f32[256,560]{1,0:T(8,128)S(1)} all-gather(f32[128,560]{1,0:T(8,128)S(1)} %get-tuple-element.42), channel_id=1, replica_groups={{0,1},{2,3},{4,5},{6,7},{8,9},{10,11},{12,13},{14,15},{16,17},{18,19},{..., dimensions={0}, use_global_device_ids=true | all-gather | bytes 860160 | tf_op jit(solution)/shard_map/all_gather | solution.py:446
  72.9 9.2 %all_to_all.22.parts = bf16[4,64,560]{2,1,0:T(8,128)(2,1)S(1)} all-to-all(bf16[4,64,560]{2,1,0:T(8,128)(2,1)S(1)} %pair_kernel.3), channel_id=1, replica_groups={{0,2,4,6},{1,3,5,7},{8,10,12,14},{9,11,13,15},{16,18,20,22},{17,19,21,2..., dimensions={0} | all-to-all | bytes 573440 | tf_op jit(solution)/shard_map/all_to_all | solution.py:452
  82.2 3.2 %all_gather.15.grad_proj = bf16[128,560]{1,0:T(8,128)(2,1)S(1)} all-gather(bf16[64,560]{1,0:T(8,128)(2,1)S(1)} %chips_kernel.3), channel_id=1, replica_groups={{0,1},{2,3},{4,5},{6,7},{8,9},{10,11},{12,13},{14,15},{16,17},{18,19},{..., dimensions={0}, use_global_device_ids=true | all-gather | bytes 215040 | tf_op jit(solution)/shard_map/all_gather | solution.py:454
  85.4 1.0 %finish_kernel.1 = bf16[128,256]{1,0:T(8,128)(2,1)} custom-call(bf16[128,560]{1,0:T(8,128)(2,1)S(1)} %all_gather.15.grad_proj, bf16[560,256]{1,0:T(8,128)(2,1)S(1)} %bitcast.4, f32[128,256]{1,0:T(8,128)S(1)} %get-tuple-element.43.direct), custom_call_target="tpu_custom_call" | custom-call | tf_op jit(solution)/shard_map/finish_kernel/pallas_call | solution.py:561
  (11 shorter events, 0.1 us)
Async XLA Ops:
  11.4 3.6 %copy-start.2 = (bf16[128,256]{1,0:T(8,128)(2,1)S(1)}, bf16[128,256]{1,0:T(8,128)(2,1)}, u32[]{:S(2)}) copy-start(bf16[128,256]{1,0:T(8,128)(2,1)} %cotangent.1) | copy-start | bytes 196612
  11.4 3.6 %copy-start.3 = (f32[2,12,256]{2,0,1:T(2,128)S(1)}, f32[2,12,256]{2,0,1:T(2,128)}, u32[]{:S(2)}) copy-start(f32[2,12,256]{2,0,1:T(2,128)} %param.12) | copy-start | bytes 73732
  11.4 10.7 %all-to-all-start = ((bf16[4,64,560]{2,1,0:T(8,128)(2,1)}), bf16[4,64,560]{2,1,0:T(8,128)(2,1)S(1)}, u32[]{:S(2)}, u32[]{:S(2)}) async-start(bf16[4,64,560]{2,1,0:T(8,128)(2,1)} %pair_kernel.2), calls=%async_computation | async-start | bytes 655360 | tf_op jit(solution)/shard_map/all_to_all | solution.py:452
  15.0 0.7 copy-start.4
  15.0 0.7 copy-start.5
  15.9 9.0 %copy-start = (bf16[2,256,256]{2,1,0:T(8,128)(2,1)S(1)}, bf16[2,256,256]{2,1,0:T(8,128)(2,1)}, u32[]{:S(2)}) copy-start(bf16[2,256,256]{2,1,0:T(8,128)(2,1)} %refs_1_.3) | copy-start | bytes 786436
  58.2 4.7 %collective-permute-start = (f32[2,16,256]{2,1,0:T(8,128)S(1)}, f32[2,16,256]{2,1,0:T(8,128)S(1)}, u32[]{:S(2)}, u32[]{:S(2)}) collective-permute-start(f32[2,16,256]{2,1,0:T(8,128)S(1)} %get-tuple-element.40), channel_id=1, source_target_pairs={{0,8},{8,0},{16,24},{24,16},{32,40},{40,32},{48,56},{56,48},{64,72... | collective-permute-start | bytes 98312 | tf_op jit(solution)/shard_map/ppermute | solution.py:517
  82.1 3.3 %copy-start.1 = (bf16[256,560]{0,1:T(8,128)(2,1)S(1)}, bf16[256,560]{0,1:T(8,128)(2,1)}, u32[]{:S(2)}) copy-start(bf16[256,560]{0,1:T(8,128)(2,1)} %param.9) | copy-start | bytes 860164

commit v7 on v6

--- a/solution.py
+++ b/solution.py
@@ -259,9 +259,26 @@
         other[kind] = every[here + 1 - 2 * way]
 
 
+def early_kernel(projected, rates, delta, spread, fades):
+    _, steps, depth, _, _ = fades.shape
+    rank = (projected.shape[1] - 4 * depth) // 2
+    for way in range(2):
+        spread_gates(projected[:, 2 * rank :], spread.at[way], 2 * way * depth)
+
+    def walk(step, _):
+        for way in range(2):
+            d = delta[way, at(step), :]
+            for n in range(depth):
+                fades[way, step, n] = jnp.exp2(d * rates[way, n])
+        return _
+
+    lax.fori_loop(0, steps, walk, 0)
+
+
 def direction_gradient(
     way,
-    projected,
+    spread,
+    fades,
     w_delta,
     rates,
     signal,
@@ -277,18 +294,14 @@
     gate_grad,
     weight,
     grad_pre,
-    fades,
     kept,
     products,
-    spread,
 ):
     rows, width = signal.shape
-    rank = w_delta.shape[1]
     depth = rates.shape[1]
     steps = rows // GROUPS
     blocks = width // LANES
     first = 2 * way * depth
-    spread_gates(projected[:, 2 * rank :], spread, first)
     weight[...] = delta[way] * signal[...]
 
     def entering(kind):
@@ -312,18 +325,16 @@
 
     def walk_states(index, states):
         step = index + way * (steps - 1 - 2 * index)
-        d, w, g = pieces(delta.at[way], step), pieces(weight, step), pieces(cot, step)
+        w, g = pieces(weight, step), pieces(cot, step)
         total = pieces(core, step)
         rows_of = [[] for _ in range(blocks)]
         result = []
         for n in range(depth):
-            gate_in = gate_at(spread, step, n)
-            gate_out = gate_at(spread, step, depth + n)
+            gate_in = gate_at(spread.at[way], step, n)
+            gate_out = gate_at(spread.at[way], step, depth + n)
             for block in range(blocks):
                 lanes = lane_block(block)
-                fade = jnp.exp2(d[block] * rates[way, n, :, lanes])
-                fades[step, n, :, lanes] = fade
-                faded = fade * states[n * blocks + block]
+                faded = fades[way, step, n, :, lanes] * states[n * blocks + block]
                 kept[step, n, :, lanes] = faded
                 state = faded + w[block] * gate_in
                 total[block] = total[block] + gate_out * state
@@ -344,12 +355,12 @@
         fading = [jnp.zeros((GROUPS, LANES), F32)] * blocks
         result = []
         for n in range(depth):
-            gate_in = gate_at(spread, step, n)
-            gate_out = gate_at(spread, step, depth + n)
+            gate_in = gate_at(spread.at[way], step, n)
+            gate_out = gate_at(spread.at[way], step, depth + n)
             for block in range(blocks):
                 lanes = lane_block(block)
                 adjoint = g[block] * gate_out + carried[n * blocks + block]
-                result.append(fades[step, n, :, lanes] * adjoint)
+                result.append(fades[way, step, n, :, lanes] * adjoint)
                 through[block] = through[block] + adjoint * gate_in
                 fading[block] = fading[block] + (
                     adjoint * kept[step, n, :, lanes] * rates[way, n, :, lanes]
@@ -386,8 +397,8 @@
 
 
 def own_gradient_kernel(skip_gain, *refs):
-    signal, cot = refs[3:5]
-    core, direct, _, gate_grad = refs[10:14]
+    signal, cot = refs[4:6]
+    core, direct, _, gate_grad = refs[11:15]
     core[...] = skip_gain[...] * signal[...]
     direct[...] = skip_gain[...] * cot[...]
     gate_grad[...] = jnp.zeros_like(gate_grad)
@@ -395,19 +406,22 @@
 
 
 def other_gradient_kernel(own_core, own_direct, own_low, own_gates, *refs):
-    inputs = refs[:10]
-    layer_out, parts_out, direct, core, low, gate_grad = refs[10:16]
+    inputs = refs[:11]
+    core, parts_out, direct, low, gate_grad = refs[11:16]
     way = 1 - lax.axis_index("seq") % 2
     core[...] = own_core[...]
     direct[...] = own_direct[...]
     gate_grad[...] = own_gates[...]
     direction_gradient(way, *inputs, core, direct, low, gate_grad, *refs[16:])
-    rows, rank = low.shape
+    rank = low.shape[1]
     gates = parts_out.shape[1] - 2 * rank
     parts_out[:, pl.ds(pl.multiple_of(way * rank, LANES), rank)] = low[...]
     parts_out[:, pl.ds(pl.multiple_of((1 - way) * rank, LANES), rank)] = own_low[...]
     parts_out[:, 2 * rank :] = gate_grad[:, :gates]
-    ungroup = grouping(rows, inverse=True)
+
+
+def layer_kernel(core, layer_out):
+    ungroup = grouping(core.shape[0], inverse=True)
     layer_out[...] = dot(ungroup, core[...].astype(BF16)).astype(BF16)
 
 
@@ -507,6 +521,15 @@
     )(projected, w_delta, bias, rates, signal_wide, cot_wide)
     parts = exchange(payload, along_y)
     copies = kernel(row_kernel, shape(shards // 4, slots, width, dtype=BF16), 4)(parts, flat)
+    spread, fades = kernel(
+        early_kernel,
+        (
+            shape(2, rows, 2 * depth * LANES),
+            shape(2, steps, depth, GROUPS, width),
+        ),
+        8,
+        cost=1 << 22,
+    )(projected, rates, delta)
     row_totals = exchange(copies, along_z)
     entries, others = kernel(
         entry_kernel,
@@ -517,7 +540,8 @@
     swapped = lax.ppermute(others, "seq", [(shard, shard ^ 1) for shard in range(shards)])
     rank = w_delta.shape[1]
     inputs = (
-        projected,
+        spread,
+        fades,
         w_delta,
         rates,
         signal_wide,
@@ -531,9 +555,7 @@
         ((rows, width), F32),
         ((rows, width), F32),
         stack,
-        stack,
         ((2, rows * depth, width), BF16),
-        ((rows, 2 * depth * LANES), F32),
     )
     own = kernel(
         own_gradient_kernel,
@@ -543,20 +565,17 @@
             shape(rows, rank),
             shape(rows, LANES),
         ),
-        20,
+        10,
         scratch,
         cost=1 << 22,
     )(gain, *inputs, entries)
-    layer_out, grad_parts, direct = kernel(
+    core, grad_parts, direct = kernel(
         other_gradient_kernel,
-        (
-            shape(rows, width, dtype=BF16),
-            shape(rows, columns),
-            shape(rows, width),
-        ),
-        20,
-        (((rows, width), F32), ((rows, rank), F32), ((rows, LANES), F32)) + scratch,
+        (shape(rows, width), shape(rows, columns), shape(rows, width)),
+        10,
+        (((rows, rank), F32), ((rows, LANES), F32)) + scratch,
     )(*own, *inputs, swapped)
+    layer_out = kernel(layer_kernel, shape(rows, width, dtype=BF16), 4, cost=1 << 20)(core)
     grad_proj = sum_over_chan(grad_parts)
     signal_grad = kernel(finish_kernel, shape(rows, width, dtype=BF16), 8)(
         grad_proj, w_turned, direct

time: 86.8 us -> 87.6 us (level)
  blocking collectives: 61.3 us -> 51.2 us
  waiting for transfers between devices: 6.22 us -> 10.2 us
  starting transfers between devices: 5.78 us -> 9.1 us
  local copies, waits for them, and re-layouts: 0.68 us -> 2.94 us
  Pallas kernels: 11.7 us -> 12.8 us
    all_to_all x1 -> x0, blocking collectives: 9.18 us -> none  [sum_over_chan(): lax.all_to_all(copies, 'chan', 0, 0, tiled=True, axis_index_groups=across)]
    all_to_all x1 -> x2, waiting for transfers between devices: 6.19 us -> 10.2 us  [sum_over_chan(): lax.all_to_all(copies, 'chan', 0, 0, tiled=True, axis_index_groups=across)]
    all_to_all x1 -> x2, starting transfers between devices: 3.58 us -> 6.91 us  [sum_over_chan(): lax.all_to_all(copies, 'chan', 0, 0, tiled=True, axis_index_groups=across)]
    unnamed x12, local copies, waits for them, and re-layouts: 0.68 us -> 2.94 us
    pallas_call x1 -> x3, Pallas kernels: 3.01 us -> 3.86 us  [the longest x1 1.96 us: local(): kernel(other_gradient_kernel, (shape(rows, width), shape(rows, columns),...]
  transfers between devices with their start and end apart: 2 -> 3, of which waited for: 1 -> 2; matrix products, arithmetic and copies ran while one was open for 0% -> 0% of each run, Pallas kernels for 3% -> 5%
where the time goes in v7:
time: 87.6 us; the launch traced here: 87 us
  blocking collectives  51.2 us (58%)
  Pallas kernels  12.8 us (15%)
  waiting for transfers between devices  10.2 us (12%)
  starting transfers between devices  9.1 us (10%)
  local copies, waits for them, and re-layouts  2.94 us (3%)
    all_to_all x2, blocking collectives, exchange(): lax.all_to_all(array, 'seq', 0, 0, tiled=True, axis_index_groups=groups)  30.4 us
    all_gather x2, blocking collectives, sum_over_chan(): lax.all_gather(part, 'chan', axis=0, tiled=True, axis_index_groups=pairs)  15.2 us
    all_to_all x2, waiting for transfers between devices, sum_over_chan(): lax.all_to_all(copies, 'chan', 0, 0, tiled=True, axis_index_groups=across)  10.2 us
    all_to_all x2, starting transfers between devices, sum_over_chan(): lax.all_to_all(copies, 'chan', 0, 0, tiled=True, axis_index_groups=across)  6.91 us
    all_gather x2, blocking collectives, sum_over_chan(): lax.all_gather(half, 'chan', axis=0, tiled=True, axis_index_groups=pairs)  5.59 us
    unnamed x12, local copies, waits for them, and re-layouts  2.94 us
    pallas_call x1, Pallas kernels, local(): kernel(summary_kernel, (shape(2, rows, width), shape(2, rows, width), sha...  2.61 us
    ppermute x1, starting transfers between devices, local(): lax.ppermute(others, 'seq', [(shard, shard ^ 1) for shard in range(shards)])  2.19 us
  transfers between devices with their start and end apart: 3, of which 2 were waited for; matrix products, arithmetic and copies ran while one was open for 0% of the time, Pallas kernels for 5%

profile of v7, /device:TPU:1, one launch (start us, length us, event | category | flops | bytes accessed | tf_op | source)
XLA Modules:
  0.0 87.0 jit_solution(9978149154066337575)
XLA Ops:
  0.6 1.3 %project_kernel.1 = (f32[128,256]{1,0:T(8,128)S(1)}, f32[128,560]{1,0:T(8,128)S(1)}) custom-call(bf16[128,256]{1,0:T(8,128)(2,1)} %signal.1, bf16[560,256]{1,0:T(8,128)(2,1)} %bitcast.3), custom_call_target="tpu_custom_call" | custom-call | tf_op jit(solution)/shard_map/project_kernel/pallas_call | solution.py:487
  2.0 8.7 %all_gather.12.both = f32[256,560]{1,0:T(8,128)S(1)} all-gather(f32[128,560]{1,0:T(8,128)S(1)} %get-tuple-element.26), channel_id=1, replica_groups={{0,1},{2,3},{4,5},{6,7},{8,9},{10,11},{12,13},{14,15},{16,17},{18,19},{..., dimensions={0}, use_global_device_ids=true | all-gather | bytes 860160 | tf_op jit(solution)/shard_map/all_gather | solution.py:460
  10.7 0.7 pair_kernel.2
  11.5 3.5 %all-to-all-start = ((bf16[4,64,560]{2,1,0:T(8,128)(2,1)}), bf16[4,64,560]{2,1,0:T(8,128)(2,1)S(1)}, u32[]{:S(2)}, u32[]{:S(2)}) async-start(bf16[4,64,560]{2,1,0:T(8,128)(2,1)} %pair_kernel.2), calls=%async_computation | async-start | bytes 655360 | tf_op jit(solution)/shard_map/all_to_all | solution.py:466
  14.9 0.8 copy-done.2
  15.8 0.7 copy-done.3
  16.5 0.7 copy-done.4
  17.2 0.7 copy-done.5
  18.0 3.9 %all-to-all-done.parts = bf16[4,64,560]{2,1,0:T(8,128)(2,1)S(1)} async-done(((bf16[4,64,560]{2,1,0:T(8,128)(2,1)}), bf16[4,64,560]{2,1,0:T(8,128)(2,1)S(1)}, u32[]{:S(2)}, u32[]{:S(2)}) %all-to-all-start) | async-done | bytes 286752 | tf_op jit(solution)/shard_map/all_to_all | solution.py:466
  22.0 2.8 %all_gather.13.projected = bf16[128,560]{1,0:T(8,128)(2,1)S(1)} all-gather(bf16[64,560]{1,0:T(8,128)(2,1)S(1)} %chips_kernel.2), channel_id=1, replica_groups={{0,1},{2,3},{4,5},{6,7},{8,9},{10,11},{12,13},{14,15},{16,17},{18,19},{..., dimensions={0}, use_global_device_ids=true | all-gather | bytes 215040 | tf_op jit(solution)/shard_map/all_gather | solution.py:468
  24.8 2.6 %summary_kernel.1 = (f32[2,128,256]{2,1,0:T(8,128)S(1)}, f32[2,128,256]{2,1,0:T(8,128)S(1)}, f32[4,12,8,256]{3,2,1,0:T(8,128)S(1)}, f32[4,8,256]{2,1,0:T(8,128)S(1)}, bf16[4,2,16,256]{3,2,1,0:T(8,128)(2,1)S(1)}) custom-call(bf16[128,560]{1,0:T(8,128)(2,1)S(1)} %all_gather.13.projected, bf16[2,256,256]{2,1,0:T(8,128)(2,1)S(1)} %copy-done, ...), custom_call_target="tpu_custom_call" | custom-call | tf_op jit(solution)/shard_map/summary_kernel/pallas_call | solution.py:510
  27.4 6.8 %all_to_all.20.parts = bf16[4,2,16,256]{3,2,1,0:T(8,128)(2,1)S(1)} all-to-all(bf16[4,2,16,256]{3,2,1,0:T(8,128)(2,1)S(1)} %get-tuple-element.37), channel_id=1, replica_groups={{0,8,16,24},{32,40,48,56},{64,72,80,88},{96,104,112,120},{128,136,144,1..., dimensions={0} | all-to-all | bytes 131072 | tf_op jit(solution)/shard_map/all_to_all | solution.py:485
  34.4 23.6 %all_to_all.21.rows = bf16[16,16,256]{2,1,0:T(8,128)(2,1)S(1)} all-to-all(bf16[16,16,256]{2,1,0:T(8,128)(2,1)S(1)} %row_kernel.1), channel_id=1, replica_groups={{0,32,64,96,128,160,192,224,256,288,320,352,384,416,448,480},{8,40,72,1..., dimensions={0} | all-to-all | bytes 262144 | tf_op jit(solution)/shard_map/all_to_all | solution.py:485
  58.2 2.2 %collective-permute-start = (f32[2,16,256]{2,1,0:T(8,128)S(1)}, f32[2,16,256]{2,1,0:T(8,128)S(1)}, u32[]{:S(2)}, u32[]{:S(2)}) collective-permute-start(f32[2,16,256]{2,1,0:T(8,128)S(1)} %get-tuple-element.44), channel_id=1, source_target_pairs={{0,8},{8,0},{16,24},{24,16},{32,40},{40,32},{48,56},{56,48},{64,72... | collective-permute-start | bytes 98312 | tf_op jit(solution)/shard_map/ppermute | solution.py:540
  60.4 1.1 %early_kernel.1 = (f32[2,128,3072]{2,1,0:T(8,128)S(1)}, f32[2,16,12,8,256]{4,3,2,1,0:T(8,128)S(1)}) custom-call(bf16[128,560]{1,0:T(8,128)(2,1)S(1)} %all_gather.13.projected, f32[2,12,8,256]{3,2,1,0:T(8,128)S(1)} %get-tuple-element.27.rates.refs_3_, f32[2,128,256]{2,1,0:T(8,128)S(1)} %get-tuple-element.31.delta.refs_6_), custom_call_target="tpu_custom_call" | custom-call | flops 4194304 | bytes 4194304 | tf_op jit(solution)/shard_map/early_kernel/pallas_call | solution.py:524
  61.5 2.0 %own_gradient_kernel.1 = (f32[128,256]{1,0:T(8,128)S(1)}, f32[128,256]{1,0:T(8,128)S(1)}, f32[128,256]{1,0:T(8,128)S(1)}, f32[128,128]{1,0:T(8,128)S(1)}) custom-call(f32[1,256]{1,0:T(1,128)S(1)} %get-tuple-element.25.skip_gain, f32[2,128,3072]{2,1,0:T(8,128)S(1)} %get-tuple-element.32.refs_0_, f32[2,16,12,8,256]{4,3,2,1,0:T(8,128)S(1)} %get-tuple-element.33.refs_1_, ...), custom_call_target="tpu_custom_call" | custom-call | flops 4194304 | bytes 4194304 | tf_op jit(solution)/shard_map/own_gradient_kernel/pallas_call | solution.py:560
  63.5 2.0 %other_gradient_kernel.1 = (f32[128,256]{1,0:T(8,128)S(1)}, f32[128,560]{1,0:T(8,128)S(1)}, f32[128,256]{1,0:T(8,128)S(1)}) custom-call(f32[128,256]{1,0:T(8,128)S(1)} %get-tuple-element.40.own_core, f32[128,256]{1,0:T(8,128)S(1)} %get-tuple-element.41.own_direct, f32[128,256]{1,0:T(8,128)S(1)} %get-tuple-element.42.own_low, ...), custom_call_target="tpu_custom_call" | custom-call | tf_op jit(solution)/shard_map/other_gradient_kernel/pallas_call | solution.py:572
  65.4 6.5 %all_gather.14.both = f32[256,560]{1,0:T(8,128)S(1)} all-gather(f32[128,560]{1,0:T(8,128)S(1)} %get-tuple-element.46), channel_id=1, replica_groups={{0,1},{2,3},{4,5},{6,7},{8,9},{10,11},{12,13},{14,15},{16,17},{18,19},{..., dimensions={0}, use_global_device_ids=true | all-gather | bytes 860160 | tf_op jit(solution)/shard_map/all_gather | solution.py:460
  71.9 0.7 pair_kernel.3
  72.7 3.5 %all-to-all-start.3 = ((bf16[4,64,560]{2,1,0:T(8,128)(2,1)}), bf16[4,64,560]{2,1,0:T(8,128)(2,1)S(1)}, u32[]{:S(2)}, u32[]{:S(2)}) async-start(bf16[4,64,560]{2,1,0:T(8,128)(2,1)} %pair_kernel.3), calls=%async_computation.3 | async-start | bytes 655360 | tf_op jit(solution)/shard_map/all_to_all | solution.py:466
  76.1 0.8 layer_kernel.1
  76.9 6.3 %all-to-all-done.3.parts = bf16[4,64,560]{2,1,0:T(8,128)(2,1)S(1)} async-done(((bf16[4,64,560]{2,1,0:T(8,128)(2,1)}), bf16[4,64,560]{2,1,0:T(8,128)(2,1)S(1)}, u32[]{:S(2)}, u32[]{:S(2)}) %all-to-all-start.3) | async-done | bytes 286752 | tf_op jit(solution)/shard_map/all_to_all | solution.py:466
  83.2 2.8 %all_gather.15.grad_proj = bf16[128,560]{1,0:T(8,128)(2,1)S(1)} all-gather(bf16[64,560]{1,0:T(8,128)(2,1)S(1)} %chips_kernel.3), channel_id=1, replica_groups={{0,1},{2,3},{4,5},{6,7},{8,9},{10,11},{12,13},{14,15},{16,17},{18,19},{..., dimensions={0}, use_global_device_ids=true | all-gather | bytes 215040 | tf_op jit(solution)/shard_map/all_gather | solution.py:468
  86.0 1.0 %finish_kernel.1 = bf16[128,256]{1,0:T(8,128)(2,1)} custom-call(bf16[128,560]{1,0:T(8,128)(2,1)S(1)} %all_gather.15.grad_proj, bf16[560,256]{1,0:T(8,128)(2,1)S(1)} %bitcast.4, f32[128,256]{1,0:T(8,128)S(1)} %get-tuple-element.47.direct), custom_call_target="tpu_custom_call" | custom-call | tf_op jit(solution)/shard_map/finish_kernel/pallas_call | solution.py:580
  (14 shorter events, 0.6 us)
Async XLA Ops:
  0.6 24.2 %copy-start = (bf16[2,256,256]{2,1,0:T(8,128)(2,1)S(1)}, bf16[2,256,256]{2,1,0:T(8,128)(2,1)}, u32[]{:S(2)}) copy-start(bf16[2,256,256]{2,1,0:T(8,128)(2,1)} %refs_2_.3) | copy-start | bytes 786436
  11.5 10.5 %all-to-all-start = ((bf16[4,64,560]{2,1,0:T(8,128)(2,1)}), bf16[4,64,560]{2,1,0:T(8,128)(2,1)S(1)}, u32[]{:S(2)}, u32[]{:S(2)}) async-start(bf16[4,64,560]{2,1,0:T(8,128)(2,1)} %pair_kernel.2), calls=%async_computation | async-start | bytes 655360 | tf_op jit(solution)/shard_map/all_to_all | solution.py:466
  14.9 0.8 copy-start.2
  15.8 0.7 copy-start.3
  16.5 0.7 copy-start.4
  17.2 0.7 copy-start.5
  58.2 5.3 %collective-permute-start = (f32[2,16,256]{2,1,0:T(8,128)S(1)}, f32[2,16,256]{2,1,0:T(8,128)S(1)}, u32[]{:S(2)}, u32[]{:S(2)}) collective-permute-start(f32[2,16,256]{2,1,0:T(8,128)S(1)} %get-tuple-element.44), channel_id=1, source_target_pairs={{0,8},{8,0},{16,24},{24,16},{32,40},{40,32},{48,56},{56,48},{64,72... | collective-permute-start | bytes 98312 | tf_op jit(solution)/shard_map/ppermute | solution.py:540
  65.4 20.6 %copy-start.1 = (bf16[256,560]{0,1:T(8,128)(2,1)S(1)}, bf16[256,560]{0,1:T(8,128)(2,1)}, u32[]{:S(2)}) copy-start(bf16[256,560]{0,1:T(8,128)(2,1)} %param.9) | copy-start | bytes 860164
  72.7 10.5 %all-to-all-start.3 = ((bf16[4,64,560]{2,1,0:T(8,128)(2,1)}), bf16[4,64,560]{2,1,0:T(8,128)(2,1)S(1)}, u32[]{:S(2)}, u32[]{:S(2)}) async-start(bf16[4,64,560]{2,1,0:T(8,128)(2,1)} %pair_kernel.3), calls=%async_computation.3 | async-start | bytes 655360 | tf_op jit(solution)/shard_map/all_to_all | solution.py:466

commit v8 on v7

--- a/solution.py
+++ b/solution.py
@@ -148,7 +148,7 @@
                     result.append(fade * states[n * blocks + block] + w[block] * gate)
             return (tuple(result), tuple(t + x for t, x in zip(total, d)))
 
-        states, total = lax.fori_loop(0, steps, walk_states, (many, (zero,) * blocks))
+        states, total = lax.fori_loop(0, steps, walk_states, (many, (zero,) * blocks), unroll=4)
 
         def walk_adjoints(index, carried):
             step = index if falling else steps - 1 - index
@@ -161,7 +161,7 @@
                     result.append(fade * (g[block] * gate + carried[n * blocks + block]))
             return tuple(result)
 
-        carried = lax.fori_loop(0, steps, walk_adjoints, many)
+        carried = lax.fori_loop(0, steps, walk_adjoints, many, unroll=4)
         for block in range(blocks):
             lanes = lane_block(block)
 
@@ -319,15 +319,14 @@
 
     def put_products(which, step, rows_of):
         start = pl.multiple_of(step * depth * GROUPS, 2 * GROUPS)
-        for block in range(blocks):
-            stacked = jnp.concatenate(rows_of[block], 0).astype(BF16)
-            products[which, pl.ds(start, depth * GROUPS), lane_block(block)] = stacked
+        stacked = jnp.concatenate(rows_of, 0).astype(BF16)
+        products[pl.ds(start, depth * GROUPS), lane_block(which)] = stacked
 
     def walk_states(index, states):
         step = index + way * (steps - 1 - 2 * index)
         w, g = pieces(weight, step), pieces(cot, step)
         total = pieces(core, step)
-        rows_of = [[] for _ in range(blocks)]
+        rows_of = []
         result = []
         for n in range(depth):
             gate_in = gate_at(spread.at[way], step, n)
@@ -338,19 +337,20 @@
                 kept[step, n, :, lanes] = faded
                 state = faded + w[block] * gate_in
                 total[block] = total[block] + gate_out * state
-                rows_of[block].append(g[block] * state)
+                product = g[block] * state if block == 0 else product + g[block] * state
                 result.append(state)
+            rows_of.append(product)
         for block in range(blocks):
             core[at(step), lane_block(block)] = total[block]
         put_products(1, step, rows_of)
         return tuple(result)
 
-    lax.fori_loop(0, steps, walk_states, entering(0))
+    lax.fori_loop(0, steps, walk_states, entering(0), unroll=4)
 
     def walk_adjoints(index, carried):
         step = steps - 1 - index + way * (2 * index - steps + 1)
         w, g = pieces(weight, step), pieces(cot, step)
-        rows_of = [[] for _ in range(blocks)]
+        rows_of = []
         through = [jnp.zeros((GROUPS, LANES), F32)] * blocks
         fading = [jnp.zeros((GROUPS, LANES), F32)] * blocks
         result = []
@@ -365,7 +365,8 @@
                 fading[block] = fading[block] + (
                     adjoint * kept[step, n, :, lanes] * rates[way, n, :, lanes]
                 )
-                rows_of[block].append(adjoint * w[block])
+                product = adjoint * w[block] if block == 0 else product + adjoint * w[block]
+            rows_of.append(product)
         put_products(0, step, rows_of)
         for block in range(blocks):
             lanes = lane_block(block)
@@ -376,24 +377,27 @@
             grad_pre[at(step), lanes] = grad_delta * slope[way, at(step), lanes]
         return tuple(result)
 
-    lax.fori_loop(0, steps, walk_adjoints, entering(1))
+    lax.fori_loop(0, steps, walk_adjoints, entering(1), unroll=4)
     low[...] = dot(grad_pre[...].astype(BF16), w_delta[way], NT)
-    ones = jnp.ones((width, LANES), BF16)
+    row = lax.broadcasted_iota(jnp.int32, (2 * LANES, 2 * LANES), 0)
+    column = lax.broadcasted_iota(jnp.int32, (2 * LANES, 2 * LANES), 1)
+    halves = jnp.where(row // LANES == column // LANES, 1.0, 0.0).astype(BF16)
     lane = lax.broadcasted_iota(jnp.int32, (GROUPS, LANES), 1) - first
     height = depth * GROUPS
     for start in range(0, steps, 4):
-        merged = [
-            gate_grad[(start + step) * GROUPS : (start + step + 1) * GROUPS] for step in range(4)
-        ]
-        for which in range(2):
-            sums = dot(products[which, start * height : (start + 4) * height], ones)
-            for step in range(4):
+        sums = dot(products[start * height : (start + 4) * height, :], halves)
+        for step in range(4):
+            spot = slice((start + step) * GROUPS, (start + step + 1) * GROUPS)
+            merged = gate_grad[spot]
+            for which in range(2):
                 for n in range(depth):
-                    row = step * height + n * GROUPS
-                    merged[step] = jnp.where(
-                        lane == which * depth + n, sums[row : row + GROUPS], merged[step]
+                    top = step * height + n * GROUPS
+                    merged = jnp.where(
+                        lane == which * depth + n,
+                        sums[top : top + GROUPS, lane_block(which)],
+                        merged,
                     )
-        gate_grad[start * GROUPS : (start + 4) * GROUPS] = jnp.concatenate(merged, 0)
+            gate_grad[spot] = merged
 
 
 def own_gradient_kernel(skip_gain, *refs):
@@ -420,14 +424,10 @@
     parts_out[:, 2 * rank :] = gate_grad[:, :gates]
 
 
-def layer_kernel(core, layer_out):
-    ungroup = grouping(core.shape[0], inverse=True)
+def finish_kernel(grad_proj, w_proj, direct, core, layer_out, signal_grad):
+    ungroup = grouping(direct.shape[0], inverse=True)
     layer_out[...] = dot(ungroup, core[...].astype(BF16)).astype(BF16)
-
-
-def finish_kernel(grad_proj, w_proj, direct, signal_grad):
     total = dot(grad_proj[...], w_proj[...]) + direct[...]
-    ungroup = grouping(direct.shape[0], inverse=True)
     signal_grad[...] = dot(ungroup, total.astype(BF16)).astype(BF16)
 
 
@@ -555,7 +555,7 @@
         ((rows, width), F32),
         ((rows, width), F32),
         stack,
-        ((2, rows * depth, width), BF16),
+        ((rows * depth, 2 * LANES), BF16),
     )
     own = kernel(
         own_gradient_kernel,
@@ -575,10 +575,10 @@
         10,
         (((rows, rank), F32), ((rows, LANES), F32)) + scratch,
     )(*own, *inputs, swapped)
-    layer_out = kernel(layer_kernel, shape(rows, width, dtype=BF16), 4, cost=1 << 20)(core)
     grad_proj = sum_over_chan(grad_parts)
-    signal_grad = kernel(finish_kernel, shape(rows, width, dtype=BF16), 8)(
-        grad_proj, w_turned, direct
+    result = shape(rows, width, dtype=BF16)
+    layer_out, signal_grad = kernel(finish_kernel, (result, result), 8)(
+        grad_proj, w_turned, direct, core
     )
     return (layer_out, signal_grad)
 

time: 87.6 us -> 84.8 us (0.968)
  blocking collectives: 51.2 us -> 61.2 us
  waiting for transfers between devices: 10.2 us -> 3.95 us
  starting transfers between devices: 9.1 us -> 5.65 us
  Pallas kernels: 12.8 us -> 9.86 us
    all_to_all x0 -> x1, blocking collectives: none -> 9.18 us  [sum_over_chan(): lax.all_to_all(copies, 'chan', 0, 0, tiled=True, axis_index_groups=across)]
    all_to_all x2 -> x1, waiting for transfers between devices: 10.2 us -> 3.95 us  [sum_over_chan(): lax.all_to_all(copies, 'chan', 0, 0, tiled=True, axis_index_groups=across)]
    all_to_all x2 -> x1, starting transfers between devices: 6.91 us -> 3.45 us  [sum_over_chan(): lax.all_to_all(copies, 'chan', 0, 0, tiled=True, axis_index_groups=across)]
    pallas_call x2 -> x1, Pallas kernels: 1.79 us -> 1.02 us  [local(): kernel(finish_kernel, (result, result), 8)]
  transfers between devices with their start and end apart: 3 -> 2, of which waited for: 2 -> 1; matrix products, arithmetic and copies ran while one was open for 0% -> 0% of each run, Pallas kernels for 5% -> 3%
where the time goes in v8:
time: 84.8 us; the launch traced here: 84.3 us
  blocking collectives  61.2 us (72%)
  Pallas kernels  9.86 us (12%)
  starting transfers between devices  5.65 us (7%)
  waiting for transfers between devices  3.95 us (5%)
  local copies, waits for them, and re-layouts  2.94 us (3%)
    all_to_all x2, blocking collectives, exchange(): lax.all_to_all(array, 'seq', 0, 0, tiled=True, axis_index_groups=groups)  30.4 us
    all_gather x2, blocking collectives, sum_over_chan(): lax.all_gather(part, 'chan', axis=0, tiled=True, axis_index_groups=pairs)  15.7 us
    all_to_all x1, blocking collectives, sum_over_chan(): lax.all_to_all(copies, 'chan', 0, 0, tiled=True, axis_index_groups=across)  9.18 us
    all_gather x2, blocking collectives, sum_over_chan(): lax.all_gather(half, 'chan', axis=0, tiled=True, axis_index_groups=pairs)  5.88 us
    all_to_all x1, waiting for transfers between devices, sum_over_chan(): lax.all_to_all(copies, 'chan', 0, 0, tiled=True, axis_index_groups=across)  3.95 us
    all_to_all x1, starting transfers between devices, sum_over_chan(): lax.all_to_all(copies, 'chan', 0, 0, tiled=True, axis_index_groups=across)  3.45 us
    unnamed x12, local copies, waits for them, and re-layouts  2.94 us
    ppermute x1, starting transfers between devices, local(): lax.ppermute(others, 'seq', [(shard, shard ^ 1) for shard in range(shards)])  2.19 us
  transfers between devices with their start and end apart: 2, of which 1 were waited for; matrix products, arithmetic and copies ran while one was open for 0% of the time, Pallas kernels for 3%

profile of v8, /device:TPU:1, one launch (start us, length us, event | category | flops | bytes accessed | tf_op | source)
XLA Modules:
  0.0 84.3 jit_solution(6748014663472398707)
XLA Ops:
  0.6 1.3 %project_kernel.1 = (f32[128,256]{1,0:T(8,128)S(1)}, f32[128,560]{1,0:T(8,128)S(1)}) custom-call(bf16[128,256]{1,0:T(8,128)(2,1)} %signal.1, bf16[560,256]{1,0:T(8,128)(2,1)} %bitcast.3), custom_call_target="tpu_custom_call" | custom-call | tf_op jit(solution)/shard_map/project_kernel/pallas_call | solution.py:487
  2.0 8.7 %all_gather.12.both = f32[256,560]{1,0:T(8,128)S(1)} all-gather(f32[128,560]{1,0:T(8,128)S(1)} %get-tuple-element.26), channel_id=1, replica_groups={{0,1},{2,3},{4,5},{6,7},{8,9},{10,11},{12,13},{14,15},{16,17},{18,19},{..., dimensions={0}, use_global_device_ids=true | all-gather | bytes 860160 | tf_op jit(solution)/shard_map/all_gather | solution.py:460
  10.7 0.7 pair_kernel.2
  11.5 3.5 %all-to-all-start = ((bf16[4,64,560]{2,1,0:T(8,128)(2,1)}), bf16[4,64,560]{2,1,0:T(8,128)(2,1)S(1)}, u32[]{:S(2)}, u32[]{:S(2)}) async-start(bf16[4,64,560]{2,1,0:T(8,128)(2,1)} %pair_kernel.2), calls=%async_computation | async-start | bytes 655360 | tf_op jit(solution)/shard_map/all_to_all | solution.py:466
  14.9 0.8 copy-done.2
  15.8 0.7 copy-done.3
  16.5 0.7 copy-done.4
  17.2 0.7 copy-done.5
  17.9 0.2 prepare_kernel.1
  18.0 3.9 %all-to-all-done.parts = bf16[4,64,560]{2,1,0:T(8,128)(2,1)S(1)} async-done(((bf16[4,64,560]{2,1,0:T(8,128)(2,1)}), bf16[4,64,560]{2,1,0:T(8,128)(2,1)S(1)}, u32[]{:S(2)}, u32[]{:S(2)}) %all-to-all-start) | async-done | bytes 286752 | tf_op jit(solution)/shard_map/all_to_all | solution.py:466
  22.0 2.8 %all_gather.13.projected = bf16[128,560]{1,0:T(8,128)(2,1)S(1)} all-gather(bf16[64,560]{1,0:T(8,128)(2,1)S(1)} %chips_kernel.2), channel_id=1, replica_groups={{0,1},{2,3},{4,5},{6,7},{8,9},{10,11},{12,13},{14,15},{16,17},{18,19},{..., dimensions={0}, use_global_device_ids=true | all-gather | bytes 215040 | tf_op jit(solution)/shard_map/all_gather | solution.py:468
  24.8 2.1 %summary_kernel.1 = (f32[2,128,256]{2,1,0:T(8,128)S(1)}, f32[2,128,256]{2,1,0:T(8,128)S(1)}, f32[4,12,8,256]{3,2,1,0:T(8,128)S(1)}, f32[4,8,256]{2,1,0:T(8,128)S(1)}, bf16[4,2,16,256]{3,2,1,0:T(8,128)(2,1)S(1)}) custom-call(bf16[128,560]{1,0:T(8,128)(2,1)S(1)} %all_gather.13.projected, bf16[2,256,256]{2,1,0:T(8,128)(2,1)S(1)} %copy-done, ...), custom_call_target="tpu_custom_call" | custom-call | tf_op jit(solution)/shard_map/summary_kernel/pallas_call | solution.py:510
  26.9 6.8 %all_to_all.20.parts = bf16[4,2,16,256]{3,2,1,0:T(8,128)(2,1)S(1)} all-to-all(bf16[4,2,16,256]{3,2,1,0:T(8,128)(2,1)S(1)} %get-tuple-element.37), channel_id=1, replica_groups={{0,8,16,24},{32,40,48,56},{64,72,80,88},{96,104,112,120},{128,136,144,1..., dimensions={0} | all-to-all | bytes 131072 | tf_op jit(solution)/shard_map/all_to_all | solution.py:485
  33.8 0.2 row_kernel.1
  33.9 23.5 %all_to_all.21.rows = bf16[16,16,256]{2,1,0:T(8,128)(2,1)S(1)} all-to-all(bf16[16,16,256]{2,1,0:T(8,128)(2,1)S(1)} %row_kernel.1), channel_id=1, replica_groups={{0,32,64,96,128,160,192,224,256,288,320,352,384,416,448,480},{8,40,72,1..., dimensions={0} | all-to-all | bytes 262144 | tf_op jit(solution)/shard_map/all_to_all | solution.py:485
  57.5 0.2 entry_kernel.1
  57.7 2.2 %collective-permute-start = (f32[2,16,256]{2,1,0:T(8,128)S(1)}, f32[2,16,256]{2,1,0:T(8,128)S(1)}, u32[]{:S(2)}, u32[]{:S(2)}) collective-permute-start(f32[2,16,256]{2,1,0:T(8,128)S(1)} %get-tuple-element.44), channel_id=1, source_target_pairs={{0,8},{8,0},{16,24},{24,16},{32,40},{40,32},{48,56},{56,48},{64,72... | collective-permute-start | bytes 98312 | tf_op jit(solution)/shard_map/ppermute | solution.py:540
  59.9 1.1 %early_kernel.1 = (f32[2,128,3072]{2,1,0:T(8,128)S(1)}, f32[2,16,12,8,256]{4,3,2,1,0:T(8,128)S(1)}) custom-call(bf16[128,560]{1,0:T(8,128)(2,1)S(1)} %all_gather.13.projected, f32[2,12,8,256]{3,2,1,0:T(8,128)S(1)} %get-tuple-element.27.rates.refs_3_, f32[2,128,256]{2,1,0:T(8,128)S(1)} %get-tuple-element.31.delta.refs_6_), custom_call_target="tpu_custom_call" | custom-call | flops 4194304 | bytes 4194304 | tf_op jit(solution)/shard_map/early_kernel/pallas_call | solution.py:524
  61.0 1.5 %own_gradient_kernel.1 = (f32[128,256]{1,0:T(8,128)S(1)}, f32[128,256]{1,0:T(8,128)S(1)}, f32[128,256]{1,0:T(8,128)S(1)}, f32[128,128]{1,0:T(8,128)S(1)}) custom-call(f32[1,256]{1,0:T(1,128)S(1)} %get-tuple-element.25.skip_gain, f32[2,128,3072]{2,1,0:T(8,128)S(1)} %get-tuple-element.32.refs_0_, f32[2,16,12,8,256]{4,3,2,1,0:T(8,128)S(1)} %get-tuple-element.33.refs_1_, ...), custom_call_target="tpu_custom_call" | custom-call | flops 4194304 | bytes 4194304 | tf_op jit(solution)/shard_map/own_gradient_kernel/pallas_call | solution.py:560
  62.5 1.5 %other_gradient_kernel.1 = (f32[128,256]{1,0:T(8,128)S(1)}, f32[128,560]{1,0:T(8,128)S(1)}, f32[128,256]{1,0:T(8,128)S(1)}) custom-call(f32[128,256]{1,0:T(8,128)S(1)} %get-tuple-element.40.own_core, f32[128,256]{1,0:T(8,128)S(1)} %get-tuple-element.41.own_direct, f32[128,256]{1,0:T(8,128)S(1)} %get-tuple-element.42.own_low, ...), custom_call_target="tpu_custom_call" | custom-call | tf_op jit(solution)/shard_map/other_gradient_kernel/pallas_call | solution.py:572
  64.0 7.0 %all_gather.14.both = f32[256,560]{1,0:T(8,128)S(1)} all-gather(f32[128,560]{1,0:T(8,128)S(1)} %get-tuple-element.45), channel_id=1, replica_groups={{0,1},{2,3},{4,5},{6,7},{8,9},{10,11},{12,13},{14,15},{16,17},{18,19},{..., dimensions={0}, use_global_device_ids=true | all-gather | bytes 860160 | tf_op jit(solution)/shard_map/all_gather | solution.py:460
  71.0 9.2 %all_to_all.22.parts = bf16[4,64,560]{2,1,0:T(8,128)(2,1)S(1)} all-to-all(bf16[4,64,560]{2,1,0:T(8,128)(2,1)S(1)} %pair_kernel.3), channel_id=1, replica_groups={{0,2,4,6},{1,3,5,7},{8,10,12,14},{9,11,13,15},{16,18,20,22},{17,19,21,2..., dimensions={0} | all-to-all | bytes 573440 | tf_op jit(solution)/shard_map/all_to_all | solution.py:466
  80.2 3.1 %all_gather.15.grad_proj = bf16[128,560]{1,0:T(8,128)(2,1)S(1)} all-gather(bf16[64,560]{1,0:T(8,128)(2,1)S(1)} %chips_kernel.3), channel_id=1, replica_groups={{0,1},{2,3},{4,5},{6,7},{8,9},{10,11},{12,13},{14,15},{16,17},{18,19},{..., dimensions={0}, use_global_device_ids=true | all-gather | bytes 215040 | tf_op jit(solution)/shard_map/all_gather | solution.py:468
  83.3 1.0 %finish_kernel.1 = (bf16[128,256]{1,0:T(8,128)(2,1)}, bf16[128,256]{1,0:T(8,128)(2,1)}) custom-call(bf16[128,560]{1,0:T(8,128)(2,1)S(1)} %all_gather.15.grad_proj, bf16[560,256]{1,0:T(8,128)(2,1)S(1)} %bitcast.4, f32[128,256]{1,0:T(8,128)S(1)} %get-tuple-element.46.direct, f32[128,256]{1,0:T(8,128)S(1)} %get-tuple-element.47.core), custom_call_target="tpu_custom_call" | custom-call | tf_op jit(solution)/shard_map/finish_kernel/pallas_call | solution.py:580
  (12 shorter events, 0.1 us)
Async XLA Ops:
  0.6 24.2 %copy-start = (bf16[2,256,256]{2,1,0:T(8,128)(2,1)S(1)}, bf16[2,256,256]{2,1,0:T(8,128)(2,1)}, u32[]{:S(2)}) copy-start(bf16[2,256,256]{2,1,0:T(8,128)(2,1)} %refs_2_.3) | copy-start | bytes 786436
  11.5 10.5 %all-to-all-start = ((bf16[4,64,560]{2,1,0:T(8,128)(2,1)}), bf16[4,64,560]{2,1,0:T(8,128)(2,1)S(1)}, u32[]{:S(2)}, u32[]{:S(2)}) async-start(bf16[4,64,560]{2,1,0:T(8,128)(2,1)} %pair_kernel.2), calls=%async_computation | async-start | bytes 655360 | tf_op jit(solution)/shard_map/all_to_all | solution.py:466
  14.9 0.8 copy-start.2
  15.8 0.7 copy-start.3
  16.5 0.7 copy-start.4
  17.2 0.7 copy-start.5
  57.7 4.8 %collective-permute-start = (f32[2,16,256]{2,1,0:T(8,128)S(1)}, f32[2,16,256]{2,1,0:T(8,128)S(1)}, u32[]{:S(2)}, u32[]{:S(2)}) collective-permute-start(f32[2,16,256]{2,1,0:T(8,128)S(1)} %get-tuple-element.44), channel_id=1, source_target_pairs={{0,8},{8,0},{16,24},{24,16},{32,40},{40,32},{48,56},{56,48},{64,72... | collective-permute-start | bytes 98312 | tf_op jit(solution)/shard_map/ppermute | solution.py:540
  63.9 19.3 %copy-start.1 = (bf16[256,560]{0,1:T(8,128)(2,1)S(1)}, bf16[256,560]{0,1:T(8,128)(2,1)}, u32[]{:S(2)}) copy-start(bf16[256,560]{0,1:T(8,128)(2,1)} %param.9) | copy-start | bytes 860164

commit v9 on v8

--- a/solution.py
+++ b/solution.py
@@ -107,7 +107,7 @@
     signal,
     cot,
     delta_out,
-    slope_out,
+    pre_out,
     local_out,
     ahead_out,
     payload,
@@ -128,7 +128,7 @@
         pre = dot(projected[:, way * rank : (way + 1) * rank], w_delta[way]) + bias[way : way + 1]
         delta = jnp.maximum(pre, 0.0) + jnp.log1p(jnp.exp(-jnp.abs(pre)))
         delta_out[way] = delta
-        slope_out[way] = 1.0 / (1.0 + jnp.exp(-pre))
+        pre_out[way] = pre
         weight[...] = delta * signal[...]
         falling = way == 1
         zero = jnp.zeros((GROUPS, LANES), F32)
@@ -256,10 +256,12 @@
             every[shard] = state
             state = pass_by(state, parts[shard, kind].astype(F32), rates)
         mine[kind] = every[here]
-        other[kind] = every[here + 1 - 2 * way]
-
-
-def early_kernel(projected, rates, delta, spread, fades):
+        other[kind] = every[here + 1 - 2 * way].astype(BF16)
+
+
+def early_kernel(projected, rates, delta, pre, spread, fades, slope):
+    for way in range(2):
+        slope[way] = 1.0 / (1.0 + jnp.exp(-pre[way]))
     _, steps, depth, _, _ = fades.shape
     rank = (projected.shape[1] - 4 * depth) // 2
     for way in range(2):
@@ -305,11 +307,12 @@
     weight[...] = delta[way] * signal[...]
 
     def entering(kind):
+        arrived = entries[kind].astype(F32)
         gap = [ahead[2 * way + kind, :, lane_block(block)] for block in range(blocks)]
         return tuple(
             local[2 * way + kind, n, :, lane_block(block)]
             + jnp.exp2(gap[block] * rates[way, n, :, lane_block(block)])
-            * entries[kind, n : n + 1, lane_block(block)]
+            * arrived[n : n + 1, lane_block(block)]
             for n in range(depth)
             for block in range(blocks)
         )
@@ -507,7 +510,7 @@
     projected = sum_over_chan(part)
     wide = ((rows, 4 * depth * LANES), F32)
     stack = ((steps, depth, GROUPS, width), F32)
-    delta, slope, local_states, ahead, payload = kernel(
+    delta, pre, local_states, ahead, payload = kernel(
         summary_kernel,
         (
             shape(2, rows, width),
@@ -521,19 +524,20 @@
     )(projected, w_delta, bias, rates, signal_wide, cot_wide)
     parts = exchange(payload, along_y)
     copies = kernel(row_kernel, shape(shards // 4, slots, width, dtype=BF16), 4)(parts, flat)
-    spread, fades = kernel(
+    spread, fades, slope = kernel(
         early_kernel,
         (
             shape(2, rows, 2 * depth * LANES),
             shape(2, steps, depth, GROUPS, width),
+            shape(2, rows, width),
         ),
         8,
         cost=1 << 22,
-    )(projected, rates, delta)
+    )(projected, rates, delta, pre)
     row_totals = exchange(copies, along_z)
     entries, others = kernel(
         entry_kernel,
-        (shape(2, slots, width), shape(2, slots, width)),
+        (shape(2, slots, width), shape(2, slots, width, dtype=BF16)),
         4,
         (((4, slots, width), F32),),
     )(row_totals, parts, flat)

time: 84.8 us -> 84.6 us (level)
  no operation moved by 1% of the time
where the time goes in v9:
time: 84.6 us; the launch traced here: 84.1 us
  blocking collectives  61 us (72%)
  Pallas kernels  9.84 us (12%)
  starting transfers between devices  5.65 us (7%)
  waiting for transfers between devices  3.95 us (5%)
  local copies, waits for them, and re-layouts  2.94 us (3%)
    all_to_all x2, blocking collectives, exchange(): lax.all_to_all(array, 'seq', 0, 0, tiled=True, axis_index_groups=groups)  30.4 us
    all_gather x2, blocking collectives, sum_over_chan(): lax.all_gather(part, 'chan', axis=0, tiled=True, axis_index_groups=pairs)  15.5 us
    all_to_all x1, blocking collectives, sum_over_chan(): lax.all_to_all(copies, 'chan', 0, 0, tiled=True, axis_index_groups=across)  9.18 us
    all_gather x2, blocking collectives, sum_over_chan(): lax.all_gather(half, 'chan', axis=0, tiled=True, axis_index_groups=pairs)  5.88 us
    all_to_all x1, waiting for transfers between devices, sum_over_chan(): lax.all_to_all(copies, 'chan', 0, 0, tiled=True, axis_index_groups=across)  3.95 us
    all_to_all x1, starting transfers between devices, sum_over_chan(): lax.all_to_all(copies, 'chan', 0, 0, tiled=True, axis_index_groups=across)  3.45 us
    unnamed x12, local copies, waits for them, and re-layouts  2.94 us
    ppermute x1, starting transfers between devices, local(): lax.ppermute(others, 'seq', [(shard, shard ^ 1) for shard in range(shards)])  2.19 us
  transfers between devices with their start and end apart: 2, of which 1 were waited for; matrix products, arithmetic and copies ran while one was open for 0% of the time, Pallas kernels for 3%

profile of v9, /device:TPU:1, one launch (start us, length us, event | category | flops | bytes accessed | tf_op | source)
XLA Modules:
  0.0 84.1 jit_solution(1286409383409628505)
XLA Ops:
  0.6 1.3 %project_kernel.1 = (f32[128,256]{1,0:T(8,128)S(1)}, f32[128,560]{1,0:T(8,128)S(1)}) custom-call(bf16[128,256]{1,0:T(8,128)(2,1)} %signal.1, bf16[560,256]{1,0:T(8,128)(2,1)} %bitcast.3), custom_call_target="tpu_custom_call" | custom-call | tf_op jit(solution)/shard_map/project_kernel/pallas_call | solution.py:490
  2.0 8.7 %all_gather.12.both = f32[256,560]{1,0:T(8,128)S(1)} all-gather(f32[128,560]{1,0:T(8,128)S(1)} %get-tuple-element.27), channel_id=1, replica_groups={{0,1},{2,3},{4,5},{6,7},{8,9},{10,11},{12,13},{14,15},{16,17},{18,19},{..., dimensions={0}, use_global_device_ids=true | all-gather | bytes 860160 | tf_op jit(solution)/shard_map/all_gather | solution.py:463
  10.7 0.7 pair_kernel.2
  11.5 3.5 %all-to-all-start = ((bf16[4,64,560]{2,1,0:T(8,128)(2,1)}), bf16[4,64,560]{2,1,0:T(8,128)(2,1)S(1)}, u32[]{:S(2)}, u32[]{:S(2)}) async-start(bf16[4,64,560]{2,1,0:T(8,128)(2,1)} %pair_kernel.2), calls=%async_computation | async-start | bytes 655360 | tf_op jit(solution)/shard_map/all_to_all | solution.py:469
  14.9 0.8 copy-done.2
  15.8 0.7 copy-done.3
  16.5 0.7 copy-done.4
  17.2 0.7 copy-done.5
  17.9 0.2 prepare_kernel.1
  18.0 3.9 %all-to-all-done.parts = bf16[4,64,560]{2,1,0:T(8,128)(2,1)S(1)} async-done(((bf16[4,64,560]{2,1,0:T(8,128)(2,1)}), bf16[4,64,560]{2,1,0:T(8,128)(2,1)S(1)}, u32[]{:S(2)}, u32[]{:S(2)}) %all-to-all-start) | async-done | bytes 286752 | tf_op jit(solution)/shard_map/all_to_all | solution.py:469
  22.0 2.8 %all_gather.13.projected = bf16[128,560]{1,0:T(8,128)(2,1)S(1)} all-gather(bf16[64,560]{1,0:T(8,128)(2,1)S(1)} %chips_kernel.2), channel_id=1, replica_groups={{0,1},{2,3},{4,5},{6,7},{8,9},{10,11},{12,13},{14,15},{16,17},{18,19},{..., dimensions={0}, use_global_device_ids=true | all-gather | bytes 215040 | tf_op jit(solution)/shard_map/all_gather | solution.py:471
  24.8 2.1 %summary_kernel.1 = (f32[2,128,256]{2,1,0:T(8,128)S(1)}, f32[2,128,256]{2,1,0:T(8,128)S(1)}, f32[4,12,8,256]{3,2,1,0:T(8,128)S(1)}, f32[4,8,256]{2,1,0:T(8,128)S(1)}, bf16[4,2,16,256]{3,2,1,0:T(8,128)(2,1)S(1)}) custom-call(bf16[128,560]{1,0:T(8,128)(2,1)S(1)} %all_gather.13.projected, bf16[2,256,256]{2,1,0:T(8,128)(2,1)S(1)} %copy-done, ...), custom_call_target="tpu_custom_call" | custom-call | tf_op jit(solution)/shard_map/summary_kernel/pallas_call | solution.py:513
  26.9 6.8 %all_to_all.20.parts = bf16[4,2,16,256]{3,2,1,0:T(8,128)(2,1)S(1)} all-to-all(bf16[4,2,16,256]{3,2,1,0:T(8,128)(2,1)S(1)} %get-tuple-element.39), channel_id=1, replica_groups={{0,8,16,24},{32,40,48,56},{64,72,80,88},{96,104,112,120},{128,136,144,1..., dimensions={0} | all-to-all | bytes 131072 | tf_op jit(solution)/shard_map/all_to_all | solution.py:488
  33.7 0.2 row_kernel.1
  33.9 23.5 %all_to_all.21.rows = bf16[16,16,256]{2,1,0:T(8,128)(2,1)S(1)} all-to-all(bf16[16,16,256]{2,1,0:T(8,128)(2,1)S(1)} %row_kernel.1), channel_id=1, replica_groups={{0,32,64,96,128,160,192,224,256,288,320,352,384,416,448,480},{8,40,72,1..., dimensions={0} | all-to-all | bytes 262144 | tf_op jit(solution)/shard_map/all_to_all | solution.py:488
  57.4 0.2 entry_kernel.1
  57.6 2.2 %collective-permute-start = (bf16[2,16,256]{2,1,0:T(8,128)(2,1)S(1)}, bf16[2,16,256]{2,1,0:T(8,128)(2,1)S(1)}, u32[]{:S(2)}, u32[]{:S(2)}) collective-permute-start(bf16[2,16,256]{2,1,0:T(8,128)(2,1)S(1)} %get-tuple-element.46), channel_id=1, source_target_pairs={{0,8},{8,0},{16,24},{24,16},{32,40},{40,32},{48,56},{56,48},{64,72... | collective-permute-start | bytes 49160 | tf_op jit(solution)/shard_map/ppermute | solution.py:544
  59.8 1.1 %early_kernel.1 = (f32[2,128,3072]{2,1,0:T(8,128)S(1)}, f32[2,16,12,8,256]{4,3,2,1,0:T(8,128)S(1)}, f32[2,128,256]{2,1,0:T(8,128)S(1)}) custom-call(bf16[128,560]{1,0:T(8,128)(2,1)S(1)} %all_gather.13.projected, f32[2,12,8,256]{3,2,1,0:T(8,128)S(1)} %get-tuple-element.28.rates.refs_3_, f32[2,128,256]{2,1,0:T(8,128)S(1)} %get-tuple-element.32.delta.refs_6_, ...), custom_call_target="tpu_custom_call" | custom-call | flops 4194304 | bytes 4194304 | tf_op jit(solution)/shard_map/early_kernel/pallas_call | solution.py:527
  61.0 1.5 %own_gradient_kernel.1 = (f32[128,256]{1,0:T(8,128)S(1)}, f32[128,256]{1,0:T(8,128)S(1)}, f32[128,256]{1,0:T(8,128)S(1)}, f32[128,128]{1,0:T(8,128)S(1)}) custom-call(f32[1,256]{1,0:T(1,128)S(1)} %get-tuple-element.26.skip_gain, f32[2,128,3072]{2,1,0:T(8,128)S(1)} %get-tuple-element.34.refs_0_, f32[2,16,12,8,256]{4,3,2,1,0:T(8,128)S(1)} %get-tuple-element.35.refs_1_, ...), custom_call_target="tpu_custom_call" | custom-call | flops 4194304 | bytes 4194304 | tf_op jit(solution)/shard_map/own_gradient_kernel/pallas_call | solution.py:564
  62.4 1.5 %other_gradient_kernel.1 = (f32[128,256]{1,0:T(8,128)S(1)}, f32[128,560]{1,0:T(8,128)S(1)}, f32[128,256]{1,0:T(8,128)S(1)}) custom-call(f32[128,256]{1,0:T(8,128)S(1)} %get-tuple-element.42.own_core, f32[128,256]{1,0:T(8,128)S(1)} %get-tuple-element.43.own_direct, f32[128,256]{1,0:T(8,128)S(1)} %get-tuple-element.44.own_low, ...), custom_call_target="tpu_custom_call" | custom-call | tf_op jit(solution)/shard_map/other_gradient_kernel/pallas_call | solution.py:576
  63.9 6.8 %all_gather.14.both = f32[256,560]{1,0:T(8,128)S(1)} all-gather(f32[128,560]{1,0:T(8,128)S(1)} %get-tuple-element.47), channel_id=1, replica_groups={{0,1},{2,3},{4,5},{6,7},{8,9},{10,11},{12,13},{14,15},{16,17},{18,19},{..., dimensions={0}, use_global_device_ids=true | all-gather | bytes 860160 | tf_op jit(solution)/shard_map/all_gather | solution.py:463
  70.7 9.2 %all_to_all.22.parts = bf16[4,64,560]{2,1,0:T(8,128)(2,1)S(1)} all-to-all(bf16[4,64,560]{2,1,0:T(8,128)(2,1)S(1)} %pair_kernel.3), channel_id=1, replica_groups={{0,2,4,6},{1,3,5,7},{8,10,12,14},{9,11,13,15},{16,18,20,22},{17,19,21,2..., dimensions={0} | all-to-all | bytes 573440 | tf_op jit(solution)/shard_map/all_to_all | solution.py:469
  80.0 3.1 %all_gather.15.grad_proj = bf16[128,560]{1,0:T(8,128)(2,1)S(1)} all-gather(bf16[64,560]{1,0:T(8,128)(2,1)S(1)} %chips_kernel.3), channel_id=1, replica_groups={{0,1},{2,3},{4,5},{6,7},{8,9},{10,11},{12,13},{14,15},{16,17},{18,19},{..., dimensions={0}, use_global_device_ids=true | all-gather | bytes 215040 | tf_op jit(solution)/shard_map/all_gather | solution.py:471
  83.1 1.0 %finish_kernel.1 = (bf16[128,256]{1,0:T(8,128)(2,1)}, bf16[128,256]{1,0:T(8,128)(2,1)}) custom-call(bf16[128,560]{1,0:T(8,128)(2,1)S(1)} %all_gather.15.grad_proj, bf16[560,256]{1,0:T(8,128)(2,1)S(1)} %bitcast.4, f32[128,256]{1,0:T(8,128)S(1)} %get-tuple-element.48.direct, f32[128,256]{1,0:T(8,128)S(1)} %get-tuple-element.49.core), custom_call_target="tpu_custom_call" | custom-call | tf_op jit(solution)/shard_map/finish_kernel/pallas_call | solution.py:584
  (12 shorter events, 0.1 us)
Async XLA Ops:
  0.6 24.2 %copy-start = (bf16[2,256,256]{2,1,0:T(8,128)(2,1)S(1)}, bf16[2,256,256]{2,1,0:T(8,128)(2,1)}, u32[]{:S(2)}) copy-start(bf16[2,256,256]{2,1,0:T(8,128)(2,1)} %refs_2_.3) | copy-start | bytes 786436
  11.5 10.5 %all-to-all-start = ((bf16[4,64,560]{2,1,0:T(8,128)(2,1)}), bf16[4,64,560]{2,1,0:T(8,128)(2,1)S(1)}, u32[]{:S(2)}, u32[]{:S(2)}) async-start(bf16[4,64,560]{2,1,0:T(8,128)(2,1)} %pair_kernel.2), calls=%async_computation | async-start | bytes 655360 | tf_op jit(solution)/shard_map/all_to_all | solution.py:469
  14.9 0.8 %copy-start.2 = (bf16[128,256]{1,0:T(8,128)(2,1)S(1)}, bf16[128,256]{1,0:T(8,128)(2,1)}, u32[]{:S(2)}) copy-start(bf16[128,256]{1,0:T(8,128)(2,1)} %cotangent.1) | copy-start | bytes 196612
  15.8 0.7 copy-start.3
  16.5 0.7 copy-start.4
  17.2 0.7 copy-start.5
  57.6 4.8 %collective-permute-start = (bf16[2,16,256]{2,1,0:T(8,128)(2,1)S(1)}, bf16[2,16,256]{2,1,0:T(8,128)(2,1)S(1)}, u32[]{:S(2)}, u32[]{:S(2)}) collective-permute-start(bf16[2,16,256]{2,1,0:T(8,128)(2,1)S(1)} %get-tuple-element.46), channel_id=1, source_target_pairs={{0,8},{8,0},{16,24},{24,16},{32,40},{40,32},{48,56},{56,48},{64,72... | collective-permute-start | bytes 49160 | tf_op jit(solution)/shard_map/ppermute | solution.py:544
  63.9 19.1 %copy-start.1 = (bf16[256,560]{0,1:T(8,128)(2,1)S(1)}, bf16[256,560]{0,1:T(8,128)(2,1)}, u32[]{:S(2)}) copy-start(bf16[256,560]{0,1:T(8,128)(2,1)} %param.9) | copy-start | bytes 860164

commit v10 on v8

--- a/solution.py
+++ b/solution.py
@@ -148,7 +148,7 @@
                     result.append(fade * states[n * blocks + block] + w[block] * gate)
             return (tuple(result), tuple(t + x for t, x in zip(total, d)))
 
-        states, total = lax.fori_loop(0, steps, walk_states, (many, (zero,) * blocks), unroll=4)
+        states, total = lax.fori_loop(0, steps, walk_states, (many, (zero,) * blocks), unroll=8)
 
         def walk_adjoints(index, carried):
             step = index if falling else steps - 1 - index
@@ -161,7 +161,7 @@
                     result.append(fade * (g[block] * gate + carried[n * blocks + block]))
             return tuple(result)
 
-        carried = lax.fori_loop(0, steps, walk_adjoints, many, unroll=4)
+        carried = lax.fori_loop(0, steps, walk_adjoints, many, unroll=8)
         for block in range(blocks):
             lanes = lane_block(block)
 
@@ -272,7 +272,7 @@
                 fades[way, step, n] = jnp.exp2(d * rates[way, n])
         return _
 
-    lax.fori_loop(0, steps, walk, 0)
+    lax.fori_loop(0, steps, walk, 0, unroll=4)
 
 
 def direction_gradient(
@@ -345,7 +345,7 @@
         put_products(1, step, rows_of)
         return tuple(result)
 
-    lax.fori_loop(0, steps, walk_states, entering(0), unroll=4)
+    lax.fori_loop(0, steps, walk_states, entering(0), unroll=8)
 
     def walk_adjoints(index, carried):
         step = steps - 1 - index + way * (2 * index - steps + 1)
@@ -377,7 +377,7 @@
             grad_pre[at(step), lanes] = grad_delta * slope[way, at(step), lanes]
         return tuple(result)
 
-    lax.fori_loop(0, steps, walk_adjoints, entering(1), unroll=4)
+    lax.fori_loop(0, steps, walk_adjoints, entering(1), unroll=8)
     low[...] = dot(grad_pre[...].astype(BF16), w_delta[way], NT)
     row = lax.broadcasted_iota(jnp.int32, (2 * LANES, 2 * LANES), 0)
     column = lax.broadcasted_iota(jnp.int32, (2 * LANES, 2 * LANES), 1)

time: 84.8 us -> 84.7 us (level)
  no operation moved by 1% of the time
where the time goes in v10:
time: 84.7 us; the launch traced here: 84.2 us
  blocking collectives  61.3 us (72%)
  Pallas kernels  9.63 us (11%)
  starting transfers between devices  5.65 us (7%)
  waiting for transfers between devices  3.96 us (5%)
  local copies, waits for them, and re-layouts  2.94 us (3%)
    all_to_all x2, blocking collectives, exchange(): lax.all_to_all(array, 'seq', 0, 0, tiled=True, axis_index_groups=groups)  30.4 us
    all_gather x2, blocking collectives, sum_over_chan(): lax.all_gather(part, 'chan', axis=0, tiled=True, axis_index_groups=pairs)  15.9 us
    all_to_all x1, blocking collectives, sum_over_chan(): lax.all_to_all(copies, 'chan', 0, 0, tiled=True, axis_index_groups=across)  9.18 us
    all_gather x2, blocking collectives, sum_over_chan(): lax.all_gather(half, 'chan', axis=0, tiled=True, axis_index_groups=pairs)  5.88 us
    all_to_all x1, waiting for transfers between devices, sum_over_chan(): lax.all_to_all(copies, 'chan', 0, 0, tiled=True, axis_index_groups=across)  3.95 us
    all_to_all x1, starting transfers between devices, sum_over_chan(): lax.all_to_all(copies, 'chan', 0, 0, tiled=True, axis_index_groups=across)  3.45 us
    unnamed x12, local copies, waits for them, and re-layouts  2.94 us
    ppermute x1, starting transfers between devices, local(): lax.ppermute(others, 'seq', [(shard, shard ^ 1) for shard in range(shards)])  2.19 us
  transfers between devices with their start and end apart: 2, of which 1 were waited for; matrix products, arithmetic and copies ran while one was open for 0% of the time, Pallas kernels for 3%

profile of v10, /device:TPU:1, one launch (start us, length us, event | category | flops | bytes accessed | tf_op | source)
XLA Modules:
  0.0 84.2 jit_solution(10504568209549438795)
XLA Ops:
  0.6 1.3 %project_kernel.1 = (f32[128,256]{1,0:T(8,128)S(1)}, f32[128,560]{1,0:T(8,128)S(1)}) custom-call(bf16[128,256]{1,0:T(8,128)(2,1)} %signal.1, bf16[560,256]{1,0:T(8,128)(2,1)} %bitcast.3), custom_call_target="tpu_custom_call" | custom-call | tf_op jit(solution)/shard_map/project_kernel/pallas_call | solution.py:487
  2.0 8.7 %all_gather.12.both = f32[256,560]{1,0:T(8,128)S(1)} all-gather(f32[128,560]{1,0:T(8,128)S(1)} %get-tuple-element.26), channel_id=1, replica_groups={{0,1},{2,3},{4,5},{6,7},{8,9},{10,11},{12,13},{14,15},{16,17},{18,19},{..., dimensions={0}, use_global_device_ids=true | all-gather | bytes 860160 | tf_op jit(solution)/shard_map/all_gather | solution.py:460
  10.7 0.7 pair_kernel.2
  11.5 3.5 %all-to-all-start = ((bf16[4,64,560]{2,1,0:T(8,128)(2,1)}), bf16[4,64,560]{2,1,0:T(8,128)(2,1)S(1)}, u32[]{:S(2)}, u32[]{:S(2)}) async-start(bf16[4,64,560]{2,1,0:T(8,128)(2,1)} %pair_kernel.2), calls=%async_computation | async-start | bytes 655360 | tf_op jit(solution)/shard_map/all_to_all | solution.py:466
  14.9 0.8 copy-done.2
  15.8 0.7 copy-done.3
  16.5 0.7 copy-done.4
  17.2 0.7 copy-done.5
  17.9 0.2 prepare_kernel.1
  18.0 3.9 %all-to-all-done.parts = bf16[4,64,560]{2,1,0:T(8,128)(2,1)S(1)} async-done(((bf16[4,64,560]{2,1,0:T(8,128)(2,1)}), bf16[4,64,560]{2,1,0:T(8,128)(2,1)S(1)}, u32[]{:S(2)}, u32[]{:S(2)}) %all-to-all-start) | async-done | bytes 286752 | tf_op jit(solution)/shard_map/all_to_all | solution.py:466
  22.0 2.8 %all_gather.13.projected = bf16[128,560]{1,0:T(8,128)(2,1)S(1)} all-gather(bf16[64,560]{1,0:T(8,128)(2,1)S(1)} %chips_kernel.2), channel_id=1, replica_groups={{0,1},{2,3},{4,5},{6,7},{8,9},{10,11},{12,13},{14,15},{16,17},{18,19},{..., dimensions={0}, use_global_device_ids=true | all-gather | bytes 215040 | tf_op jit(solution)/shard_map/all_gather | solution.py:468
  24.8 2.1 %summary_kernel.1 = (f32[2,128,256]{2,1,0:T(8,128)S(1)}, f32[2,128,256]{2,1,0:T(8,128)S(1)}, f32[4,12,8,256]{3,2,1,0:T(8,128)S(1)}, f32[4,8,256]{2,1,0:T(8,128)S(1)}, bf16[4,2,16,256]{3,2,1,0:T(8,128)(2,1)S(1)}) custom-call(bf16[128,560]{1,0:T(8,128)(2,1)S(1)} %all_gather.13.projected, bf16[2,256,256]{2,1,0:T(8,128)(2,1)S(1)} %copy-done, ...), custom_call_target="tpu_custom_call" | custom-call | tf_op jit(solution)/shard_map/summary_kernel/pallas_call | solution.py:510
  26.9 6.8 %all_to_all.20.parts = bf16[4,2,16,256]{3,2,1,0:T(8,128)(2,1)S(1)} all-to-all(bf16[4,2,16,256]{3,2,1,0:T(8,128)(2,1)S(1)} %get-tuple-element.37), channel_id=1, replica_groups={{0,8,16,24},{32,40,48,56},{64,72,80,88},{96,104,112,120},{128,136,144,1..., dimensions={0} | all-to-all | bytes 131072 | tf_op jit(solution)/shard_map/all_to_all | solution.py:485
  33.7 0.2 row_kernel.1
  33.9 23.5 %all_to_all.21.rows = bf16[16,16,256]{2,1,0:T(8,128)(2,1)S(1)} all-to-all(bf16[16,16,256]{2,1,0:T(8,128)(2,1)S(1)} %row_kernel.1), channel_id=1, replica_groups={{0,32,64,96,128,160,192,224,256,288,320,352,384,416,448,480},{8,40,72,1..., dimensions={0} | all-to-all | bytes 262144 | tf_op jit(solution)/shard_map/all_to_all | solution.py:485
  57.5 0.2 entry_kernel.1
  57.6 2.2 %collective-permute-start = (f32[2,16,256]{2,1,0:T(8,128)S(1)}, f32[2,16,256]{2,1,0:T(8,128)S(1)}, u32[]{:S(2)}, u32[]{:S(2)}) collective-permute-start(f32[2,16,256]{2,1,0:T(8,128)S(1)} %get-tuple-element.44), channel_id=1, source_target_pairs={{0,8},{8,0},{16,24},{24,16},{32,40},{40,32},{48,56},{56,48},{64,72... | collective-permute-start | bytes 98312 | tf_op jit(solution)/shard_map/ppermute | solution.py:540
  59.8 1.0 %early_kernel.1 = (f32[2,128,3072]{2,1,0:T(8,128)S(1)}, f32[2,16,12,8,256]{4,3,2,1,0:T(8,128)S(1)}) custom-call(bf16[128,560]{1,0:T(8,128)(2,1)S(1)} %all_gather.13.projected, f32[2,12,8,256]{3,2,1,0:T(8,128)S(1)} %get-tuple-element.27.rates.refs_3_, f32[2,128,256]{2,1,0:T(8,128)S(1)} %get-tuple-element.31.delta.refs_6_), custom_call_target="tpu_custom_call" | custom-call | flops 4194304 | bytes 4194304 | tf_op jit(solution)/shard_map/early_kernel/pallas_call | solution.py:524
  60.9 1.4 %own_gradient_kernel.1 = (f32[128,256]{1,0:T(8,128)S(1)}, f32[128,256]{1,0:T(8,128)S(1)}, f32[128,256]{1,0:T(8,128)S(1)}, f32[128,128]{1,0:T(8,128)S(1)}) custom-call(f32[1,256]{1,0:T(1,128)S(1)} %get-tuple-element.25.skip_gain, f32[2,128,3072]{2,1,0:T(8,128)S(1)} %get-tuple-element.32.refs_0_, f32[2,16,12,8,256]{4,3,2,1,0:T(8,128)S(1)} %get-tuple-element.33.refs_1_, ...), custom_call_target="tpu_custom_call" | custom-call | flops 4194304 | bytes 4194304 | tf_op jit(solution)/shard_map/own_gradient_kernel/pallas_call | solution.py:560
  62.3 1.4 %other_gradient_kernel.1 = (f32[128,256]{1,0:T(8,128)S(1)}, f32[128,560]{1,0:T(8,128)S(1)}, f32[128,256]{1,0:T(8,128)S(1)}) custom-call(f32[128,256]{1,0:T(8,128)S(1)} %get-tuple-element.40.own_core, f32[128,256]{1,0:T(8,128)S(1)} %get-tuple-element.41.own_direct, f32[128,256]{1,0:T(8,128)S(1)} %get-tuple-element.42.own_low, ...), custom_call_target="tpu_custom_call" | custom-call | tf_op jit(solution)/shard_map/other_gradient_kernel/pallas_call | solution.py:572
  63.7 7.1 %all_gather.14.both = f32[256,560]{1,0:T(8,128)S(1)} all-gather(f32[128,560]{1,0:T(8,128)S(1)} %get-tuple-element.45), channel_id=1, replica_groups={{0,1},{2,3},{4,5},{6,7},{8,9},{10,11},{12,13},{14,15},{16,17},{18,19},{..., dimensions={0}, use_global_device_ids=true | all-gather | bytes 860160 | tf_op jit(solution)/shard_map/all_gather | solution.py:460
  70.9 9.2 %all_to_all.22.parts = bf16[4,64,560]{2,1,0:T(8,128)(2,1)S(1)} all-to-all(bf16[4,64,560]{2,1,0:T(8,128)(2,1)S(1)} %pair_kernel.3), channel_id=1, replica_groups={{0,2,4,6},{1,3,5,7},{8,10,12,14},{9,11,13,15},{16,18,20,22},{17,19,21,2..., dimensions={0} | all-to-all | bytes 573440 | tf_op jit(solution)/shard_map/all_to_all | solution.py:466
  80.1 3.1 %all_gather.15.grad_proj = bf16[128,560]{1,0:T(8,128)(2,1)S(1)} all-gather(bf16[64,560]{1,0:T(8,128)(2,1)S(1)} %chips_kernel.3), channel_id=1, replica_groups={{0,1},{2,3},{4,5},{6,7},{8,9},{10,11},{12,13},{14,15},{16,17},{18,19},{..., dimensions={0}, use_global_device_ids=true | all-gather | bytes 215040 | tf_op jit(solution)/shard_map/all_gather | solution.py:468
  83.2 1.0 %finish_kernel.1 = (bf16[128,256]{1,0:T(8,128)(2,1)}, bf16[128,256]{1,0:T(8,128)(2,1)}) custom-call(bf16[128,560]{1,0:T(8,128)(2,1)S(1)} %all_gather.15.grad_proj, bf16[560,256]{1,0:T(8,128)(2,1)S(1)} %bitcast.4, f32[128,256]{1,0:T(8,128)S(1)} %get-tuple-element.46.direct, f32[128,256]{1,0:T(8,128)S(1)} %get-tuple-element.47.core), custom_call_target="tpu_custom_call" | custom-call | tf_op jit(solution)/shard_map/finish_kernel/pallas_call | solution.py:580
  (12 shorter events, 0.1 us)
Async XLA Ops:
  0.6 24.2 %copy-start = (bf16[2,256,256]{2,1,0:T(8,128)(2,1)S(1)}, bf16[2,256,256]{2,1,0:T(8,128)(2,1)}, u32[]{:S(2)}) copy-start(bf16[2,256,256]{2,1,0:T(8,128)(2,1)} %refs_2_.3) | copy-start | bytes 786436
  11.5 10.5 %all-to-all-start = ((bf16[4,64,560]{2,1,0:T(8,128)(2,1)}), bf16[4,64,560]{2,1,0:T(8,128)(2,1)S(1)}, u32[]{:S(2)}, u32[]{:S(2)}) async-start(bf16[4,64,560]{2,1,0:T(8,128)(2,1)} %pair_kernel.2), calls=%async_computation | async-start | bytes 655360 | tf_op jit(solution)/shard_map/all_to_all | solution.py:466
  14.9 0.8 %copy-start.2 = (bf16[128,256]{1,0:T(8,128)(2,1)S(1)}, bf16[128,256]{1,0:T(8,128)(2,1)}, u32[]{:S(2)}) copy-start(bf16[128,256]{1,0:T(8,128)(2,1)} %cotangent.1) | copy-start | bytes 196612
  15.8 0.7 copy-start.3
  16.5 0.7 copy-start.4
  17.2 0.7 copy-start.5
  57.6 4.7 %collective-permute-start = (f32[2,16,256]{2,1,0:T(8,128)S(1)}, f32[2,16,256]{2,1,0:T(8,128)S(1)}, u32[]{:S(2)}, u32[]{:S(2)}) collective-permute-start(f32[2,16,256]{2,1,0:T(8,128)S(1)} %get-tuple-element.44), channel_id=1, source_target_pairs={{0,8},{8,0},{16,24},{24,16},{32,40},{40,32},{48,56},{56,48},{64,72... | collective-permute-start | bytes 98312 | tf_op jit(solution)/shard_map/ppermute | solution.py:540
  63.7 19.5 %copy-start.1 = (bf16[256,560]{0,1:T(8,128)(2,1)S(1)}, bf16[256,560]{0,1:T(8,128)(2,1)}, u32[]{:S(2)}) copy-start(bf16[256,560]{0,1:T(8,128)(2,1)} %param.9) | copy-start | bytes 860164

commit v11 on v9

--- a/solution.py
+++ b/solution.py
@@ -148,7 +148,7 @@
                     result.append(fade * states[n * blocks + block] + w[block] * gate)
             return (tuple(result), tuple(t + x for t, x in zip(total, d)))
 
-        states, total = lax.fori_loop(0, steps, walk_states, (many, (zero,) * blocks), unroll=4)
+        states, total = lax.fori_loop(0, steps, walk_states, (many, (zero,) * blocks), unroll=8)
 
         def walk_adjoints(index, carried):
             step = index if falling else steps - 1 - index
@@ -161,7 +161,7 @@
                     result.append(fade * (g[block] * gate + carried[n * blocks + block]))
             return tuple(result)
 
-        carried = lax.fori_loop(0, steps, walk_adjoints, many, unroll=4)
+        carried = lax.fori_loop(0, steps, walk_adjoints, many, unroll=8)
         for block in range(blocks):
             lanes = lane_block(block)
 
@@ -274,7 +274,7 @@
                 fades[way, step, n] = jnp.exp2(d * rates[way, n])
         return _
 
-    lax.fori_loop(0, steps, walk, 0)
+    lax.fori_loop(0, steps, walk, 0, unroll=4)
 
 
 def direction_gradient(
@@ -348,7 +348,7 @@
         put_products(1, step, rows_of)
         return tuple(result)
 
-    lax.fori_loop(0, steps, walk_states, entering(0), unroll=4)
+    lax.fori_loop(0, steps, walk_states, entering(0), unroll=8)
 
     def walk_adjoints(index, carried):
         step = steps - 1 - index + way * (2 * index - steps + 1)
@@ -380,7 +380,7 @@
             grad_pre[at(step), lanes] = grad_delta * slope[way, at(step), lanes]
         return tuple(result)
 
-    lax.fori_loop(0, steps, walk_adjoints, entering(1), unroll=4)
+    lax.fori_loop(0, steps, walk_adjoints, entering(1), unroll=8)
     low[...] = dot(grad_pre[...].astype(BF16), w_delta[way], NT)
     row = lax.broadcasted_iota(jnp.int32, (2 * LANES, 2 * LANES), 0)
     column = lax.broadcasted_iota(jnp.int32, (2 * LANES, 2 * LANES), 1)

time: 84.6 us -> 84.5 us (level)
  no operation moved by 1% of the time
where the time goes in v11:
time: 84.5 us; the launch traced here: 84 us
  blocking collectives  61.1 us (72%)
  Pallas kernels  9.61 us (11%)
  starting transfers between devices  5.65 us (7%)
  waiting for transfers between devices  3.95 us (5%)
  local copies, waits for them, and re-layouts  2.94 us (3%)
    all_to_all x2, blocking collectives, exchange(): lax.all_to_all(array, 'seq', 0, 0, tiled=True, axis_index_groups=groups)  30.4 us
    all_gather x2, blocking collectives, sum_over_chan(): lax.all_gather(part, 'chan', axis=0, tiled=True, axis_index_groups=pairs)  15.7 us
    all_to_all x1, blocking collectives, sum_over_chan(): lax.all_to_all(copies, 'chan', 0, 0, tiled=True, axis_index_groups=across)  9.18 us
    all_gather x2, blocking collectives, sum_over_chan(): lax.all_gather(half, 'chan', axis=0, tiled=True, axis_index_groups=pairs)  5.88 us
    all_to_all x1, waiting for transfers between devices, sum_over_chan(): lax.all_to_all(copies, 'chan', 0, 0, tiled=True, axis_index_groups=across)  3.95 us
    all_to_all x1, starting transfers between devices, sum_over_chan(): lax.all_to_all(copies, 'chan', 0, 0, tiled=True, axis_index_groups=across)  3.45 us
    unnamed x12, local copies, waits for them, and re-layouts  2.94 us
    ppermute x1, starting transfers between devices, local(): lax.ppermute(others, 'seq', [(shard, shard ^ 1) for shard in range(shards)])  2.19 us
  transfers between devices with their start and end apart: 2, of which 1 were waited for; matrix products, arithmetic and copies ran while one was open for 0% of the time, Pallas kernels for 3%

profile of v11, /device:TPU:1, one launch (start us, length us, event | category | flops | bytes accessed | tf_op | source)
XLA Modules:
  0.0 84.0 jit_solution(13431415476774662524)
XLA Ops:
  0.6 1.3 %project_kernel.1 = (f32[128,256]{1,0:T(8,128)S(1)}, f32[128,560]{1,0:T(8,128)S(1)}) custom-call(bf16[128,256]{1,0:T(8,128)(2,1)} %signal.1, bf16[560,256]{1,0:T(8,128)(2,1)} %bitcast.3), custom_call_target="tpu_custom_call" | custom-call | tf_op jit(solution)/shard_map/project_kernel/pallas_call | solution.py:490
  2.0 8.7 %all_gather.12.both = f32[256,560]{1,0:T(8,128)S(1)} all-gather(f32[128,560]{1,0:T(8,128)S(1)} %get-tuple-element.27), channel_id=1, replica_groups={{0,1},{2,3},{4,5},{6,7},{8,9},{10,11},{12,13},{14,15},{16,17},{18,19},{..., dimensions={0}, use_global_device_ids=true | all-gather | bytes 860160 | tf_op jit(solution)/shard_map/all_gather | solution.py:463
  10.7 0.7 pair_kernel.2
  11.5 3.5 %all-to-all-start = ((bf16[4,64,560]{2,1,0:T(8,128)(2,1)}), bf16[4,64,560]{2,1,0:T(8,128)(2,1)S(1)}, u32[]{:S(2)}, u32[]{:S(2)}) async-start(bf16[4,64,560]{2,1,0:T(8,128)(2,1)} %pair_kernel.2), calls=%async_computation | async-start | bytes 655360 | tf_op jit(solution)/shard_map/all_to_all | solution.py:469
  14.9 0.8 copy-done.2
  15.8 0.7 copy-done.3
  16.5 0.7 copy-done.4
  17.2 0.7 copy-done.5
  17.9 0.2 prepare_kernel.1
  18.0 3.9 %all-to-all-done.parts = bf16[4,64,560]{2,1,0:T(8,128)(2,1)S(1)} async-done(((bf16[4,64,560]{2,1,0:T(8,128)(2,1)}), bf16[4,64,560]{2,1,0:T(8,128)(2,1)S(1)}, u32[]{:S(2)}, u32[]{:S(2)}) %all-to-all-start) | async-done | bytes 286752 | tf_op jit(solution)/shard_map/all_to_all | solution.py:469
  22.0 2.8 %all_gather.13.projected = bf16[128,560]{1,0:T(8,128)(2,1)S(1)} all-gather(bf16[64,560]{1,0:T(8,128)(2,1)S(1)} %chips_kernel.2), channel_id=1, replica_groups={{0,1},{2,3},{4,5},{6,7},{8,9},{10,11},{12,13},{14,15},{16,17},{18,19},{..., dimensions={0}, use_global_device_ids=true | all-gather | bytes 215040 | tf_op jit(solution)/shard_map/all_gather | solution.py:471
  24.8 2.0 %summary_kernel.1 = (f32[2,128,256]{2,1,0:T(8,128)S(1)}, f32[2,128,256]{2,1,0:T(8,128)S(1)}, f32[4,12,8,256]{3,2,1,0:T(8,128)S(1)}, f32[4,8,256]{2,1,0:T(8,128)S(1)}, bf16[4,2,16,256]{3,2,1,0:T(8,128)(2,1)S(1)}) custom-call(bf16[128,560]{1,0:T(8,128)(2,1)S(1)} %all_gather.13.projected, bf16[2,256,256]{2,1,0:T(8,128)(2,1)S(1)} %copy-done, ...), custom_call_target="tpu_custom_call" | custom-call | tf_op jit(solution)/shard_map/summary_kernel/pallas_call | solution.py:513
  26.9 6.8 %all_to_all.20.parts = bf16[4,2,16,256]{3,2,1,0:T(8,128)(2,1)S(1)} all-to-all(bf16[4,2,16,256]{3,2,1,0:T(8,128)(2,1)S(1)} %get-tuple-element.39), channel_id=1, replica_groups={{0,8,16,24},{32,40,48,56},{64,72,80,88},{96,104,112,120},{128,136,144,1..., dimensions={0} | all-to-all | bytes 131072 | tf_op jit(solution)/shard_map/all_to_all | solution.py:488
  33.7 0.2 row_kernel.1
  33.9 23.5 %all_to_all.21.rows = bf16[16,16,256]{2,1,0:T(8,128)(2,1)S(1)} all-to-all(bf16[16,16,256]{2,1,0:T(8,128)(2,1)S(1)} %row_kernel.1), channel_id=1, replica_groups={{0,32,64,96,128,160,192,224,256,288,320,352,384,416,448,480},{8,40,72,1..., dimensions={0} | all-to-all | bytes 262144 | tf_op jit(solution)/shard_map/all_to_all | solution.py:488
  57.4 0.2 entry_kernel.1
  57.6 2.2 %collective-permute-start = (bf16[2,16,256]{2,1,0:T(8,128)(2,1)S(1)}, bf16[2,16,256]{2,1,0:T(8,128)(2,1)S(1)}, u32[]{:S(2)}, u32[]{:S(2)}) collective-permute-start(bf16[2,16,256]{2,1,0:T(8,128)(2,1)S(1)} %get-tuple-element.46), channel_id=1, source_target_pairs={{0,8},{8,0},{16,24},{24,16},{32,40},{40,32},{48,56},{56,48},{64,72... | collective-permute-start | bytes 49160 | tf_op jit(solution)/shard_map/ppermute | solution.py:544
  59.8 1.0 %early_kernel.1 = (f32[2,128,3072]{2,1,0:T(8,128)S(1)}, f32[2,16,12,8,256]{4,3,2,1,0:T(8,128)S(1)}, f32[2,128,256]{2,1,0:T(8,128)S(1)}) custom-call(bf16[128,560]{1,0:T(8,128)(2,1)S(1)} %all_gather.13.projected, f32[2,12,8,256]{3,2,1,0:T(8,128)S(1)} %get-tuple-element.28.rates.refs_3_, f32[2,128,256]{2,1,0:T(8,128)S(1)} %get-tuple-element.32.delta.refs_6_, ...), custom_call_target="tpu_custom_call" | custom-call | flops 4194304 | bytes 4194304 | tf_op jit(solution)/shard_map/early_kernel/pallas_call | solution.py:527
  60.8 1.4 %own_gradient_kernel.1 = (f32[128,256]{1,0:T(8,128)S(1)}, f32[128,256]{1,0:T(8,128)S(1)}, f32[128,256]{1,0:T(8,128)S(1)}, f32[128,128]{1,0:T(8,128)S(1)}) custom-call(f32[1,256]{1,0:T(1,128)S(1)} %get-tuple-element.26.skip_gain, f32[2,128,3072]{2,1,0:T(8,128)S(1)} %get-tuple-element.34.refs_0_, f32[2,16,12,8,256]{4,3,2,1,0:T(8,128)S(1)} %get-tuple-element.35.refs_1_, ...), custom_call_target="tpu_custom_call" | custom-call | flops 4194304 | bytes 4194304 | tf_op jit(solution)/shard_map/own_gradient_kernel/pallas_call | solution.py:564
  62.3 1.4 %other_gradient_kernel.1 = (f32[128,256]{1,0:T(8,128)S(1)}, f32[128,560]{1,0:T(8,128)S(1)}, f32[128,256]{1,0:T(8,128)S(1)}) custom-call(f32[128,256]{1,0:T(8,128)S(1)} %get-tuple-element.42.own_core, f32[128,256]{1,0:T(8,128)S(1)} %get-tuple-element.43.own_direct, f32[128,256]{1,0:T(8,128)S(1)} %get-tuple-element.44.own_low, ...), custom_call_target="tpu_custom_call" | custom-call | tf_op jit(solution)/shard_map/other_gradient_kernel/pallas_call | solution.py:576
  63.7 6.9 %all_gather.14.both = f32[256,560]{1,0:T(8,128)S(1)} all-gather(f32[128,560]{1,0:T(8,128)S(1)} %get-tuple-element.47), channel_id=1, replica_groups={{0,1},{2,3},{4,5},{6,7},{8,9},{10,11},{12,13},{14,15},{16,17},{18,19},{..., dimensions={0}, use_global_device_ids=true | all-gather | bytes 860160 | tf_op jit(solution)/shard_map/all_gather | solution.py:463
  70.7 9.2 %all_to_all.22.parts = bf16[4,64,560]{2,1,0:T(8,128)(2,1)S(1)} all-to-all(bf16[4,64,560]{2,1,0:T(8,128)(2,1)S(1)} %pair_kernel.3), channel_id=1, replica_groups={{0,2,4,6},{1,3,5,7},{8,10,12,14},{9,11,13,15},{16,18,20,22},{17,19,21,2..., dimensions={0} | all-to-all | bytes 573440 | tf_op jit(solution)/shard_map/all_to_all | solution.py:469
  79.9 3.1 %all_gather.15.grad_proj = bf16[128,560]{1,0:T(8,128)(2,1)S(1)} all-gather(bf16[64,560]{1,0:T(8,128)(2,1)S(1)} %chips_kernel.3), channel_id=1, replica_groups={{0,1},{2,3},{4,5},{6,7},{8,9},{10,11},{12,13},{14,15},{16,17},{18,19},{..., dimensions={0}, use_global_device_ids=true | all-gather | bytes 215040 | tf_op jit(solution)/shard_map/all_gather | solution.py:471
  83.0 1.0 %finish_kernel.1 = (bf16[128,256]{1,0:T(8,128)(2,1)}, bf16[128,256]{1,0:T(8,128)(2,1)}) custom-call(bf16[128,560]{1,0:T(8,128)(2,1)S(1)} %all_gather.15.grad_proj, bf16[560,256]{1,0:T(8,128)(2,1)S(1)} %bitcast.4, f32[128,256]{1,0:T(8,128)S(1)} %get-tuple-element.48.direct, f32[128,256]{1,0:T(8,128)S(1)} %get-tuple-element.49.core), custom_call_target="tpu_custom_call" | custom-call | tf_op jit(solution)/shard_map/finish_kernel/pallas_call | solution.py:584
  (12 shorter events, 0.1 us)
Async XLA Ops:
  0.6 24.2 %copy-start = (bf16[2,256,256]{2,1,0:T(8,128)(2,1)S(1)}, bf16[2,256,256]{2,1,0:T(8,128)(2,1)}, u32[]{:S(2)}) copy-start(bf16[2,256,256]{2,1,0:T(8,128)(2,1)} %refs_2_.3) | copy-start | bytes 786436
  11.5 10.5 %all-to-all-start = ((bf16[4,64,560]{2,1,0:T(8,128)(2,1)}), bf16[4,64,560]{2,1,0:T(8,128)(2,1)S(1)}, u32[]{:S(2)}, u32[]{:S(2)}) async-start(bf16[4,64,560]{2,1,0:T(8,128)(2,1)} %pair_kernel.2), calls=%async_computation | async-start | bytes 655360 | tf_op jit(solution)/shard_map/all_to_all | solution.py:469
  14.9 0.8 %copy-start.2 = (bf16[128,256]{1,0:T(8,128)(2,1)S(1)}, bf16[128,256]{1,0:T(8,128)(2,1)}, u32[]{:S(2)}) copy-start(bf16[128,256]{1,0:T(8,128)(2,1)} %cotangent.1) | copy-start | bytes 196612
  15.8 0.7 copy-start.3
  16.5 0.7 copy-start.4
  17.2 0.7 copy-start.5
  57.6 4.7 %collective-permute-start = (bf16[2,16,256]{2,1,0:T(8,128)(2,1)S(1)}, bf16[2,16,256]{2,1,0:T(8,128)(2,1)S(1)}, u32[]{:S(2)}, u32[]{:S(2)}) collective-permute-start(bf16[2,16,256]{2,1,0:T(8,128)(2,1)S(1)} %get-tuple-element.46), channel_id=1, source_target_pairs={{0,8},{8,0},{16,24},{24,16},{32,40},{40,32},{48,56},{56,48},{64,72... | collective-permute-start | bytes 49160 | tf_op jit(solution)/shard_map/ppermute | solution.py:544
  63.7 19.3 %copy-start.1 = (bf16[256,560]{0,1:T(8,128)(2,1)S(1)}, bf16[256,560]{0,1:T(8,128)(2,1)}, u32[]{:S(2)}) copy-start(bf16[256,560]{0,1:T(8,128)(2,1)} %param.9) | copy-start | bytes 860164
